TPU v7x, 256 devices: a whole 4x4x8 slice. The times are simulated.
256 devices in a mesh: ap: 32 (over x, z_hi, core), pass: 8 (over y, z_lo).
Axes of the slice: x: 4, y: 4, z: 8 (z_hi: 4, z_lo: 2; z = z_hi * 2 + z_lo), core: 2. Of those that a mesh axis runs over, the one named last changes fastest.
Arguments:
- echo_record: bfloat16 [2, 64, 2048, 512], P(None, 'pass', 'ap'), may hold values from -6 to 6
- along_track_kernel: bfloat16 [2, 1024, 2048], P(None, None, 'ap'), may hold values from -0.1875 to 0.1875
- slant_distance_kernel: bfloat16 [2, 512, 256], replicated, may hold values from -0.1875 to 0.1875
- vertical_lags: int32 [64], P('pass'), may hold values from 0 to 64
- lateral_lags: int32 [64], P('pass'), may hold values from 0 to 32
- orbit_source_survey: int32 [64], replicated, may hold values from 0 to 63, each once
- normal_spacings: float32 [64], replicated, may hold values from -1 to 1
Outputs:
- profile: float32 [2, 1024, 256, 512], P(None, ('ap', 'pass'))
All inputs are finite; a program needn't handle non-finite values.
Results may differ from a plain program's by a relative error of at most 0.02.
Values may be sent and summed in bfloat16 or wider, within the bound.
No kernel may reach another device: no remote copies, remote signals or barrier semaphores. Data moves between devices by JAX's collectives and lax.ppermute only.
A program may use at most 128 MiB of HBM per device.

v0:
```python
import jax
import jax.numpy as jnp
from jax import lax
from jax.sharding import PartitionSpec as P

HEIGHT_CELLS = 512
ITERS = 4
SPAN = 2
COL_MAX = 32


shrink_level = 0.1


def phasor_dictionary(normal_spacings, orbit_source_survey, height_cell_number):
    support_mask = (
        orbit_source_survey[:, None]
        == jnp.arange(normal_spacings.shape[0], dtype=jnp.int32)[None, :]
    ).astype(normal_spacings.dtype)
    chosen_height_cells = jnp.sum(support_mask * normal_spacings[None, :], axis=1)
    orbit_start_positions = (
        jnp.arange(height_cell_number).astype(normal_spacings.dtype) - height_cell_number // 2
    )
    phases = jnp.pi * chosen_height_cells[:, None] * orbit_start_positions[None, :]
    return (jnp.cos(phases), jnp.sin(phases))


def shrink_steps(obs_re, obs_im, inphase_phasor_part, quadrature_phasor_part):
    passes = inphase_phasor_part.shape[0]
    height_cell_number = inphase_phasor_part.shape[1]
    prof_re = jnp.zeros((obs_re.shape[0], height_cell_number), jnp.float32)
    prof_im = jnp.zeros((obs_re.shape[0], height_cell_number), jnp.float32)
    for sweep_index in range(ITERS):
        if sweep_index == 0:
            resid_re = obs_re
            resid_im = obs_im
        else:
            pred_re = jnp.dot(prof_re, inphase_phasor_part.T) - jnp.dot(
                prof_im, quadrature_phasor_part.T
            )
            pred_im = jnp.dot(prof_re, quadrature_phasor_part.T) + jnp.dot(
                prof_im, inphase_phasor_part.T
            )
            resid_re = obs_re - pred_re / height_cell_number
            resid_im = obs_im - pred_im / height_cell_number
        grad_re = jnp.dot(resid_re, inphase_phasor_part) + jnp.dot(resid_im, quadrature_phasor_part)
        grad_im = jnp.dot(resid_im, inphase_phasor_part) - jnp.dot(resid_re, quadrature_phasor_part)
        moved_re = prof_re + grad_re / passes
        moved_im = prof_im + grad_im / passes
        prof_re = moved_re - jnp.clip(moved_re, -shrink_level, shrink_level)
        prof_im = moved_im - jnp.clip(moved_im, -shrink_level, shrink_level)
    return (prof_re, prof_im)


def focus_range(echo_record, slant_distance_kernel):
    kernel_re, kernel_im = (slant_distance_kernel[0], slant_distance_kernel[1])
    focus_re = jnp.einsum(
        "ptf,fc->ptc", echo_record[0], kernel_re, preferred_element_type=jnp.float32
    ) - jnp.einsum("ptf,fc->ptc", echo_record[1], kernel_im, preferred_element_type=jnp.float32)
    focus_im = jnp.einsum(
        "ptf,fc->ptc", echo_record[0], kernel_im, preferred_element_type=jnp.float32
    ) + jnp.einsum("ptf,fc->ptc", echo_record[1], kernel_re, preferred_element_type=jnp.float32)
    return (focus_re.astype(jnp.bfloat16), focus_im.astype(jnp.bfloat16))


def azimuth_terms(kernel_re, kernel_im, focus_re, focus_im):
    pattern = "prt,ptc->prc"
    image_re = jnp.einsum(
        pattern, kernel_re, focus_re, preferred_element_type=jnp.float32
    ) - jnp.einsum(pattern, kernel_im, focus_im, preferred_element_type=jnp.float32)
    image_im = jnp.einsum(
        pattern, kernel_re, focus_im, preferred_element_type=jnp.float32
    ) + jnp.einsum(pattern, kernel_im, focus_re, preferred_element_type=jnp.float32)
    return (image_re, image_im)


def shift_kernel(kernel, vertical_lags, margin):
    padded = jnp.pad(kernel, ((0, 0), (margin, 0), (0, 0)))

    def choose_rows(offset):
        return lax.dynamic_slice_in_dim(padded, margin - offset, kernel.shape[1], 1)

    return jax.vmap(choose_rows, out_axes=1)(vertical_lags)


def shift_columns(image_block, lateral_lags):
    padded = jnp.pad(image_block, ((0, 0), (0, 0), (0, 0), (COL_MAX, 0)))

    def choose_cols(planes, offset):
        return lax.dynamic_slice_in_dim(planes, COL_MAX - offset, image_block.shape[3], 2)

    return jax.vmap(choose_cols, in_axes=(1, 0), out_axes=1)(padded, lateral_lags)


def body(
    echo_record,
    along_track_kernel,
    slant_distance_kernel,
    vertical_lags,
    lateral_lags,
    orbit_source_survey,
    normal_spacings,
):
    ap_count = lax.axis_size("ap")
    strip_height = along_track_kernel.shape[1] // ap_count
    focus_re, focus_im = focus_range(echo_record, slant_distance_kernel)
    kernel = shift_kernel(along_track_kernel, vertical_lags, SPAN * strip_height)
    image_re, image_im = azimuth_terms(kernel[0], kernel[1], focus_re, focus_im)
    image_block = lax.psum_scatter(
        jnp.stack([image_re, image_im]).astype(jnp.bfloat16), "ap", scatter_dimension=2, tiled=True
    ).astype(jnp.float32)
    aligned = shift_columns(image_block, lateral_lags).astype(jnp.bfloat16)
    inphase_phasor_part, quadrature_phasor_part = phasor_dictionary(
        normal_spacings, orbit_source_survey, HEIGHT_CELLS
    )
    stacked = lax.all_to_all(aligned, "pass", split_axis=2, concat_axis=1, tiled=True)
    row_count = stacked.shape[2]
    col_count = stacked.shape[3]
    flattened = stacked.astype(jnp.float32).reshape(2, stacked.shape[1], row_count * col_count)
    prof_re, prof_im = shrink_steps(
        flattened[0].T, flattened[1].T, inphase_phasor_part, quadrature_phasor_part
    )
    return jnp.stack([prof_re, prof_im]).reshape(
        2, row_count, col_count, inphase_phasor_part.shape[1]
    )


def solution(mesh):
    return jax.shard_map(
        body,
        mesh=mesh,
        in_specs=(
            P(None, "pass", "ap", None),
            P(None, None, "ap"),
            P(),
            P("pass"),
            P("pass"),
            P(),
            P(),
        ),
        out_specs=P(None, ("ap", "pass"), None, None),
        check_vma=False,
    )
```

profile of v0, /device:TPU:1, one launch (start us, length us, event | category | flops | bytes accessed | tf_op | source)
XLA Modules:
  0.0 217.5 jit_solution(17733385962184569064)
XLA Ops:
  6.5 2.2 %fusion.22 = f32[8,64,256]{2,1,0:T(8,128)} fusion(bf16[2,8,64,512]{3,2,1,0:T(8,128)(2,1)} %param.7, bf16[2,512,256]{2,1,0:T(8,128)(2,1)} %param.9), kind=kOutput, calls=%fused_computation.50 | convolution fusion | flops 134217728 | bytes 1310720 | tf_op jit(solution)/shard_map/ptf,fc->ptc/dot_general | solution.py:57
  8.8 2.2 %fusion.20 = f32[8,64,256]{2,1,0:T(8,128)} fusion(bf16[2,8,64,512]{3,2,1,0:T(8,128)(2,1)} %param.7, bf16[2,512,256]{2,1,0:T(8,128)(2,1)} %param.9), kind=kOutput, calls=%fused_computation.48 | convolution fusion | flops 134217728 | bytes 1310720 | tf_op jit(solution)/shard_map/ptf,fc->ptc/dot_general | solution.py:60
  11.4 13.0 %while.1 = (s32[]{:T(128)}, bf16[2,1088,64]{2,1,0:T(8,128)(2,1)S(1)}, s32[8,3]{0,1:T(4,128)S(1)}, bf16[8,2,1024,64]{2,3,0,1:T(8,128)(2,1)S(1)}, s32[]{:T(128)}) while((s32[]{:T(128)}, bf16[2,1088,64]{2,1,0:T(8,128)(2,1)S(1)}, s32[8,3]{0,1:T(4,128)S(1)}, bf16[8,2,1024,64]{2,3,0,1:T(8,128)(2,1)S(1)}, s32[]{:T(128)}) %tuple.18), condition=%wide.while_cond, body=%wide.while_body.sunk | while | flops 2 | bytes 1572969 | solution.py:81
  24.4 1.6 fusion.2
  26.0 1.6 fusion.3
  27.6 1.3 fusion.17
  28.9 1.3 fusion.16
  30.2 1.3 fusion
  31.5 3.4 %fusion.1 = bf16[1,8,1024,256]{3,2,1,0:T(8,128)(2,1)} fusion(f32[8,1024,256]{2,1,0:T(8,128)S(1)} %fusion.16, bf16[8,64,256]{2,1,0:T(8,128)(2,1)S(1)} %fusion.2, bf16[2,8,1024,64]{2,3,1,0:T(8,128)(2,1)S(1)} %bitcast.105), kind=kOutput, calls=%fused_computation.8 | convolution fusion | flops 272629760 | bytes 13893632 | tf_op jit(solution)/shard_map/prt,ptc->prc/dot_general | solution.py:73
  34.9 6.2 %pad_maximum_fusion = bf16[2,8,1024,256]{3,2,1,0:T(8,128)(2,1)} fusion(bf16[1,8,1024,256]{3,2,1,0:T(8,128)(2,1)} %fusion.1, bf16[1,8,1024,256]{3,2,1,0:T(8,128)(2,1)S(1)} %fusion), kind=kLoop, calls=%fused_computation.4 | loop fusion | flops 4194304 | bytes 16777216 | tf_op jit(solution)/shard_map/stack | solution.py:110
  41.8 123.7 %reduce-scatter.2.cloned.1.call-done = bf16[2,8,32,256]{3,2,1,0:T(8,128)(2,1)} async-done(((bf16[2,8,1024,256]{3,2,1,0:T(8,128)(2,1)}), bf16[2,8,32,256]{3,2,1,0:T(8,128)(2,1)}) %reduce-scatter.2.cloned.1.call-update) | async-done | bytes 262160 | tf_op jit(solution)/shard_map/reduce_scatter | solution.py:109
  165.4 1.2 convert_bitcast_fusion.1
  166.6 1.2 copy.23
  167.8 3.3 %gather_fusion = bf16[8,2,32,256]{2,1,3,0:T(2,128)(2,1)S(1)} fusion(bf16[8,2,32,288]{2,1,0,3:T(2,128)(2,1)S(1)} %copy.23, s32[8]{0:T(128)S(1)} %fusion.108), kind=kCustom, calls=%fused_computation | custom fusion | bytes 524416 | tf_op jit(solution)/shard_map/vmap()/gather | solution.py:90
  171.1 1.3 copy.24
  172.4 4.2 %all-to-all-start = ((bf16[2,8,32,256]{3,1,0,2:T(8,128)(2,1)}), bf16[2,8,32,256]{3,1,0,2:T(8,128)(2,1)S(1)}, u32[]{:S(2)}, u32[]{:S(2)}) async-start(bf16[2,8,32,256]{3,1,0,2:T(8,128)(2,1)} %copy.24), calls=%async_computation.1 | async-start | bytes 524288 | tf_op jit(solution)/shard_map/all_to_all | solution.py:116
  176.8 5.9 %all-to-all-done = bf16[2,8,32,256]{3,1,0,2:T(8,128)(2,1)S(1)} async-done(((bf16[2,8,32,256]{3,1,0,2:T(8,128)(2,1)}), bf16[2,8,32,256]{3,1,0,2:T(8,128)(2,1)S(1)}, u32[]{:S(2)}, u32[]{:S(2)}) %all-to-all-start) | async-done | bytes 262176 | tf_op jit(solution)/shard_map/all_to_all | solution.py:116
  184.6 0.9 clamp_subtract_fusion.7
  187.1 0.9 clamp_subtract_fusion.6
  188.9 0.9 fusion.43
  190.6 0.9 fusion.41
  191.5 1.0 clamp_subtract_fusion.5
  194.2 1.0 clamp_subtract_fusion.4
  196.0 0.9 fusion.40
  196.9 1.0 fusion.9
  197.9 0.9 fusion.38
  198.8 1.0 clamp_subtract_fusion.3
  201.5 1.0 clamp_subtract_fusion.2
  203.3 0.9 fusion.37
  205.9 1.0 clamp_subtract_fusion.1
  206.9 1.0 clamp_subtract_fusion
  207.9 2.8 %pad_maximum_fusion.1 = f32[2,4,256,512]{3,2,1,0:T(8,128)} fusion(f32[1,4,256,512]{3,2,1,0:T(8,128)S(1)} %bitcast.101, f32[1,4,256,512]{3,2,1,0:T(8,128)S(1)} %bitcast.100), kind=kLoop, calls=%fused_computation.9 | loop fusion | flops 1048576 | bytes 8388608 | tf_op jit(solution)/shard_map/stack | solution.py:123
  (79 shorter events, 25.7 us)
Async XLA Ops:
  6.5 4.4 %copy-start.1 = (s32[8]{0:T(128)S(1)}, s32[8]{0:T(128)}, u32[]{:S(2)}) copy-start(s32[8]{0:T(128)} %param.10) | copy-start | bytes 100
  6.5 4.5 %copy-start = (bf16[2,1024,64]{1,2,0:T(8,128)(2,1)S(1)}, bf16[2,1024,64]{1,2,0:T(8,128)(2,1)}, u32[]{:S(2)}) copy-start(bf16[2,1024,64]{1,2,0:T(8,128)(2,1)} %param.8) | copy-start | bytes 786436
  6.5 158.9 %reduce-scatter.2.cloned.1.call-start = ((), (), s32[]{:S(2)}) async-start(), calls=%async_computation.2 | async-start | bytes 8650752 | tf_op jit(solution)/shard_map/reduce_scatter | solution.py:109
  41.1 0.7 copy-start.2
  166.6 10.0 %copy-start.3 = (f32[64]{0:T(128)S(1)}, f32[64]{0:T(128)}, u32[]{:S(2)}) copy-start(f32[64]{0:T(128)} %param.13) | copy-start | bytes 772
  166.6 10.0 %copy-start.4 = (s32[64]{0:T(128)S(1)}, s32[64]{0:T(128)}, u32[]{:S(2)}) copy-start(s32[64]{0:T(128)} %param.12) | copy-start | bytes 772
  172.4 10.3 %all-to-all-start = ((bf16[2,8,32,256]{3,1,0,2:T(8,128)(2,1)}), bf16[2,8,32,256]{3,1,0,2:T(8,128)(2,1)S(1)}, u32[]{:S(2)}, u32[]{:S(2)}) async-start(bf16[2,8,32,256]{3,1,0,2:T(8,128)(2,1)} %copy.24), calls=%async_computation.1 | async-start | bytes 524288 | tf_op jit(solution)/shard_map/all_to_all | solution.py:116
Sparse Core Ops, SparseCore 0:
  41.2 124.1 reduce-scatter.1
where the time goes:
time: 219 us; the launch traced here: 218 us
  waiting for transfers between devices  130 us (59%)
  matrix products  40 us (18%)
  local copies, waits for them, and re-layouts  20.7 us (9%)
  between operations  13.6 us (6%)
  other arithmetic  9.16 us (4%)
  starting transfers between devices  4.16 us (2%)
    reduce_scatter x1, waiting for transfers between devices, body(): lax.psum_scatter(jnp.stack([image_re, image_im]).astype(jnp.bfloat16), 'a...  124 us
    gather x40, local copies, waits for them, and re-layouts  12.7 us
    another operation x1, other arithmetic, body(): jnp.stack([image_re, image_im]).astype(jnp.bfloat16)  6.19 us
    all_to_all x1, waiting for transfers between devices, body(): lax.all_to_all(aligned, 'pass', split_axis=2, concat_axis=1, tiled=True)  5.92 us
  transfers between devices with their start and end apart: 2, of which 2 were waited for; matrix products, arithmetic and copies ran while one was open for 0% of the time, Pallas kernels for 0%

commit v1 on v0

v1 whole, which is shorter than its diff:
```python
import jax
import jax.numpy as jnp
from jax import lax
from jax.experimental import pallas as pl
from jax.experimental.pallas import tpu as pltpu
from jax.sharding import Mesh, PartitionSpec as P

BINS = 512
ITERS = 4
ROW_MAX = 64
LEVEL = 0.1

VMEM = pl.BlockSpec(memory_space=pltpu.VMEM)
SMEM = pl.BlockSpec(memory_space=pltpu.SMEM)


def dot(a, b, ca, cb):
    return lax.dot_general(a, b, (((ca,), (cb,)), ((), ())), preferred_element_type=jnp.float32)


def focus_kernel(lat_ref, echo_ref, kern_ref, out_ref):
    passes, _, pulses, cols = out_ref.shape
    kr = kern_ref[0]
    ki = kern_ref[1]
    col = lax.broadcasted_iota(jnp.int32, (pulses, cols), 1)
    for q in range(passes):
        er = echo_ref[0, q]
        ei = echo_ref[1, q]
        lag = lat_ref[q]
        keep = col >= lag
        fr = dot(er, kr, 1, 0) - dot(ei, ki, 1, 0)
        fi = dot(er, ki, 1, 0) + dot(ei, kr, 1, 0)
        fr = jnp.where(keep, pltpu.roll(fr, lag, 1), 0.0)
        fi = jnp.where(keep, pltpu.roll(fi, lag, 1), 0.0)
        out_ref[q, 0] = fr.astype(out_ref.dtype)
        out_ref[q, 1] = fi.astype(out_ref.dtype)


def image_kernel(q_ref, ver_ref, at_ref, f_ref, out_ref, re_ref, im_ref):
    parts, _, pulses, rows = at_ref.shape
    cols = f_ref.shape[3]
    lag = ver_ref[q_ref[0]]
    fr = f_ref[:, 0].reshape(parts * pulses, cols)
    fi = f_ref[:, 1].reshape(parts * pulses, cols)
    re_ref[0:ROW_MAX] = jnp.zeros((ROW_MAX, cols), jnp.float32)
    im_ref[0:ROW_MAX] = jnp.zeros((ROW_MAX, cols), jnp.float32)
    step = 256
    for r0 in range(0, rows, step):
        ar = at_ref[:, 0, :, r0 : r0 + step].reshape(parts * pulses, step)
        ai = at_ref[:, 1, :, r0 : r0 + step].reshape(parts * pulses, step)
        re_ref[ROW_MAX + r0 : ROW_MAX + r0 + step] = dot(ar, fr, 0, 0) - dot(ai, fi, 0, 0)
        im_ref[ROW_MAX + r0 : ROW_MAX + r0 + step] = dot(ar, fi, 0, 0) + dot(ai, fr, 0, 0)
    block = 128
    start = ROW_MAX - lag
    base = pl.multiple_of(start // 8 * 8, 8)
    rest = start - base

    def shifted(ref, r0):
        wide = ref[pl.ds(base + r0, block + 8)]
        return pltpu.roll(wide, block + 8 - rest, 0)[:block]

    sub = lax.broadcasted_iota(jnp.int32, (block // 8, 8, cols), 1)
    for r0 in range(0, rows, block):
        re = shifted(re_ref, r0).reshape(block // 8, 8, cols)
        im = shifted(im_ref, r0).reshape(block // 8, 8, cols)
        first = jnp.where(sub < 4, re, pltpu.roll(im, 4, 1))
        second = jnp.where(sub < 4, pltpu.roll(re, 4, 1), im)
        both = jnp.stack([first, second], axis=1).reshape(2 * block, cols)
        out_ref[2 * r0 : 2 * r0 + 2 * block] = both.astype(out_ref.dtype)


def recover_kernel(img_ref, g_ref, h_ref, out_ref, y_ref):
    i = pl.program_id(0)
    xs, parts, others, eight, cols = img_ref.shape
    passes = xs * others

    @pl.when(i == 0)
    def _():
        for x in range(xs):
            acc = img_ref[x, 0].astype(jnp.float32)
            for z in range(1, parts):
                acc = acc + img_ref[x, z].astype(jnp.float32)
            acc = acc.reshape(others * eight, cols)
            for c in range(cols // 128):
                y_ref[c, x * others * eight : (x + 1) * others * eight] = acc[:, c * 128 : c * 128 + 128]

    g = g_ref[...]
    h = h_ref[...]
    y = jnp.concatenate(
        [
            jnp.concatenate(
                [
                    y_ref.at[c][pl.ds(i, passes, stride=eight), :],
                    y_ref.at[c][pl.ds(eight // 2 + i, passes, stride=eight), :],
                ],
                axis=0,
            ).T
            for c in range(cols // 128)
        ],
        axis=0,
    )
    yb = y.astype(jnp.bfloat16)
    yt = yb.astype(jnp.float32)
    v = dot(yb, g, 1, 0)
    u = v - jnp.clip(v, -LEVEL, LEVEL)
    for _ in range(ITERS - 1):
        resid = yt - dot(u.astype(jnp.bfloat16), h, 1, 0)
        v = u + dot(resid.astype(jnp.bfloat16), g, 1, 0)
        u = v - jnp.clip(v, -LEVEL, LEVEL)
    out_ref[0, 0] = u[:, :BINS]
    out_ref[1, 0] = u[:, BINS:]


def steering(normal_spacings, source):
    chosen = jnp.sum(
        jnp.where(
            source[:, None] == jnp.arange(normal_spacings.shape[0], dtype=jnp.int32)[None, :],
            normal_spacings[None, :],
            0.0,
        ),
        axis=1,
    )
    bins = jnp.arange(BINS).astype(normal_spacings.dtype) - BINS // 2
    phases = jnp.pi * chosen[:, None] * bins[None, :]
    return jnp.cos(phases), jnp.sin(phases)


def body(echo, along, slant, vertical, lateral, survey, spacings):
    passes = vertical.shape[0]
    pulses = along.shape[2]
    rows = along.shape[1]
    cols = slant.shape[2]
    total = survey.shape[0]
    near = ("x", "c")
    every = ("x", "zh", "c", "y", "zl")
    bf = jnp.bfloat16

    at = lax.all_gather(jnp.transpose(along, (0, 2, 1)), near, axis=0)
    focus = pl.pallas_call(
        focus_kernel,
        out_shape=jax.ShapeDtypeStruct((passes, 2, pulses, cols), bf),
        in_specs=[SMEM, VMEM, VMEM],
        out_specs=VMEM,
        name="focus",
    )(lateral, echo, slant)
    focus = lax.all_to_all(focus, near, 0, 0, tiled=True)
    mine = (lax.axis_index("x") * 2 + lax.axis_index("c")).astype(jnp.int32).reshape(1)
    image = pl.pallas_call(
        image_kernel,
        out_shape=jax.ShapeDtypeStruct((2 * rows, cols), bf),
        in_specs=[SMEM, SMEM, VMEM, VMEM],
        out_specs=VMEM,
        scratch_shapes=[pltpu.VMEM((rows + ROW_MAX + 8, cols), jnp.float32)] * 2,
        compiler_params=pltpu.CompilerParams(vmem_limit_bytes=40 << 20),
        name="image",
    )(mine, vertical, at, focus)
    image = lax.all_to_all(image, every, 0, 0, tiled=True)

    order = survey.reshape(total // passes, passes).T.reshape(total)
    cos, sin = steering(spacings, order)
    g = jnp.concatenate(
        [jnp.concatenate([cos, -sin], axis=1), jnp.concatenate([sin, cos], axis=1)], axis=0
    )
    gb = (g / total).astype(bf)
    hb = (g.T / BINS).astype(bf)
    nx = lax.axis_size("x")
    nz = lax.axis_size("zh")
    own = 4
    image = image.reshape(nx, nz, total // nx, 2 * own, cols)
    return pl.pallas_call(
        recover_kernel,
        grid=(own,),
        out_shape=jax.ShapeDtypeStruct((2, own, cols, BINS), jnp.float32),
        in_specs=[
            pl.BlockSpec(image.shape, lambda i: (0, 0, 0, 0, 0)),
            pl.BlockSpec(gb.shape, lambda i: (0, 0)),
            pl.BlockSpec(hb.shape, lambda i: (0, 0)),
        ],
        out_specs=pl.BlockSpec((2, 1, cols, BINS), lambda i: (0, i, 0, 0)),
        scratch_shapes=[pltpu.VMEM((cols // 128, total * 2 * own, 128), jnp.float32)],
        compiler_params=pltpu.CompilerParams(vmem_limit_bytes=40 << 20),
        name="recover",
    )(image, gb, hb)


def solution(mesh):
    fine = Mesh(mesh.devices.reshape(4, 4, 2, 4, 2), ("x", "zh", "c", "y", "zl"))
    ap = ("x", "zh", "c")
    group = ("y", "zl")
    return jax.shard_map(
        body,
        mesh=fine,
        in_specs=(
            P(None, group, ap, None),
            P(None, None, ap),
            P(),
            P(group),
            P(group),
            P(),
            P(),
        ),
        out_specs=P(None, ap + group, None, None),
        check_vma=False,
    )
```

time: 219 us -> 105 us (0.48)
  waiting for transfers between devices: 130 us -> 54.5 us
  matrix products: 40 us -> 0 us
  local copies, waits for them, and re-layouts: 20.7 us -> 2.63 us
  starting transfers between devices: 4.16 us -> 18.4 us
  Pallas kernels: 0 us -> 14.2 us
  other arithmetic: 9.16 us -> 1.38 us
    reduce_scatter x1 -> x0, waiting for transfers between devices: 124 us -> none  [body(): lax.psum_scatter(jnp.stack([image_re, image_im]).astype(jnp.bfloat16), 'a...]
    dot_general x36 -> x0, matrix products: 40 us -> none  [the longest x4 3.94 us: shrink_steps(): jnp.dot(resid_re, quadrature_phasor_part)]
    all_to_all x1 -> x2, waiting for transfers between devices: 5.92 us -> 39.9 us  [the longest x1 30.4 us: body(): image = lax.all_to_all(image, every, 0, 0, tiled=True)]
    gather x41 -> x0, local copies, waits for them, and re-layouts: 16 us -> none
    all_to_all x1 -> x2, starting transfers between devices: 4.16 us -> 18.4 us  [the longest x1 11.8 us: body(): image = lax.all_to_all(image, every, 0, 0, tiled=True)]
    pallas_call x0 -> x3, Pallas kernels: none -> 14.2 us  [the longest x1 6.79 us: body(): pl.pallas_call(recover_kernel, grid=(own,), out_shape=jax.ShapeDtypeStruc...]
    all_gather x0 -> x1, waiting for transfers between devices: none -> 13.9 us  [body(): at = lax.all_gather(jnp.transpose(along, (0, 2, 1)), near, axis=0)]
    another operation x2 -> x0, other arithmetic: 8.96 us -> none  [the longest x1 6.19 us: body(): jnp.stack([image_re, image_im]).astype(jnp.bfloat16)]
  transfers between devices with their start and end apart: 2 -> 3, of which waited for: 2 -> 3; matrix products, arithmetic and copies ran while one was open for 0% -> 2% of each run, Pallas kernels for 0% -> 4%
where the time goes in v1:
time: 105 us
  waiting for transfers between devices  54.5 us (52%)
  starting transfers between devices  18.4 us (18%)
  Pallas kernels  14.2 us (14%)
  between operations  13.5 us (13%)
  local copies, waits for them, and re-layouts  2.63 us (3%)
  other arithmetic  1.38 us (1%)
    all_to_all x1, waiting for transfers between devices, body(): image = lax.all_to_all(image, every, 0, 0, tiled=True)  30.4 us
    all_gather x1, waiting for transfers between devices, body(): at = lax.all_gather(jnp.transpose(along, (0, 2, 1)), near, axis=0)  13.9 us
    all_to_all x1, starting transfers between devices, body(): image = lax.all_to_all(image, every, 0, 0, tiled=True)  11.8 us
    all_to_all x1, waiting for transfers between devices, body(): focus = lax.all_to_all(focus, near, 0, 0, tiled=True)  9.5 us
    pallas_call x1, Pallas kernels, body(): pl.pallas_call(recover_kernel, grid=(own,), out_shape=jax.ShapeDtypeStruc...  6.79 us
    all_to_all x1, starting transfers between devices, body(): focus = lax.all_to_all(focus, near, 0, 0, tiled=True)  6.64 us
    pallas_call x1, Pallas kernels, body(): pl.pallas_call(focus_kernel, out_shape=jax.ShapeDtypeStruct((passes, 2, p...  3.81 us
    pallas_call x1, Pallas kernels, body(): pl.pallas_call(image_kernel, out_shape=jax.ShapeDtypeStruct((2 * rows, co...  3.55 us
  transfers between devices with their start and end apart: 3, of which 3 were waited for; matrix products, arithmetic and copies ran while one was open for 2% of the time, Pallas kernels for 4%

profile of v1, /device:TPU:1, one launch (start us, length us, event | category | flops | bytes accessed | tf_op | source)
XLA Modules:
  0.0 104.6 jit_solution(10586808147856664523)
XLA Ops:
  6.5 0.0 all-gather.3.cloned.1.call-start
  6.5 0.7 all-gather.3.cloned.1.call-update
  7.3 0.0 copy-start.2
  7.3 0.0 copy-start.3
  7.3 3.8 %focus.1 = bf16[8,2,64,256]{3,2,1,0:T(8,128)(2,1)} custom-call(s32[8]{0:T(128)} %lat_ref.1, bf16[2,8,64,512]{3,2,1,0:T(8,128)(2,1)} %echo_ref.1, bf16[2,512,256]{2,1,0:T(8,128)(2,1)} %kern_ref.1), custom_call_target="tpu_custom_call" | custom-call | tf_op jit(solution)/shard_map/focus/pallas_call | solution.py:139
  11.1 6.6 %all-to-all-start = ((bf16[8,2,64,256]{3,2,1,0:T(8,128)(2,1)}), bf16[8,2,64,256]{3,2,1,0:T(8,128)(2,1)S(1)}, u32[]{:S(2)}, u32[]{:S(2)}) async-start(bf16[8,2,64,256]{3,2,1,0:T(8,128)(2,1)} %focus.1), calls=%async_computation | async-start | bytes 1048576 | tf_op jit(solution)/shard_map/all_to_all | solution.py:146
  17.7 9.5 %all-to-all-done.f_ref = bf16[8,2,64,256]{3,2,1,0:T(8,128)(2,1)S(1)} async-done(((bf16[8,2,64,256]{3,2,1,0:T(8,128)(2,1)}), bf16[8,2,64,256]{3,2,1,0:T(8,128)(2,1)S(1)}, u32[]{:S(2)}, u32[]{:S(2)}) %all-to-all-start) | async-done | bytes 524320 | tf_op jit(solution)/shard_map/all_to_all | solution.py:146
  27.2 13.9 %all-gather.3.cloned.1.call-done = bf16[16,64,1024]{2,1,0:T(8,128)(2,1)} async-done(((bf16[2,64,1024]{2,1,0:T(8,128)(2,1)}), bf16[16,64,1024]{2,1,0:T(8,128)(2,1)}) %all-gather.3.cloned.1.call-update) | async-done | bytes 2097168 | tf_op jit(solution)/shard_map/all_gather | solution.py:138
  41.2 0.0 copy-start
  41.2 1.6 %copy-done = bf16[16,64,1024]{2,1,0:T(8,128)(2,1)S(1)} copy-done((bf16[16,64,1024]{2,1,0:T(8,128)(2,1)S(1)}, bf16[16,64,1024]{2,1,0:T(8,128)(2,1)}, u32[]{:S(2)}) %copy-start) | copy-done | bytes 2097176
  42.7 0.0 copy-start.1
  42.8 0.7 copy-done.1
  43.4 3.5 %image.1 = bf16[2048,256]{1,0:T(8,128)(2,1)} custom-call(s32[1]{0:T(128)} %bitcast.q_ref, s32[8]{0:T(128)S(1)} %copy-done.1, bf16[8,2,64,1024]{3,2,1,0:T(8,128)(2,1)S(1)} %bitcast.9, bf16[8,2,64,256]{3,2,1,0:T(8,128)(2,1)S(1)} %all-to-all-done.f_ref), custom_call_target="tpu_custom_call" | custom-call | tf_op jit(solution)/shard_map/image/pallas_call | solution.py:148
  47.0 11.8 %all-to-all-start.1 = ((bf16[256,8,256]{2,1,0:T(8,128)(2,1)}), bf16[256,8,256]{2,1,0:T(8,128)(2,1)S(1)}, u32[]{:S(2)}, u32[]{:S(2)}) async-start(bf16[256,8,256]{2,1,0:T(8,128)(2,1)} %bitcast.3), calls=%async_computation.1 | async-start | bytes 2097152 | tf_op jit(solution)/shard_map/all_to_all | solution.py:157
  58.7 0.0 copy-done.2
  58.8 0.1 reshape.25
  58.8 0.1 copy.12
  58.9 0.1 eq.15
  59.0 0.0 copy-done.3
  59.0 0.2 select_reduce_fusion
  59.2 1.0 fusion.1
  60.2 0.2 fusion
  60.4 0.1 copy.13.g_ref
  60.6 30.4 %all-to-all-done.1 = bf16[256,8,256]{2,1,0:T(8,128)(2,1)S(1)} async-done(((bf16[256,8,256]{2,1,0:T(8,128)(2,1)}), bf16[256,8,256]{2,1,0:T(8,128)(2,1)S(1)}, u32[]{:S(2)}, u32[]{:S(2)}) %all-to-all-start.1) | async-done | bytes 1048608 | tf_op jit(solution)/shard_map/all_to_all | solution.py:157
  90.9 6.8 %recover.1 = f32[2,4,256,512]{3,2,1,0:T(8,128)} custom-call(bf16[4,4,16,8,256]{4,3,2,1,0:T(8,128)(2,1)S(1)} %bitcast.8, bf16[128,1024]{1,0:T(8,128)(2,1)S(1)} %copy.13.g_ref, bf16[1024,128]{1,0:T(8,128)(2,1)S(1)} %get-tuple-element.5.h_ref), custom_call_target="tpu_custom_call" | custom-call | tf_op jit(solution)/shard_map/recover/pallas_call | solution.py:170
  (2 shorter events, 0.0 us)
Async XLA Ops:
  6.5 34.6 %all-gather.3.cloned.1.call-start = ((), (), s32[]{:S(2)}) async-start(), calls=%async_computation.2 | async-start | bytes 2359296 | tf_op jit(solution)/shard_map/all_gather | solution.py:138
  7.3 51.5 %copy-start.2 = (s32[64]{0:T(128)S(1)}, s32[64]{0:T(128)}, u32[]{:S(2)}) copy-start(s32[64]{0:T(128)} %param.12) | copy-start | bytes 772
  7.3 51.7 %copy-start.3 = (f32[64]{0:T(128)S(1)}, f32[64]{0:T(128)}, u32[]{:S(2)}) copy-start(f32[64]{0:T(128)} %param.13) | copy-start | bytes 772
  11.1 16.1 %all-to-all-start = ((bf16[8,2,64,256]{3,2,1,0:T(8,128)(2,1)}), bf16[8,2,64,256]{3,2,1,0:T(8,128)(2,1)S(1)}, u32[]{:S(2)}, u32[]{:S(2)}) async-start(bf16[8,2,64,256]{3,2,1,0:T(8,128)(2,1)} %focus.1), calls=%async_computation | async-start | bytes 1048576 | tf_op jit(solution)/shard_map/all_to_all | solution.py:146
  41.2 1.6 %copy-start = (bf16[16,64,1024]{2,1,0:T(8,128)(2,1)S(1)}, bf16[16,64,1024]{2,1,0:T(8,128)(2,1)}, u32[]{:S(2)}) copy-start(bf16[16,64,1024]{2,1,0:T(8,128)(2,1)} %all-gather.3.cloned.1.call-done) | copy-start | bytes 6291460
  42.7 0.7 copy-start.1
  47.0 44.0 %all-to-all-start.1 = ((bf16[256,8,256]{2,1,0:T(8,128)(2,1)}), bf16[256,8,256]{2,1,0:T(8,128)(2,1)S(1)}, u32[]{:S(2)}, u32[]{:S(2)}) async-start(bf16[256,8,256]{2,1,0:T(8,128)(2,1)} %bitcast.3), calls=%async_computation.1 | async-start | bytes 2097152 | tf_op jit(solution)/shard_map/all_to_all | solution.py:157
Sparse Core Ops, SparseCore 0:
  9.2 31.8 all-gather.2

commit v2 on v1

--- a/solution.py
+++ b/solution.py
@@ -36,18 +36,20 @@
         out_ref[q, 1] = fi.astype(out_ref.dtype)
 
 
-def image_kernel(q_ref, ver_ref, at_ref, f_ref, out_ref, re_ref, im_ref):
-    parts, _, pulses, rows = at_ref.shape
-    cols = f_ref.shape[3]
-    lag = ver_ref[q_ref[0]]
-    fr = f_ref[:, 0].reshape(parts * pulses, cols)
-    fi = f_ref[:, 1].reshape(parts * pulses, cols)
+def image_kernel(order_ref, ver_ref, *refs):
+    f_ref, out_ref, re_ref, im_ref = refs[-4:]
+    at_refs = refs[:-4]
+    _, _, _, cols = f_ref.shape
+    rows = at_refs[0].shape[2]
+    lag = ver_ref[order_ref[0]]
+    fr = jnp.concatenate([f_ref[order_ref[k], 0] for k in range(len(at_refs))], axis=0)
+    fi = jnp.concatenate([f_ref[order_ref[k], 1] for k in range(len(at_refs))], axis=0)
     re_ref[0:ROW_MAX] = jnp.zeros((ROW_MAX, cols), jnp.float32)
     im_ref[0:ROW_MAX] = jnp.zeros((ROW_MAX, cols), jnp.float32)
     step = 256
     for r0 in range(0, rows, step):
-        ar = at_ref[:, 0, :, r0 : r0 + step].reshape(parts * pulses, step)
-        ai = at_ref[:, 1, :, r0 : r0 + step].reshape(parts * pulses, step)
+        ar = jnp.concatenate([ref[0, :, r0 : r0 + step] for ref in at_refs], axis=0)
+        ai = jnp.concatenate([ref[1, :, r0 : r0 + step] for ref in at_refs], axis=0)
         re_ref[ROW_MAX + r0 : ROW_MAX + r0 + step] = dot(ar, fr, 0, 0) - dot(ai, fi, 0, 0)
         im_ref[ROW_MAX + r0 : ROW_MAX + r0 + step] = dot(ar, fi, 0, 0) + dot(ai, fr, 0, 0)
     block = 128
@@ -135,7 +137,18 @@
     every = ("x", "zh", "c", "y", "zl")
     bf = jnp.bfloat16
 
-    at = lax.all_gather(jnp.transpose(along, (0, 2, 1)), near, axis=0)
+    nx = lax.axis_size("x")
+    nz = lax.axis_size("zh")
+
+    def turn(value, step):
+        return lax.ppermute(value, "x", [(i, (i + step) % nx) for i in range(nx)])
+
+    def swap(value):
+        return lax.ppermute(value, "c", [(0, 1), (1, 0)])
+
+    at = jnp.transpose(along, (0, 2, 1))
+    held = [at] + [turn(at, s) for s in range(1, nx)]
+    held = held + [swap(value) for value in held]
     focus = pl.pallas_call(
         focus_kernel,
         out_shape=jax.ShapeDtypeStruct((passes, 2, pulses, cols), bf),
@@ -144,27 +157,28 @@
         name="focus",
     )(lateral, echo, slant)
     focus = lax.all_to_all(focus, near, 0, 0, tiled=True)
-    mine = (lax.axis_index("x") * 2 + lax.axis_index("c")).astype(jnp.int32).reshape(1)
+    x = lax.axis_index("x")
+    c = lax.axis_index("c")
+    steps = jnp.arange(2 * nx, dtype=jnp.int32)
+    order = (x - steps % nx) % nx * 2 + (c + steps // nx) % 2
     image = pl.pallas_call(
         image_kernel,
         out_shape=jax.ShapeDtypeStruct((2 * rows, cols), bf),
-        in_specs=[SMEM, SMEM, VMEM, VMEM],
+        in_specs=[SMEM, SMEM] + [VMEM] * (2 * nx + 1),
         out_specs=VMEM,
         scratch_shapes=[pltpu.VMEM((rows + ROW_MAX + 8, cols), jnp.float32)] * 2,
         compiler_params=pltpu.CompilerParams(vmem_limit_bytes=40 << 20),
         name="image",
-    )(mine, vertical, at, focus)
+    )(order.astype(jnp.int32), vertical, *held, focus)
     image = lax.all_to_all(image, every, 0, 0, tiled=True)
 
-    order = survey.reshape(total // passes, passes).T.reshape(total)
-    cos, sin = steering(spacings, order)
+    source = survey.reshape(total // passes, passes).T.reshape(total)
+    cos, sin = steering(spacings, source)
     g = jnp.concatenate(
         [jnp.concatenate([cos, -sin], axis=1), jnp.concatenate([sin, cos], axis=1)], axis=0
     )
     gb = (g / total).astype(bf)
     hb = (g.T / BINS).astype(bf)
-    nx = lax.axis_size("x")
-    nz = lax.axis_size("zh")
     own = 4
     image = image.reshape(nx, nz, total // nx, 2 * own, cols)
     return pl.pallas_call(

time: 105 us -> 81.4 us (0.78)
  waiting for transfers between devices: 54.5 us -> 38.2 us
  between operations: 13.5 us -> 0.09 us
  starting transfers between devices: 18.4 us -> 25.3 us
    all_gather x1 -> x0, waiting for transfers between devices: 13.9 us -> none  [body(): at = lax.all_gather(jnp.transpose(along, (0, 2, 1)), near, axis=0)]
    ppermute x0 -> x7, starting transfers between devices: none -> 6.44 us  [the longest x3 4.43 us: turn(): return lax.ppermute(value, 'x', [(i, (i + step) % nx) for i in range(nx)])]
    all_to_all x1, waiting for transfers between devices: 9.5 us -> 4.73 us  [body(): focus = lax.all_to_all(focus, near, 0, 0, tiled=True)]
    ppermute x0 -> x7, waiting for transfers between devices: none -> 3.11 us  [the longest x3 3.1 us: turn(): return lax.ppermute(value, 'x', [(i, (i + step) % nx) for i in range(nx)])]
  transfers between devices with their start and end apart: 3 -> 9, of which waited for: 3 -> 3; matrix products, arithmetic and copies ran while one was open for 2% -> 2% of each run, Pallas kernels for 4% -> 5%
where the time goes in v2:
time: 81.4 us; the launch traced here: 81.1 us
  waiting for transfers between devices  38.2 us (47%)
  starting transfers between devices  25.3 us (31%)
  Pallas kernels  14.2 us (17%)
  local copies, waits for them, and re-layouts  1.98 us (2%)
  other arithmetic  1.4 us (2%)
    all_to_all x1, waiting for transfers between devices, body(): image = lax.all_to_all(image, every, 0, 0, tiled=True)  30.4 us
    all_to_all x1, starting transfers between devices, body(): image = lax.all_to_all(image, every, 0, 0, tiled=True)  12.6 us
    pallas_call x1, Pallas kernels, body(): pl.pallas_call(recover_kernel, grid=(own,), out_shape=jax.ShapeDtypeStruc...  6.8 us
    all_to_all x1, starting transfers between devices, body(): focus = lax.all_to_all(focus, near, 0, 0, tiled=True)  6.24 us
    all_to_all x1, waiting for transfers between devices, body(): focus = lax.all_to_all(focus, near, 0, 0, tiled=True)  4.73 us
    ppermute x3, starting transfers between devices, turn(): return lax.ppermute(value, 'x', [(i, (i + step) % nx) for i in range(nx)])  4.43 us
    pallas_call x1, Pallas kernels, body(): pl.pallas_call(focus_kernel, out_shape=jax.ShapeDtypeStruct((passes, 2, p...  3.8 us
    pallas_call x1, Pallas kernels, body(): pl.pallas_call(image_kernel, out_shape=jax.ShapeDtypeStruct((2 * rows, co...  3.58 us
  transfers between devices with their start and end apart: 9, of which 3 were waited for; matrix products, arithmetic and copies ran while one was open for 2% of the time, Pallas kernels for 5%

profile of v2, /device:TPU:1, one launch (start us, length us, event | category | flops | bytes accessed | tf_op | source)
XLA Modules:
  0.0 81.1 jit_solution(14980065042150409702)
XLA Ops:
  0.0 3.3 %collective-permute-start.2 = (bf16[2,64,1024]{2,1,0:T(8,128)(2,1)}, bf16[2,64,1024]{2,1,0:T(8,128)(2,1)S(1)}, u32[]{:S(2)}, u32[]{:S(2)}) collective-permute-start(bf16[2,64,1024]{2,1,0:T(8,128)(2,1)} %bitcast.7), channel_id=1, source_target_pairs={{0,192},{64,0},{128,64},{192,128},{1,193},{65,1},{129,65},{193,129... | collective-permute-start | bytes 786440 | tf_op jit(solution)/shard_map/ppermute | solution.py:144
  3.3 0.5 collective-permute-start.1
  3.8 0.6 collective-permute-start
  4.4 3.8 %focus.1 = bf16[8,2,64,256]{3,2,1,0:T(8,128)(2,1)} custom-call(s32[8]{0:T(128)} %lat_ref.1, bf16[2,8,64,512]{3,2,1,0:T(8,128)(2,1)} %echo_ref.1, bf16[2,512,256]{2,1,0:T(8,128)(2,1)} %kern_ref.1), custom_call_target="tpu_custom_call" | custom-call | tf_op jit(solution)/shard_map/focus/pallas_call | solution.py:152
  8.2 6.2 %all-to-all-start = ((bf16[8,2,64,256]{3,2,1,0:T(8,128)(2,1)}), bf16[8,2,64,256]{3,2,1,0:T(8,128)(2,1)S(1)}, u32[]{:S(2)}, u32[]{:S(2)}) async-start(bf16[8,2,64,256]{3,2,1,0:T(8,128)(2,1)} %focus.1), calls=%async_computation | async-start | bytes 1048576 | tf_op jit(solution)/shard_map/all_to_all | solution.py:159
  14.5 0.0 collective-permute-start.3
  14.5 0.0 collective-permute-done.2.refs_3_
  14.5 1.3 %collective-permute-start.6 = (bf16[2,64,1024]{2,1,0:T(8,128)(2,1)S(1)}, bf16[2,64,1024]{2,1,0:T(8,128)(2,1)S(1)}, u32[]{:S(2)}, u32[]{:S(2)}) collective-permute-start(bf16[2,64,1024]{2,1,0:T(8,128)(2,1)S(1)} %collective-permute-done.2.refs_3_), channel_id=1, source_target_pairs={{0,8},{8,0},{1,9},{9,1},{2,10},{10,2},{3,11},{11,3},{4,12},{12,4},... | collective-permute-start | bytes 786440 | tf_op jit(solution)/shard_map/ppermute | solution.py:147
  15.8 0.0 collective-permute-done.1.refs_2_
  15.8 0.0 collective-permute-start.5
  15.8 3.1 %collective-permute-done.refs_1_ = bf16[2,64,1024]{2,1,0:T(8,128)(2,1)S(1)} collective-permute-done((bf16[2,64,1024]{2,1,0:T(8,128)(2,1)}, bf16[2,64,1024]{2,1,0:T(8,128)(2,1)S(1)}, u32[]{:S(2)}, u32[]{:S(2)}) %collective-permute-start) | collective-permute-done | bytes 262176 | tf_op jit(solution)/shard_map/ppermute | solution.py:144
  18.9 0.7 collective-permute-start.4
  19.6 0.0 collective-permute-done.3.refs_4_
  19.6 4.7 %all-to-all-done.refs_8_ = bf16[8,2,64,256]{3,2,1,0:T(8,128)(2,1)S(1)} async-done(((bf16[8,2,64,256]{3,2,1,0:T(8,128)(2,1)}), bf16[8,2,64,256]{3,2,1,0:T(8,128)(2,1)S(1)}, u32[]{:S(2)}, u32[]{:S(2)}) %all-to-all-start) | async-done | bytes 524320 | tf_op jit(solution)/shard_map/all_to_all | solution.py:159
  24.3 0.0 collective-permute-done.6.refs_7_
  24.4 0.0 collective-permute-done.5.refs_6_
  24.4 0.0 collective-permute-done.4.refs_5_
  24.4 0.0 copy-start
  24.4 0.9 %copy-done = bf16[2,1024,64]{1,2,0:T(8,128)(2,1)S(1)} copy-done((bf16[2,1024,64]{1,2,0:T(8,128)(2,1)S(1)}, bf16[2,1024,64]{1,2,0:T(8,128)(2,1)}, u32[]{:S(2)}) %copy-start) | copy-done | bytes 262168
  25.3 0.7 copy-done.1
  26.0 3.6 %image.1 = bf16[2048,256]{1,0:T(8,128)(2,1)} custom-call(s32[8]{0:T(128)S(1)} %fusion.2.order_ref, s32[8]{0:T(128)S(1)} %copy-done.1, bf16[2,64,1024]{2,1,0:T(8,128)(2,1)S(1)} %bitcast.11, bf16[2,64,1024]{2,1,0:T(8,128)(2,1)S(1)} %collective-permute-done.refs_1_, bf16[2,64,1024]{2,1,0:T(8,128)(2,1)S(1)} %collective-permute-done.1.refs_2_, ...), custom_call_target="tpu_custom_call" | custom-call | tf_op jit(solution)/shard_map/image/pallas_call | solution.py:164
  29.6 12.6 %all-to-all-start.1 = ((bf16[256,8,256]{2,1,0:T(8,128)(2,1)}), bf16[256,8,256]{2,1,0:T(8,128)(2,1)S(1)}, u32[]{:S(2)}, u32[]{:S(2)}) async-start(bf16[256,8,256]{2,1,0:T(8,128)(2,1)} %bitcast.1), calls=%async_computation.1 | async-start | bytes 2097152 | tf_op jit(solution)/shard_map/all_to_all | solution.py:173
  42.1 0.0 copy-done.2
  42.2 0.1 reshape.21
  42.2 0.1 copy.10
  42.3 0.1 eq.19
  42.4 0.2 select_reduce_fusion
  42.6 1.0 %fusion.1 = (f32[64,512]{0,1:T(8,128)S(1)}, f32[64,512]{0,1:T(8,128)S(1)}, f32[64,512]{0,1:T(8,128)S(1)}) fusion(f32[512]{0:T(512)S(1)} %convert_add_fusion, f32[64]{0:T(128)S(1)} %broadcast_multiply_fusion), kind=kLoop, calls=%fused_computation.6 | loop fusion | flops 65536 | bytes 395520 | tf_op jit(solution)/shard_map/neg | solution.py:178
  43.6 0.2 fusion
  43.8 0.1 copy.11.g_ref
  44.0 30.4 %all-to-all-done.1 = bf16[256,8,256]{2,1,0:T(8,128)(2,1)S(1)} async-done(((bf16[256,8,256]{2,1,0:T(8,128)(2,1)}), bf16[256,8,256]{2,1,0:T(8,128)(2,1)S(1)}, u32[]{:S(2)}, u32[]{:S(2)}) %all-to-all-start.1) | async-done | bytes 1048608 | tf_op jit(solution)/shard_map/all_to_all | solution.py:173
  74.3 6.8 %recover.1 = f32[2,4,256,512]{3,2,1,0:T(8,128)} custom-call(bf16[4,4,16,8,256]{4,3,2,1,0:T(8,128)(2,1)S(1)} %bitcast.6, bf16[128,1024]{1,0:T(8,128)(2,1)S(1)} %copy.11.g_ref, bf16[1024,128]{1,0:T(8,128)(2,1)S(1)} %get-tuple-element.5.h_ref), custom_call_target="tpu_custom_call" | custom-call | tf_op jit(solution)/shard_map/recover/pallas_call | solution.py:184
  (7 shorter events, 0.0 us)
Async XLA Ops:
  0.0 42.1 %copy-start.2 = (s32[64]{0:T(128)S(1)}, s32[64]{0:T(128)}, u32[]{:S(2)}) copy-start(s32[64]{0:T(128)} %param.12) | copy-start | bytes 772
  0.0 42.4 %copy-start.3 = (f32[64]{0:T(128)S(1)}, f32[64]{0:T(128)}, u32[]{:S(2)}) copy-start(f32[64]{0:T(128)} %param.13) | copy-start | bytes 772
  0.0 14.5 %collective-permute-start.2 = (bf16[2,64,1024]{2,1,0:T(8,128)(2,1)}, bf16[2,64,1024]{2,1,0:T(8,128)(2,1)S(1)}, u32[]{:S(2)}, u32[]{:S(2)}) collective-permute-start(bf16[2,64,1024]{2,1,0:T(8,128)(2,1)} %bitcast.7), channel_id=1, source_target_pairs={{0,192},{64,0},{128,64},{192,128},{1,193},{65,1},{129,65},{193,129... | collective-permute-start | bytes 786440 | tf_op jit(solution)/shard_map/ppermute | solution.py:144
  3.3 12.5 %collective-permute-start.1 = (bf16[2,64,1024]{2,1,0:T(8,128)(2,1)}, bf16[2,64,1024]{2,1,0:T(8,128)(2,1)S(1)}, u32[]{:S(2)}, u32[]{:S(2)}) collective-permute-start(bf16[2,64,1024]{2,1,0:T(8,128)(2,1)} %bitcast.8), channel_id=1, source_target_pairs={{0,128},{64,192},{128,0},{192,64},{1,129},{65,193},{129,1},{193,65... | collective-permute-start | bytes 786440 | tf_op jit(solution)/shard_map/ppermute | solution.py:144
  3.8 15.0 %collective-permute-start = (bf16[2,64,1024]{2,1,0:T(8,128)(2,1)}, bf16[2,64,1024]{2,1,0:T(8,128)(2,1)S(1)}, u32[]{:S(2)}, u32[]{:S(2)}) collective-permute-start(bf16[2,64,1024]{2,1,0:T(8,128)(2,1)} %bitcast.9), channel_id=1, source_target_pairs={{0,64},{64,128},{128,192},{192,0},{1,65},{65,129},{129,193},{193,1... | collective-permute-start | bytes 786440 | tf_op jit(solution)/shard_map/ppermute | solution.py:144
  8.2 16.1 %all-to-all-start = ((bf16[8,2,64,256]{3,2,1,0:T(8,128)(2,1)}), bf16[8,2,64,256]{3,2,1,0:T(8,128)(2,1)S(1)}, u32[]{:S(2)}, u32[]{:S(2)}) async-start(bf16[8,2,64,256]{3,2,1,0:T(8,128)(2,1)} %focus.1), calls=%async_computation | async-start | bytes 1048576 | tf_op jit(solution)/shard_map/all_to_all | solution.py:159
  14.5 5.1 %collective-permute-start.3 = (bf16[2,64,1024]{2,1,0:T(8,128)(2,1)}, bf16[2,64,1024]{2,1,0:T(8,128)(2,1)S(1)}, u32[]{:S(2)}, u32[]{:S(2)}) collective-permute-start(bf16[2,64,1024]{2,1,0:T(8,128)(2,1)} %bitcast.10), channel_id=1, source_target_pairs={{0,8},{8,0},{1,9},{9,1},{2,10},{10,2},{3,11},{11,3},{4,12},{12,4},... | collective-permute-start | bytes 786440 | tf_op jit(solution)/shard_map/ppermute | solution.py:147
  14.5 9.9 %collective-permute-start.6 = (bf16[2,64,1024]{2,1,0:T(8,128)(2,1)S(1)}, bf16[2,64,1024]{2,1,0:T(8,128)(2,1)S(1)}, u32[]{:S(2)}, u32[]{:S(2)}) collective-permute-start(bf16[2,64,1024]{2,1,0:T(8,128)(2,1)S(1)} %collective-permute-done.2.refs_3_), channel_id=1, source_target_pairs={{0,8},{8,0},{1,9},{9,1},{2,10},{10,2},{3,11},{11,3},{4,12},{12,4},... | collective-permute-start | bytes 786440 | tf_op jit(solution)/shard_map/ppermute | solution.py:147
  15.8 8.6 %collective-permute-start.5 = (bf16[2,64,1024]{2,1,0:T(8,128)(2,1)S(1)}, bf16[2,64,1024]{2,1,0:T(8,128)(2,1)S(1)}, u32[]{:S(2)}, u32[]{:S(2)}) collective-permute-start(bf16[2,64,1024]{2,1,0:T(8,128)(2,1)S(1)} %collective-permute-done.1.refs_2_), channel_id=1, source_target_pairs={{0,8},{8,0},{1,9},{9,1},{2,10},{10,2},{3,11},{11,3},{4,12},{12,4},... | collective-permute-start | bytes 786440 | tf_op jit(solution)/shard_map/ppermute | solution.py:147
  18.9 5.5 %collective-permute-start.4 = (bf16[2,64,1024]{2,1,0:T(8,128)(2,1)S(1)}, bf16[2,64,1024]{2,1,0:T(8,128)(2,1)S(1)}, u32[]{:S(2)}, u32[]{:S(2)}) collective-permute-start(bf16[2,64,1024]{2,1,0:T(8,128)(2,1)S(1)} %collective-permute-done.refs_1_), channel_id=1, source_target_pairs={{0,8},{8,0},{1,9},{9,1},{2,10},{10,2},{3,11},{11,3},{4,12},{12,4},... | collective-permute-start | bytes 786440 | tf_op jit(solution)/shard_map/ppermute | solution.py:147
  24.4 1.0 %copy-start = (bf16[2,1024,64]{1,2,0:T(8,128)(2,1)S(1)}, bf16[2,1024,64]{1,2,0:T(8,128)(2,1)}, u32[]{:S(2)}) copy-start(bf16[2,1024,64]{1,2,0:T(8,128)(2,1)} %param.8) | copy-start | bytes 786436
  25.3 0.7 copy-start.1
  29.6 44.8 %all-to-all-start.1 = ((bf16[256,8,256]{2,1,0:T(8,128)(2,1)}), bf16[256,8,256]{2,1,0:T(8,128)(2,1)S(1)}, u32[]{:S(2)}, u32[]{:S(2)}) async-start(bf16[256,8,256]{2,1,0:T(8,128)(2,1)} %bitcast.1), calls=%async_computation.1 | async-start | bytes 2097152 | tf_op jit(solution)/shard_map/all_to_all | solution.py:173

commit v3 on v2

--- a/solution.py
+++ b/solution.py
@@ -1,3 +1,5 @@
+import functools
+
 import jax
 import jax.numpy as jnp
 from jax import lax
@@ -22,26 +24,25 @@
     passes, _, pulses, cols = out_ref.shape
     kr = kern_ref[0]
     ki = kern_ref[1]
+    er = echo_ref[0].reshape(passes * pulses, -1)
+    ei = echo_ref[1].reshape(passes * pulses, -1)
+    fr = dot(er, kr, 1, 0) - dot(ei, ki, 1, 0)
+    fi = dot(er, ki, 1, 0) + dot(ei, kr, 1, 0)
     col = lax.broadcasted_iota(jnp.int32, (pulses, cols), 1)
     for q in range(passes):
-        er = echo_ref[0, q]
-        ei = echo_ref[1, q]
         lag = lat_ref[q]
         keep = col >= lag
-        fr = dot(er, kr, 1, 0) - dot(ei, ki, 1, 0)
-        fi = dot(er, ki, 1, 0) + dot(ei, kr, 1, 0)
-        fr = jnp.where(keep, pltpu.roll(fr, lag, 1), 0.0)
-        fi = jnp.where(keep, pltpu.roll(fi, lag, 1), 0.0)
-        out_ref[q, 0] = fr.astype(out_ref.dtype)
-        out_ref[q, 1] = fi.astype(out_ref.dtype)
-
-
-def image_kernel(order_ref, ver_ref, *refs):
+        for part, value in enumerate((fr, fi)):
+            moved = pltpu.roll(value[q * pulses : (q + 1) * pulses], lag, 1)
+            out_ref[q, part] = jnp.where(keep, moved, 0.0).astype(out_ref.dtype)
+
+
+def image_kernel(sizes, order_ref, *refs):
     f_ref, out_ref, re_ref, im_ref = refs[-4:]
     at_refs = refs[:-4]
     _, _, _, cols = f_ref.shape
     rows = at_refs[0].shape[2]
-    lag = ver_ref[order_ref[0]]
+    lag = order_ref[len(at_refs)]
     fr = jnp.concatenate([f_ref[order_ref[k], 0] for k in range(len(at_refs))], axis=0)
     fi = jnp.concatenate([f_ref[order_ref[k], 1] for k in range(len(at_refs))], axis=0)
     re_ref[0:ROW_MAX] = jnp.zeros((ROW_MAX, cols), jnp.float32)
@@ -52,65 +53,72 @@
         ai = jnp.concatenate([ref[1, :, r0 : r0 + step] for ref in at_refs], axis=0)
         re_ref[ROW_MAX + r0 : ROW_MAX + r0 + step] = dot(ar, fr, 0, 0) - dot(ai, fi, 0, 0)
         im_ref[ROW_MAX + r0 : ROW_MAX + r0 + step] = dot(ar, fi, 0, 0) + dot(ai, fr, 0, 0)
-    block = 128
+    nx, nz, nc, ny, nl = sizes
+    block = nl * ny * nc * 4
     start = ROW_MAX - lag
     base = pl.multiple_of(start // 8 * 8, 8)
     rest = start - base
 
     def shifted(ref, r0):
         wide = ref[pl.ds(base + r0, block + 8)]
-        return pltpu.roll(wide, block + 8 - rest, 0)[:block]
+        return pltpu.roll(wide, block + 8 - rest, 0)[:block].reshape(block // 8, 8, cols)
 
     sub = lax.broadcasted_iota(jnp.int32, (block // 8, 8, cols), 1)
-    for r0 in range(0, rows, block):
-        re = shifted(re_ref, r0).reshape(block // 8, 8, cols)
-        im = shifted(im_ref, r0).reshape(block // 8, 8, cols)
-        first = jnp.where(sub < 4, re, pltpu.roll(im, 4, 1))
-        second = jnp.where(sub < 4, pltpu.roll(re, 4, 1), im)
-        both = jnp.stack([first, second], axis=1).reshape(2 * block, cols)
-        out_ref[2 * r0 : 2 * r0 + 2 * block] = both.astype(out_ref.dtype)
+    for x in range(nx):
+        for z in range(nz):
+            r0 = (x * nz + z) * block
+            re = shifted(re_ref, r0)
+            im = shifted(im_ref, r0)
+            first = jnp.where(sub < 4, re, pltpu.roll(im, 4, 1))
+            second = jnp.where(sub < 4, pltpu.roll(re, 4, 1), im)
+            both = jnp.stack([first, second], axis=1).reshape(2 * block, cols).astype(out_ref.dtype)
+            span = 8 * nl
+            for c in range(nc):
+                for y in range(ny):
+                    at = (((y * nx + x) * nc + c) * nz + z) * span
+                    piece = (c * ny + y) * span
+                    out_ref[at : at + span] = both[piece : piece + span]
 
 
 def recover_kernel(img_ref, g_ref, h_ref, out_ref, y_ref):
     i = pl.program_id(0)
-    xs, parts, others, eight, cols = img_ref.shape
-    passes = xs * others
+    outer, parts, inner, eight, cols = img_ref.shape
+    passes = outer * inner
 
     @pl.when(i == 0)
     def _():
-        for x in range(xs):
-            acc = img_ref[x, 0].astype(jnp.float32)
+        some = 8
+        for k in range(0, outer, some):
+            acc = img_ref[k : k + some, 0].astype(jnp.float32)
             for z in range(1, parts):
-                acc = acc + img_ref[x, z].astype(jnp.float32)
-            acc = acc.reshape(others * eight, cols)
+                acc = acc + img_ref[k : k + some, z].astype(jnp.float32)
+            acc = acc.reshape(some * inner * eight, cols)
+            at = k * inner * eight
             for c in range(cols // 128):
-                y_ref[c, x * others * eight : (x + 1) * others * eight] = acc[:, c * 128 : c * 128 + 128]
+                y_ref[c, at : at + some * inner * eight] = acc[:, c * 128 : c * 128 + 128]
 
     g = g_ref[...]
     h = h_ref[...]
-    y = jnp.concatenate(
-        [
-            jnp.concatenate(
-                [
-                    y_ref.at[c][pl.ds(i, passes, stride=eight), :],
-                    y_ref.at[c][pl.ds(eight // 2 + i, passes, stride=eight), :],
-                ],
-                axis=0,
-            ).T
-            for c in range(cols // 128)
-        ],
-        axis=0,
-    )
-    yb = y.astype(jnp.bfloat16)
-    yt = yb.astype(jnp.float32)
-    v = dot(yb, g, 1, 0)
-    u = v - jnp.clip(v, -LEVEL, LEVEL)
+    chains = []
+    for c in range(cols // 128):
+        re = y_ref.at[c][pl.ds(i, passes, stride=eight), :]
+        im = y_ref.at[c][pl.ds(eight // 2 + i, passes, stride=eight), :]
+        y = jnp.concatenate([re, im], axis=0).T.astype(jnp.bfloat16)
+        chains += [y[:64], y[64:]]
+    wide = [y.astype(jnp.float32) for y in chains]
+
+    def shrink(v):
+        return v - jnp.clip(v, -LEVEL, LEVEL)
+
+    us = [shrink(dot(y, g, 1, 0)) for y in chains]
     for _ in range(ITERS - 1):
-        resid = yt - dot(u.astype(jnp.bfloat16), h, 1, 0)
-        v = u + dot(resid.astype(jnp.bfloat16), g, 1, 0)
-        u = v - jnp.clip(v, -LEVEL, LEVEL)
-    out_ref[0, 0] = u[:, :BINS]
-    out_ref[1, 0] = u[:, BINS:]
+        resids = [
+            (y - dot(u.astype(jnp.bfloat16), h, 1, 0)).astype(jnp.bfloat16) for y, u in zip(wide, us)
+        ]
+        us = [shrink(u + dot(r, g, 1, 0)) for u, r in zip(us, resids)]
+    for k, u in enumerate(us):
+        out_ref[0, 0, k * 64 : k * 64 + 64] = u[:, :BINS]
+        out_ref[1, 0, k * 64 : k * 64 + 64] = u[:, BINS:]
 
 
 def steering(normal_spacings, source):
@@ -134,7 +142,7 @@
     cols = slant.shape[2]
     total = survey.shape[0]
     near = ("x", "c")
-    every = ("x", "zh", "c", "y", "zl")
+    every = ("y", "x", "c", "zh", "zl")
     bf = jnp.bfloat16
 
     nx = lax.axis_size("x")
@@ -161,18 +169,22 @@
     c = lax.axis_index("c")
     steps = jnp.arange(2 * nx, dtype=jnp.int32)
     order = (x - steps % nx) % nx * 2 + (c + steps // nx) % 2
+    lag = jnp.sum(jnp.where(jnp.arange(passes, dtype=jnp.int32) == x * 2 + c, vertical, 0))
+    table = jnp.concatenate([order.astype(jnp.int32), lag.reshape(1)])
+    sizes = tuple(lax.axis_size(name) for name in ("x", "zh", "c", "y", "zl"))
     image = pl.pallas_call(
-        image_kernel,
+        functools.partial(image_kernel, sizes),
         out_shape=jax.ShapeDtypeStruct((2 * rows, cols), bf),
-        in_specs=[SMEM, SMEM] + [VMEM] * (2 * nx + 1),
+        in_specs=[SMEM] + [VMEM] * (2 * nx + 1),
         out_specs=VMEM,
         scratch_shapes=[pltpu.VMEM((rows + ROW_MAX + 8, cols), jnp.float32)] * 2,
         compiler_params=pltpu.CompilerParams(vmem_limit_bytes=40 << 20),
         name="image",
-    )(order.astype(jnp.int32), vertical, *held, focus)
+    )(table, *held, focus)
     image = lax.all_to_all(image, every, 0, 0, tiled=True)
 
-    source = survey.reshape(total // passes, passes).T.reshape(total)
+    nc, ny, nl = sizes[2:]
+    source = survey.reshape(ny, nl, nx, nc).transpose(0, 2, 3, 1).reshape(total)
     cos, sin = steering(spacings, source)
     g = jnp.concatenate(
         [jnp.concatenate([cos, -sin], axis=1), jnp.concatenate([sin, cos], axis=1)], axis=0
@@ -180,7 +192,7 @@
     gb = (g / total).astype(bf)
     hb = (g.T / BINS).astype(bf)
     own = 4
-    image = image.reshape(nx, nz, total // nx, 2 * own, cols)
+    image = image.reshape(total // nl, nz, nl, 2 * own, cols)
     return pl.pallas_call(
         recover_kernel,
         grid=(own,),

time: 81.4 us -> 79.8 us (0.980)
  waiting for transfers between devices: 38.2 us -> 34.1 us
  starting transfers between devices: 25.3 us -> 28.1 us
  other arithmetic: 1.4 us -> 3.42 us
  Pallas kernels: 14.2 us -> 12.4 us
    all_to_all x1, waiting for transfers between devices: 4.73 us -> 1.42 us  [body(): focus = lax.all_to_all(focus, near, 0, 0, tiled=True)]
    ppermute x4, starting transfers between devices: 2.01 us -> 4.07 us  [swap(): return lax.ppermute(value, 'c', [(0, 1), (1, 0)])]
    reduce_sum x0 -> x1, other arithmetic: none -> 1.32 us  [body(): jnp.sum(jnp.where(jnp.arange(passes, dtype=jnp.int32) == x * 2 + c, verti...]
    pallas_call x1, Pallas kernels: 6.8 us -> 5.93 us  [body(): pl.pallas_call(recover_kernel, grid=(own,), out_shape=jax.ShapeDtypeStruc...]
    pallas_call x1, Pallas kernels: 3.8 us -> 2.98 us  [body(): pl.pallas_call(focus_kernel, out_shape=jax.ShapeDtypeStruct((passes, 2, p...]
  transfers between devices with their start and end apart: 9 -> 9, of which waited for: 3 -> 3; matrix products, arithmetic and copies ran while one was open for 2% -> 5% of each run, Pallas kernels for 5% -> 4%
where the time goes in v3:
time: 79.8 us; the launch traced here: 79.6 us
  waiting for transfers between devices  34.1 us (43%)
  starting transfers between devices  28.1 us (35%)
  Pallas kernels  12.4 us (16%)
  other arithmetic  3.42 us (4%)
  local copies, waits for them, and re-layouts  1.54 us (2%)
    all_to_all x1, waiting for transfers between devices, body(): image = lax.all_to_all(image, every, 0, 0, tiled=True)  30.2 us
    all_to_all x1, starting transfers between devices, body(): image = lax.all_to_all(image, every, 0, 0, tiled=True)  13.3 us
    all_to_all x1, starting transfers between devices, body(): focus = lax.all_to_all(focus, near, 0, 0, tiled=True)  6.24 us
    pallas_call x1, Pallas kernels, body(): pl.pallas_call(recover_kernel, grid=(own,), out_shape=jax.ShapeDtypeStruc...  5.93 us
    ppermute x3, starting transfers between devices, turn(): return lax.ppermute(value, 'x', [(i, (i + step) % nx) for i in range(nx)])  4.43 us
    ppermute x4, starting transfers between devices, swap(): return lax.ppermute(value, 'c', [(0, 1), (1, 0)])  4.07 us
    pallas_call x1, Pallas kernels, body(): pl.pallas_call(functools.partial(image_kernel, sizes), out_shape=jax.Shap...  3.44 us
    pallas_call x1, Pallas kernels, body(): pl.pallas_call(focus_kernel, out_shape=jax.ShapeDtypeStruct((passes, 2, p...  2.98 us
  transfers between devices with their start and end apart: 9, of which 3 were waited for; matrix products, arithmetic and copies ran while one was open for 5% of the time, Pallas kernels for 4%

profile of v3, /device:TPU:1, one launch (start us, length us, event | category | flops | bytes accessed | tf_op | source)
XLA Modules:
  0.0 79.6 jit_solution(2556550027634453231)
XLA Ops:
  0.0 3.3 %collective-permute-start.2 = (bf16[2,64,1024]{2,1,0:T(8,128)(2,1)}, bf16[2,64,1024]{2,1,0:T(8,128)(2,1)S(1)}, u32[]{:S(2)}, u32[]{:S(2)}) collective-permute-start(bf16[2,64,1024]{2,1,0:T(8,128)(2,1)} %bitcast.8), channel_id=1, source_target_pairs={{0,192},{64,0},{128,64},{192,128},{1,193},{65,1},{129,65},{193,129... | collective-permute-start | bytes 786440 | tf_op jit(solution)/shard_map/ppermute | solution.py:152
  3.3 0.5 collective-permute-start.1
  3.8 0.6 collective-permute-start
  4.4 3.0 %focus.1 = bf16[8,2,64,256]{3,2,1,0:T(8,128)(2,1)} custom-call(s32[8]{0:T(128)} %lat_ref.1, bf16[2,8,64,512]{3,2,1,0:T(8,128)(2,1)} %echo_ref.1, bf16[2,512,256]{2,1,0:T(8,128)(2,1)} %kern_ref.1), custom_call_target="tpu_custom_call" | custom-call | tf_op jit(solution)/shard_map/focus/pallas_call | solution.py:160
  7.4 6.2 %all-to-all-start = ((bf16[8,2,64,256]{3,2,1,0:T(8,128)(2,1)}), bf16[8,2,64,256]{3,2,1,0:T(8,128)(2,1)S(1)}, u32[]{:S(2)}, u32[]{:S(2)}) async-start(bf16[8,2,64,256]{3,2,1,0:T(8,128)(2,1)} %focus.1), calls=%async_computation | async-start | bytes 1048576 | tf_op jit(solution)/shard_map/all_to_all | solution.py:167
  13.7 0.0 collective-permute-start.3
  13.7 0.0 collective-permute-done.2.refs_3_
  13.7 3.5 %collective-permute-start.6 = (bf16[2,64,1024]{2,1,0:T(8,128)(2,1)S(1)}, bf16[2,64,1024]{2,1,0:T(8,128)(2,1)S(1)}, u32[]{:S(2)}, u32[]{:S(2)}) collective-permute-start(bf16[2,64,1024]{2,1,0:T(8,128)(2,1)S(1)} %collective-permute-done.2.refs_3_), channel_id=1, source_target_pairs={{0,8},{8,0},{1,9},{9,1},{2,10},{10,2},{3,11},{11,3},{4,12},{12,4},... | collective-permute-start | bytes 786440 | tf_op jit(solution)/shard_map/ppermute | solution.py:155
  17.1 0.0 collective-permute-done.1.refs_2_
  17.1 0.0 collective-permute-start.5
  17.2 2.4 %collective-permute-done.refs_1_ = bf16[2,64,1024]{2,1,0:T(8,128)(2,1)S(1)} collective-permute-done((bf16[2,64,1024]{2,1,0:T(8,128)(2,1)}, bf16[2,64,1024]{2,1,0:T(8,128)(2,1)S(1)}, u32[]{:S(2)}, u32[]{:S(2)}) %collective-permute-start) | collective-permute-done | bytes 262176 | tf_op jit(solution)/shard_map/ppermute | solution.py:152
  19.6 0.6 collective-permute-start.4
  20.2 1.3 %fusion.6 = s32[]{:T(128)} fusion(s32[8]{0:T(128)} %param.10, s32[]{:T(128)S(6)} %add.38), kind=kLoop, calls=%fused_computation.25 | loop fusion | flops 23 | bytes 40 | tf_op jit(solution)/shard_map/reduce_sum | solution.py:172
  21.5 0.7 pad_add_fusion.order_ref
  22.2 0.0 collective-permute-done.3.refs_4_
  22.2 1.4 %all-to-all-done.refs_8_ = bf16[8,2,64,256]{3,2,1,0:T(8,128)(2,1)S(1)} async-done(((bf16[8,2,64,256]{3,2,1,0:T(8,128)(2,1)}), bf16[8,2,64,256]{3,2,1,0:T(8,128)(2,1)S(1)}, u32[]{:S(2)}, u32[]{:S(2)}) %all-to-all-start) | async-done | bytes 524320 | tf_op jit(solution)/shard_map/all_to_all | solution.py:167
  23.6 0.0 collective-permute-done.6.refs_7_
  23.6 0.0 collective-permute-done.5.refs_6_
  23.6 0.0 collective-permute-done.4.refs_5_
  23.6 0.0 copy-start
  23.7 0.9 %copy-done = bf16[2,1024,64]{1,2,0:T(8,128)(2,1)S(1)} copy-done((bf16[2,1024,64]{1,2,0:T(8,128)(2,1)S(1)}, bf16[2,1024,64]{1,2,0:T(8,128)(2,1)}, u32[]{:S(2)}) %copy-start) | copy-done | bytes 262168
  24.6 3.4 %image.1 = bf16[2048,256]{1,0:T(8,128)(2,1)} custom-call(s32[9]{0:T(128)S(1)} %pad_add_fusion.order_ref, bf16[2,64,1024]{2,1,0:T(8,128)(2,1)S(1)} %bitcast.12, bf16[2,64,1024]{2,1,0:T(8,128)(2,1)S(1)} %collective-permute-done.refs_1_, bf16[2,64,1024]{2,1,0:T(8,128)(2,1)S(1)} %collective-permute-done.1.refs_2_, ...), custom_call_target="tpu_custom_call" | custom-call | tf_op jit(solution)/shard_map/image/pallas_call | solution.py:175
  28.0 13.3 %all-to-all-start.1 = ((bf16[256,8,256]{2,1,0:T(8,128)(2,1)}), bf16[256,8,256]{2,1,0:T(8,128)(2,1)S(1)}, u32[]{:S(2)}, u32[]{:S(2)}) async-start(bf16[256,8,256]{2,1,0:T(8,128)(2,1)} %bitcast.2), calls=%async_computation.1 | async-start | bytes 2097152 | tf_op jit(solution)/shard_map/all_to_all | solution.py:184
  41.4 0.1 reshape.25
  41.5 0.2 copy.12
  41.7 0.1 eq.27
  41.9 0.2 select_reduce_fusion
  42.0 1.0 %fusion.1 = (f32[64,512]{0,1:T(8,128)S(1)}, f32[64,512]{0,1:T(8,128)S(1)}, f32[64,512]{0,1:T(8,128)S(1)}) fusion(f32[512]{0:T(512)S(1)} %convert_add_fusion, f32[64]{0:T(128)S(1)} %broadcast_multiply_fusion), kind=kLoop, calls=%fused_computation.6 | loop fusion | flops 65536 | bytes 395520 | tf_op jit(solution)/shard_map/neg | solution.py:190
  43.0 0.2 fusion
  43.3 0.1 copy.13.g_ref
  43.4 30.2 %all-to-all-done.1 = bf16[256,8,256]{2,1,0:T(8,128)(2,1)S(1)} async-done(((bf16[256,8,256]{2,1,0:T(8,128)(2,1)}), bf16[256,8,256]{2,1,0:T(8,128)(2,1)S(1)}, u32[]{:S(2)}, u32[]{:S(2)}) %all-to-all-start.1) | async-done | bytes 1048608 | tf_op jit(solution)/shard_map/all_to_all | solution.py:184
  73.6 5.9 %recover.1 = f32[2,4,256,512]{3,2,1,0:T(8,128)} custom-call(bf16[32,4,2,8,256]{4,3,2,1,0:T(8,128)(2,1)S(1)} %bitcast.7, bf16[128,1024]{1,0:T(8,128)(2,1)S(1)} %copy.13.g_ref, bf16[1024,128]{1,0:T(8,128)(2,1)S(1)} %get-tuple-element.5.h_ref), custom_call_target="tpu_custom_call" | custom-call | tf_op jit(solution)/shard_map/recover/pallas_call | solution.py:196
  (7 shorter events, 0.0 us)
Async XLA Ops:
  0.0 41.4 %copy-start.1 = (s32[64]{0:T(128)S(1)}, s32[64]{0:T(128)}, u32[]{:S(2)}) copy-start(s32[64]{0:T(128)} %param.12) | copy-start | bytes 772
  0.0 41.8 %copy-start.2 = (f32[64]{0:T(128)S(1)}, f32[64]{0:T(128)}, u32[]{:S(2)}) copy-start(f32[64]{0:T(128)} %param.13) | copy-start | bytes 772
  0.0 13.7 %collective-permute-start.2 = (bf16[2,64,1024]{2,1,0:T(8,128)(2,1)}, bf16[2,64,1024]{2,1,0:T(8,128)(2,1)S(1)}, u32[]{:S(2)}, u32[]{:S(2)}) collective-permute-start(bf16[2,64,1024]{2,1,0:T(8,128)(2,1)} %bitcast.8), channel_id=1, source_target_pairs={{0,192},{64,0},{128,64},{192,128},{1,193},{65,1},{129,65},{193,129... | collective-permute-start | bytes 786440 | tf_op jit(solution)/shard_map/ppermute | solution.py:152
  3.3 13.8 %collective-permute-start.1 = (bf16[2,64,1024]{2,1,0:T(8,128)(2,1)}, bf16[2,64,1024]{2,1,0:T(8,128)(2,1)S(1)}, u32[]{:S(2)}, u32[]{:S(2)}) collective-permute-start(bf16[2,64,1024]{2,1,0:T(8,128)(2,1)} %bitcast.9), channel_id=1, source_target_pairs={{0,128},{64,192},{128,0},{192,64},{1,129},{65,193},{129,1},{193,65... | collective-permute-start | bytes 786440 | tf_op jit(solution)/shard_map/ppermute | solution.py:152
  3.8 15.7 %collective-permute-start = (bf16[2,64,1024]{2,1,0:T(8,128)(2,1)}, bf16[2,64,1024]{2,1,0:T(8,128)(2,1)S(1)}, u32[]{:S(2)}, u32[]{:S(2)}) collective-permute-start(bf16[2,64,1024]{2,1,0:T(8,128)(2,1)} %bitcast.10), channel_id=1, source_target_pairs={{0,64},{64,128},{128,192},{192,0},{1,65},{65,129},{129,193},{193,1... | collective-permute-start | bytes 786440 | tf_op jit(solution)/shard_map/ppermute | solution.py:152
  7.4 16.2 %all-to-all-start = ((bf16[8,2,64,256]{3,2,1,0:T(8,128)(2,1)}), bf16[8,2,64,256]{3,2,1,0:T(8,128)(2,1)S(1)}, u32[]{:S(2)}, u32[]{:S(2)}) async-start(bf16[8,2,64,256]{3,2,1,0:T(8,128)(2,1)} %focus.1), calls=%async_computation | async-start | bytes 1048576 | tf_op jit(solution)/shard_map/all_to_all | solution.py:167
  13.7 8.5 %collective-permute-start.3 = (bf16[2,64,1024]{2,1,0:T(8,128)(2,1)}, bf16[2,64,1024]{2,1,0:T(8,128)(2,1)S(1)}, u32[]{:S(2)}, u32[]{:S(2)}) collective-permute-start(bf16[2,64,1024]{2,1,0:T(8,128)(2,1)} %bitcast.11), channel_id=1, source_target_pairs={{0,8},{8,0},{1,9},{9,1},{2,10},{10,2},{3,11},{11,3},{4,12},{12,4},... | collective-permute-start | bytes 786440 | tf_op jit(solution)/shard_map/ppermute | solution.py:155
  13.7 10.0 %collective-permute-start.6 = (bf16[2,64,1024]{2,1,0:T(8,128)(2,1)S(1)}, bf16[2,64,1024]{2,1,0:T(8,128)(2,1)S(1)}, u32[]{:S(2)}, u32[]{:S(2)}) collective-permute-start(bf16[2,64,1024]{2,1,0:T(8,128)(2,1)S(1)} %collective-permute-done.2.refs_3_), channel_id=1, source_target_pairs={{0,8},{8,0},{1,9},{9,1},{2,10},{10,2},{3,11},{11,3},{4,12},{12,4},... | collective-permute-start | bytes 786440 | tf_op jit(solution)/shard_map/ppermute | solution.py:155
  17.1 6.5 %collective-permute-start.5 = (bf16[2,64,1024]{2,1,0:T(8,128)(2,1)S(1)}, bf16[2,64,1024]{2,1,0:T(8,128)(2,1)S(1)}, u32[]{:S(2)}, u32[]{:S(2)}) collective-permute-start(bf16[2,64,1024]{2,1,0:T(8,128)(2,1)S(1)} %collective-permute-done.1.refs_2_), channel_id=1, source_target_pairs={{0,8},{8,0},{1,9},{9,1},{2,10},{10,2},{3,11},{11,3},{4,12},{12,4},... | collective-permute-start | bytes 786440 | tf_op jit(solution)/shard_map/ppermute | solution.py:155
  19.6 4.1 %collective-permute-start.4 = (bf16[2,64,1024]{2,1,0:T(8,128)(2,1)S(1)}, bf16[2,64,1024]{2,1,0:T(8,128)(2,1)S(1)}, u32[]{:S(2)}, u32[]{:S(2)}) collective-permute-start(bf16[2,64,1024]{2,1,0:T(8,128)(2,1)S(1)} %collective-permute-done.refs_1_), channel_id=1, source_target_pairs={{0,8},{8,0},{1,9},{9,1},{2,10},{10,2},{3,11},{11,3},{4,12},{12,4},... | collective-permute-start | bytes 786440 | tf_op jit(solution)/shard_map/ppermute | solution.py:155
  23.6 1.0 %copy-start = (bf16[2,1024,64]{1,2,0:T(8,128)(2,1)S(1)}, bf16[2,1024,64]{1,2,0:T(8,128)(2,1)}, u32[]{:S(2)}) copy-start(bf16[2,1024,64]{1,2,0:T(8,128)(2,1)} %param.8) | copy-start | bytes 786436
  28.0 45.6 %all-to-all-start.1 = ((bf16[256,8,256]{2,1,0:T(8,128)(2,1)}), bf16[256,8,256]{2,1,0:T(8,128)(2,1)S(1)}, u32[]{:S(2)}, u32[]{:S(2)}) async-start(bf16[256,8,256]{2,1,0:T(8,128)(2,1)} %bitcast.2), calls=%async_computation.1 | async-start | bytes 2097152 | tf_op jit(solution)/shard_map/all_to_all | solution.py:184

commit v4 on v3

v4 whole, which is shorter than its diff:
```python
import functools

import jax
import jax.numpy as jnp
from jax import lax
from jax.experimental import pallas as pl
from jax.experimental.pallas import tpu as pltpu
from jax.sharding import Mesh, PartitionSpec as P

BINS = 512
ITERS = 4
ROW_MAX = 64
LEVEL = 0.1

VMEM = pl.BlockSpec(memory_space=pltpu.VMEM)
SMEM = pl.BlockSpec(memory_space=pltpu.SMEM)
HBM = pl.BlockSpec(memory_space=pltpu.HBM)


def dot(a, b, ca, cb):
    return lax.dot_general(a, b, (((ca,), (cb,)), ((), ())), preferred_element_type=jnp.float32)


def focus_kernel(lat_ref, echo_ref, kern_ref, *refs):
    outs = refs[:-4]
    echo, kern, echo_sem, kern_sem = refs[-4:]
    _, _, pulses, cols = outs[0].shape
    x = lax.axis_index("x")
    c = lax.axis_index("c")
    numbers = [[(x + s) % len(outs) * 2 + (c + k) % 2 for k in range(2)] for s in range(len(outs))]

    def kern_copy(part):
        return pltpu.make_async_copy(kern_ref.at[part], kern.at[part], kern_sem.at[part])

    def echo_copy(s, k, part):
        return pltpu.make_async_copy(
            echo_ref.at[part, numbers[s][k]], echo.at[part, s, k], echo_sem.at[part, s, k]
        )

    pieces = [(s, k, part) for s in range(len(outs)) for k in range(2) for part in range(2)]
    for part in range(2):
        kern_copy(part).start()
    for piece in pieces:
        echo_copy(*piece).start()
    for part in range(2):
        kern_copy(part).wait()
    kr = kern[0]
    ki = kern[1]
    col = lax.broadcasted_iota(jnp.int32, (pulses, cols), 1)
    for s, out in enumerate(outs):
        for k in range(2):
            for part in range(2):
                echo_copy(s, k, part).wait()
        er = echo[0, s].reshape(2 * pulses, -1)
        ei = echo[1, s].reshape(2 * pulses, -1)
        fr = dot(er, kr, 1, 0) - dot(ei, ki, 1, 0)
        fi = dot(er, ki, 1, 0) + dot(ei, kr, 1, 0)
        for k in range(2):
            lag = lat_ref[numbers[s][k]]
            keep = col >= lag
            for part, value in enumerate((fr, fi)):
                moved = pltpu.roll(value[k * pulses : (k + 1) * pulses], lag, 1)
                out[k, part] = jnp.where(keep, moved, 0.0).astype(out.dtype)


def image_kernel(far, lag_ref, at_ref, own_ref, *refs):
    out_ref, at_mem, own_mem, out_mem, re_ref, im_ref, at_sem, own_sem, out_sem = refs[-9:]
    tables = list(refs[:-9])
    focus_refs = [own_mem] + tables[-2 * far + 1 :]
    held = tables[: -2 * far + 1]
    rows = at_mem.shape[2]
    cols = out_ref.shape[1]
    load_own = pltpu.make_async_copy(own_ref.at[0], own_mem.at[0], own_sem)
    load = pltpu.make_async_copy(at_ref, at_mem, at_sem)
    load_own.start()
    load.start()
    load_own.wait()
    fr = jnp.concatenate([ref[i // far, 0] for i, ref in enumerate(focus_refs)], axis=0)
    fi = jnp.concatenate([ref[i // far, 1] for i, ref in enumerate(focus_refs)], axis=0)
    re_ref[0:ROW_MAX] = jnp.zeros((ROW_MAX, cols), jnp.float32)
    im_ref[0:ROW_MAX] = jnp.zeros((ROW_MAX, cols), jnp.float32)
    lag = lag_ref[0]
    start = ROW_MAX - lag
    base = pl.multiple_of(start // 8 * 8, 8)
    rest = start - base
    step = 128
    sub = lax.broadcasted_iota(jnp.int32, (step // 8, 8, cols), 1)
    load.wait()
    def planes(refs):
        mine, one, two_r, two_i, three = refs
        return (
            [mine.at[0], one.at[0], two_r, three.at[0]],
            [mine.at[1], one.at[1], two_i, three.at[1]],
        )

    own = planes([at_mem] + held[:4])
    sibling = planes(held[4:])
    real = own[0] + sibling[0]
    imag = own[1] + sibling[1]

    def product(r0):
        ar = jnp.concatenate([ref[:, r0 : r0 + step] for ref in real], axis=0)
        ai = jnp.concatenate([ref[:, r0 : r0 + step] for ref in imag], axis=0)
        return dot(ar, fr, 0, 0) - dot(ai, fi, 0, 0), dot(ar, fi, 0, 0) + dot(ai, fr, 0, 0)

    def keep(r0, value):
        re_ref[ROW_MAX + r0 : ROW_MAX + r0 + step] = value[0]
        im_ref[ROW_MAX + r0 : ROW_MAX + r0 + step] = value[1]

    def shifted(ref, r0):
        wide = ref[pl.ds(base + r0, step + 8)]
        return pltpu.roll(wide, step + 8 - rest, 0)[:step].reshape(step // 8, 8, cols)

    def copy(r0):
        piece = pl.ds(2 * r0, 2 * step)
        return pltpu.make_async_copy(out_mem.at[piece], out_ref.at[piece], out_sem.at[r0 // step])

    keep(0, product(0))
    for r0 in range(0, rows, step):
        last = r0 + step == rows
        value = None if last else product(r0 + step)
        re = shifted(re_ref, r0)
        im = shifted(im_ref, r0)
        first = jnp.where(sub < 4, re, pltpu.roll(im, 4, 1))
        second = jnp.where(sub < 4, pltpu.roll(re, 4, 1), im)
        both = jnp.stack([first, second], axis=1).reshape(2 * step, cols)
        out_mem[2 * r0 : 2 * r0 + 2 * step] = both.astype(out_mem.dtype)
        copy(r0).start()
        if not last:
            keep(r0 + step, value)
    for r0 in range(0, rows, step):
        copy(r0).wait()


def recover_kernel(img_ref, g_ref, h_ref, out_ref, y_ref):
    i = pl.program_id(0)
    outer, parts, inner, eight, cols = img_ref.shape
    passes = outer * inner

    @pl.when(i == 0)
    def _():
        some = 1
        for k in range(0, outer, some):
            acc = img_ref[k : k + some, 0].astype(jnp.float32)
            for z in range(1, parts):
                acc = acc + img_ref[k : k + some, z].astype(jnp.float32)
            acc = acc.reshape(some * inner * eight, cols)
            at = k * inner * eight
            for c in range(cols // 128):
                y_ref[c, at : at + some * inner * eight] = acc[:, c * 128 : c * 128 + 128]

    g = g_ref[...]
    h = h_ref[...]
    chains = []
    for c in range(cols // 128):
        re = y_ref.at[c][pl.ds(i, passes, stride=eight), :]
        im = y_ref.at[c][pl.ds(eight // 2 + i, passes, stride=eight), :]
        y = jnp.concatenate([re, im], axis=0).T.astype(jnp.bfloat16)
        chains += [y[:64], y[64:]]
    wide = [y.astype(jnp.float32) for y in chains]

    def shrink(v):
        return v - jnp.clip(v, -LEVEL, LEVEL)

    us = [shrink(dot(y, g, 1, 0)) for y in chains]
    for _ in range(ITERS - 1):
        resids = [
            (y - dot(u.astype(jnp.bfloat16), h, 1, 0)).astype(jnp.bfloat16) for y, u in zip(wide, us)
        ]
        us = [shrink(u + dot(r, g, 1, 0)) for u, r in zip(us, resids)]
    for k, u in enumerate(us):
        out_ref[0, 0, k * 64 : k * 64 + 64] = u[:, :BINS]
        out_ref[1, 0, k * 64 : k * 64 + 64] = u[:, BINS:]


def steering(normal_spacings, source):
    chosen = jnp.sum(
        jnp.where(
            source[:, None] == jnp.arange(normal_spacings.shape[0], dtype=jnp.int32)[None, :],
            normal_spacings[None, :],
            0.0,
        ),
        axis=1,
    )
    bins = jnp.arange(BINS).astype(normal_spacings.dtype) - BINS // 2
    phases = jnp.pi * chosen[:, None] * bins[None, :]
    return jnp.cos(phases), jnp.sin(phases)


def partial_image(echo, along, slant, vertical, lateral):
    passes = vertical.shape[0]
    pulses = along.shape[2]
    rows = along.shape[1]
    freqs, cols = slant.shape[1:]
    bf = jnp.bfloat16
    nx = lax.axis_size("x")

    def turn(value, step):
        return lax.ppermute(value, "x", [(i, (i + step) % nx) for i in range(nx)])

    def swap(value):
        return lax.ppermute(value, "c", [(0, 1), (1, 0)])

    at = jnp.transpose(along, (0, 2, 1))
    one = turn(at, 1)
    three = turn(at, 3)
    two_re = turn(one[0], 1)
    two_im = turn(three[1], 3)

    focus = pl.pallas_call(
        focus_kernel,
        out_shape=[jax.ShapeDtypeStruct((2, 2, pulses, cols), bf)] * nx,
        in_specs=[SMEM, HBM, HBM],
        out_specs=[VMEM] * nx,
        scratch_shapes=[
            pltpu.VMEM((2, nx, 2, pulses, freqs), bf),
            pltpu.VMEM((2, freqs, cols), bf),
            pltpu.SemaphoreType.DMA((2, nx, 2)),
            pltpu.SemaphoreType.DMA((2,)),
        ],
        name="focus",
    )(lateral, echo, slant)
    focus = [focus[0]] + [turn(focus[s], s) for s in range(1, nx)]
    at_late, one_late, three_late, *focus = lax.optimization_barrier((at, one, three, *focus))
    focus = focus + [swap(value) for value in focus]
    held = [one, two_re, two_im, three]
    held = held + [swap(value) for value in (at_late, one_late, two_re, two_im, three_late)]

    number = lax.axis_index("x") * 2 + lax.axis_index("c")
    lag = jnp.sum(jnp.where(jnp.arange(passes, dtype=jnp.int32) == number, vertical, 0))
    return pl.pallas_call(
        functools.partial(image_kernel, nx),
        out_shape=jax.ShapeDtypeStruct((2 * rows, cols), bf),
        in_specs=[SMEM, HBM, HBM] + [VMEM] * (len(held) + len(focus) - 1),
        out_specs=HBM,
        scratch_shapes=[
            pltpu.VMEM((2, pulses, rows), bf),
            pltpu.VMEM((1, 2, pulses, cols), bf),
            pltpu.VMEM((2 * rows, cols), bf),
            pltpu.VMEM((rows + ROW_MAX + 8, cols), jnp.float32),
            pltpu.VMEM((rows + ROW_MAX + 8, cols), jnp.float32),
            pltpu.SemaphoreType.DMA,
            pltpu.SemaphoreType.DMA,
            pltpu.SemaphoreType.DMA((rows // 128,)),
        ],
        compiler_params=pltpu.CompilerParams(vmem_limit_bytes=40 << 20),
        name="image",
    )(lag.reshape(1), at, focus[0], *held, *focus[1:])


def body(echo, along, slant, vertical, lateral, survey, spacings):
    total = survey.shape[0]
    cols = slant.shape[2]
    bf = jnp.bfloat16
    nx, nz, nc, ny, nl = (lax.axis_size(name) for name in ("x", "zh", "c", "y", "zl"))
    image = partial_image(echo, along, slant, vertical, lateral)
    image = lax.all_to_all(image, ("x", "zh", "c", "y", "zl"), 0, 0, tiled=True)

    source = survey.reshape(ny * nl, nx * nc).T.reshape(total)
    cos, sin = steering(spacings, source)
    g = jnp.concatenate(
        [jnp.concatenate([cos, -sin], axis=1), jnp.concatenate([sin, cos], axis=1)], axis=0
    )
    gb = (g / total).astype(bf)
    hb = (g.T / BINS).astype(bf)
    own = 4
    image = image.reshape(nx, nz, nc * ny * nl, 2 * own, cols)
    return pl.pallas_call(
        recover_kernel,
        grid=(own,),
        out_shape=jax.ShapeDtypeStruct((2, own, cols, BINS), jnp.float32),
        in_specs=[
            pl.BlockSpec(image.shape, lambda i: (0, 0, 0, 0, 0)),
            pl.BlockSpec(gb.shape, lambda i: (0, 0)),
            pl.BlockSpec(hb.shape, lambda i: (0, 0)),
        ],
        out_specs=pl.BlockSpec((2, 1, cols, BINS), lambda i: (0, i, 0, 0)),
        scratch_shapes=[pltpu.VMEM((cols // 128, total * 2 * own, 128), jnp.float32)],
        compiler_params=pltpu.CompilerParams(vmem_limit_bytes=40 << 20),
        name="recover",
    )(image, gb, hb)


def solution(mesh):
    fine = Mesh(mesh.devices.reshape(4, 4, 2, 4, 2), ("x", "zh", "c", "y", "zl"))
    ap = ("x", "zh", "c")
    group = ("y", "zl")
    return jax.shard_map(
        body,
        mesh=fine,
        in_specs=(
            P(None, group, ap, None),
            P(None, None, ap),
            P(),
            P(group),
            P(group),
            P(),
            P(),
        ),
        out_specs=P(None, ap + group, None, None),
        check_vma=False,
    )
```

time: 79.8 us -> 82 us (1.028)
  Pallas kernels: 12.4 us -> 13.8 us
    all_to_all x2 -> x1, starting transfers between devices: 19.6 us -> 13.4 us  [body(): image = lax.all_to_all(image, ('x', 'zh', 'c', 'y', 'zl'), 0, 0, tiled=True)]
    ppermute x3 -> x7, starting transfers between devices: 4.43 us -> 8.89 us  [turn(): return lax.ppermute(value, 'x', [(i, (i + step) % nx) for i in range(nx)])]
    ppermute x4 -> x9, starting transfers between devices: 4.07 us -> 6.57 us  [swap(): return lax.ppermute(value, 'c', [(0, 1), (1, 0)])]
    pallas_call x2, Pallas kernels: 6.42 us -> 7.89 us  [the longest x1 4.53 us: partial_image(): pl.pallas_call(focus_kernel, out_shape=[jax.ShapeDtypeStruct((2, 2, pulse...]
    all_to_all x2 -> x1, waiting for transfers between devices: 31.6 us -> 30.4 us  [body(): image = lax.all_to_all(image, ('x', 'zh', 'c', 'y', 'zl'), 0, 0, tiled=True)]
    ppermute x3 -> x7, waiting for transfers between devices: 2.43 us -> 3.48 us  [turn(): return lax.ppermute(value, 'x', [(i, (i + step) % nx) for i in range(nx)])]
    unnamed x6 -> x8, local copies, waits for them, and re-layouts: 0.95 us -> 1.86 us
  transfers between devices with their start and end apart: 9 -> 17, of which waited for: 3 -> 4; matrix products, arithmetic and copies ran while one was open for 5% -> 4% of each run, Pallas kernels for 4% -> 6%
where the time goes in v4:
time: 82 us; the launch traced here: 81.8 us
  waiting for transfers between devices  33.9 us (41%)
  starting transfers between devices  28.9 us (35%)
  Pallas kernels  13.8 us (17%)
  other arithmetic  2.75 us (3%)
  local copies, waits for them, and re-layouts  2.25 us (3%)
    all_to_all x1, waiting for transfers between devices, body(): image = lax.all_to_all(image, ('x', 'zh', 'c', 'y', 'zl'), 0, 0, tiled=True)  30.4 us
    all_to_all x1, starting transfers between devices, body(): image = lax.all_to_all(image, ('x', 'zh', 'c', 'y', 'zl'), 0, 0, tiled=True)  13.4 us
    ppermute x7, starting transfers between devices, turn(): return lax.ppermute(value, 'x', [(i, (i + step) % nx) for i in range(nx)])  8.89 us
    ppermute x9, starting transfers between devices, swap(): return lax.ppermute(value, 'c', [(0, 1), (1, 0)])  6.57 us
    pallas_call x1, Pallas kernels, body(): pl.pallas_call(recover_kernel, grid=(own,), out_shape=jax.ShapeDtypeStruc...  5.96 us
    pallas_call x1, Pallas kernels, partial_image(): pl.pallas_call(focus_kernel, out_shape=[jax.ShapeDtypeStruct((2, 2, pulse...  4.53 us
    ppermute x7, waiting for transfers between devices, turn(): return lax.ppermute(value, 'x', [(i, (i + step) % nx) for i in range(nx)])  3.48 us
    pallas_call x1, Pallas kernels, partial_image(): pl.pallas_call(functools.partial(image_kernel, nx), out_shape=jax.ShapeDt...  3.36 us
  transfers between devices with their start and end apart: 17, of which 4 were waited for; matrix products, arithmetic and copies ran while one was open for 4% of the time, Pallas kernels for 6%

profile of v4, /device:TPU:1, one launch (start us, length us, event | category | flops | bytes accessed | tf_op | source)
XLA Modules:
  0.0 81.8 jit_solution(15638789657105098299)
XLA Ops:
  0.0 3.3 %collective-permute-start.1 = (bf16[2,64,1024]{2,1,0:T(8,128)(2,1)}, bf16[2,64,1024]{2,1,0:T(8,128)(2,1)S(1)}, u32[]{:S(2)}, u32[]{:S(2)}) collective-permute-start(bf16[2,64,1024]{2,1,0:T(8,128)(2,1)} %bitcast.12), channel_id=1, source_target_pairs={{0,192},{64,0},{128,64},{192,128},{1,193},{65,1},{129,65},{193,129... | collective-permute-start | bytes 786440 | tf_op jit(solution)/shard_map/ppermute | solution.py:199
  3.3 4.5 %focus.1 = (bf16[2,2,64,256]{3,2,1,0:T(8,128)(2,1)}, bf16[2,2,64,256]{3,2,1,0:T(8,128)(2,1)}, bf16[2,2,64,256]{3,2,1,0:T(8,128)(2,1)}, bf16[2,2,64,256]{3,2,1,0:T(8,128)(2,1)}) custom-call(s32[8]{0:T(128)} %lat_ref.1, bf16[2,8,64,512]{3,2,1,0:T(8,128)(2,1)} %echo_ref.1, bf16[2,512,256]{2,1,0:T(8,128)(2,1)} %kern_ref.1), custom_call_target="tpu_custom_call" | custom-call | tf_op jit(solution)/shard_map/focus/pallas_call | solution.py:210
  7.9 0.3 collective-permute-start.2
  8.1 3.7 %collective-permute-start.3 = (bf16[2,2,64,256]{3,2,1,0:T(8,128)(2,1)}, bf16[2,2,64,256]{3,2,1,0:T(8,128)(2,1)S(1)}, u32[]{:S(2)}, u32[]{:S(2)}) collective-permute-start(bf16[2,2,64,256]{3,2,1,0:T(8,128)(2,1)} %get-tuple-element.18), channel_id=1, source_target_pairs={{0,128},{64,192},{128,0},{192,64},{1,129},{65,193},{129,1},{193,65... | collective-permute-start | bytes 393224 | tf_op jit(solution)/shard_map/ppermute | solution.py:199
  11.8 0.4 collective-permute-start.6
  12.2 1.3 %collective-permute-start.5 = (bf16[64,1024]{1,0:T(8,128)(2,1)S(1)}, bf16[64,1024]{1,0:T(8,128)(2,1)S(1)}, u32[]{:S(2)}, u32[]{:S(2)}) collective-permute-start(bf16[64,1024]{1,0:T(8,128)(2,1)S(1)} %slice_bitcast_fusion.1), channel_id=1, source_target_pairs={{0,64},{64,128},{128,192},{192,0},{1,65},{65,129},{129,193},{193,1... | collective-permute-start | bytes 393224 | tf_op jit(solution)/shard_map/ppermute | solution.py:199
  13.5 0.7 collective-permute-done.2.refs_9_
  14.2 2.6 %collective-permute-done.3.refs_10_ = bf16[2,2,64,256]{3,2,1,0:T(8,128)(2,1)S(1)} collective-permute-done((bf16[2,2,64,256]{3,2,1,0:T(8,128)(2,1)}, bf16[2,2,64,256]{3,2,1,0:T(8,128)(2,1)S(1)}, u32[]{:S(2)}, u32[]{:S(2)}) %collective-permute-start.3) | collective-permute-done | bytes 131104 | tf_op jit(solution)/shard_map/ppermute | solution.py:199
  16.8 0.1 collective-permute-done.4.refs_11_
  16.9 3.8 %collective-permute-start.12 = (bf16[2,2,64,256]{3,2,1,0:T(8,128)(2,1)}, bf16[2,2,64,256]{3,2,1,0:T(8,128)(2,1)S(1)}, u32[]{:S(2)}, u32[]{:S(2)}) collective-permute-start(bf16[2,2,64,256]{3,2,1,0:T(8,128)(2,1)} %get-tuple-element.20.own_ref), channel_id=1, source_target_pairs={{0,8},{8,0},{1,9},{9,1},{2,10},{10,2},{3,11},{11,3},{4,12},{12,4},... | collective-permute-start | bytes 393224 | tf_op jit(solution)/shard_map/ppermute | solution.py:202
  20.7 0.5 collective-permute-start.14
  21.2 0.9 %collective-permute-start.15 = (bf16[2,2,64,256]{3,2,1,0:T(8,128)(2,1)S(1)}, bf16[2,2,64,256]{3,2,1,0:T(8,128)(2,1)S(1)}, u32[]{:S(2)}, u32[]{:S(2)}) collective-permute-start(bf16[2,2,64,256]{3,2,1,0:T(8,128)(2,1)S(1)} %collective-permute-done.4.refs_11_), channel_id=1, source_target_pairs={{0,8},{8,0},{1,9},{9,1},{2,10},{10,2},{3,11},{11,3},{4,12},{12,4},... | collective-permute-start | bytes 393224 | tf_op jit(solution)/shard_map/ppermute | solution.py:202
  22.1 0.0 collective-permute-start.7
  22.1 0.5 collective-permute-start.8
  22.6 0.1 collective-permute-start.11
  22.7 0.4 collective-permute-start.10
  23.2 0.0 collective-permute-done.15.refs_15_
  23.2 0.4 collective-permute-start.9
  23.6 1.4 %fusion.2 = s32[]{:T(128)} fusion(s32[8]{0:T(128)} %param.10, s32[]{:T(128)S(6)} %add.8), kind=kLoop, calls=%fused_computation.13 | loop fusion | flops 23 | bytes 40 | tf_op jit(solution)/shard_map/reduce_sum | solution.py:230
  25.0 0.9 %copy-done = bf16[2,1024,64]{1,2,0:T(8,128)(2,1)S(1)} copy-done((bf16[2,1024,64]{1,2,0:T(8,128)(2,1)S(1)}, bf16[2,1024,64]{1,2,0:T(8,128)(2,1)}, u32[]{:S(2)}) %copy-start) | copy-done | bytes 262168
  25.9 0.9 %copy-done.1 = bf16[2,2,64,256]{3,2,1,0:T(8,128)(2,1)S(1)} copy-done((bf16[2,2,64,256]{3,2,1,0:T(8,128)(2,1)S(1)}, bf16[2,2,64,256]{3,2,1,0:T(8,128)(2,1)}, u32[]{:S(2)}) %copy-start.1) | copy-done | bytes 131096
  26.8 3.4 %image.1 = bf16[2048,256]{1,0:T(8,128)(2,1)} custom-call(s32[1]{0:T(128)} %bitcast.lag_ref, bf16[2,64,1024]{2,1,0:T(8,128)(2,1)S(1)} %bitcast.15, bf16[2,2,64,256]{3,2,1,0:T(8,128)(2,1)S(1)} %copy-done.1, bf16[2,64,1024]{2,1,0:T(8,128)(2,1)S(1)} %collective-permute-done.refs_0_, bf16[64,1024]{1,0:T(8,128)(2,1)S(1)} %collective-permute-done.5.refs_1_, ...), custom_call_target="tpu_custom_call" | custom-call | tf_op jit(solution)/shard_map/image/pallas_call | solution.py:231
  30.2 13.4 %all-to-all-start = ((bf16[256,8,256]{2,1,0:T(8,128)(2,1)}), bf16[256,8,256]{2,1,0:T(8,128)(2,1)S(1)}, u32[]{:S(2)}, u32[]{:S(2)}) async-start(bf16[256,8,256]{2,1,0:T(8,128)(2,1)} %bitcast.4), calls=%async_computation | async-start | bytes 2097152 | tf_op jit(solution)/shard_map/all_to_all | solution.py:257
  43.6 0.1 reshape.25
  43.7 0.1 copy.10
  43.8 0.1 eq.23
  43.9 0.2 select_reduce_fusion
  44.1 1.0 %fusion.1 = (f32[64,512]{0,1:T(8,128)S(1)}, f32[64,512]{0,1:T(8,128)S(1)}, f32[64,512]{0,1:T(8,128)S(1)}) fusion(f32[512]{0:T(512)S(1)} %convert_add_fusion, f32[64]{0:T(128)S(1)} %broadcast_multiply_fusion), kind=kLoop, calls=%fused_computation.8 | loop fusion | flops 65536 | bytes 395520 | tf_op jit(solution)/shard_map/neg | solution.py:262
  45.1 0.2 fusion
  45.3 0.1 copy.11.g_ref
  45.4 30.4 %all-to-all-done = bf16[256,8,256]{2,1,0:T(8,128)(2,1)S(1)} async-done(((bf16[256,8,256]{2,1,0:T(8,128)(2,1)}), bf16[256,8,256]{2,1,0:T(8,128)(2,1)S(1)}, u32[]{:S(2)}, u32[]{:S(2)}) %all-to-all-start) | async-done | bytes 1048608 | tf_op jit(solution)/shard_map/all_to_all | solution.py:257
  75.8 6.0 %recover.1 = f32[2,4,256,512]{3,2,1,0:T(8,128)} custom-call(bf16[4,4,16,8,256]{4,3,2,1,0:T(8,128)(2,1)S(1)} %bitcast.11, bf16[128,1024]{1,0:T(8,128)(2,1)S(1)} %copy.11.g_ref, bf16[1024,128]{1,0:T(8,128)(2,1)S(1)} %get-tuple-element.27.h_ref), custom_call_target="tpu_custom_call" | custom-call | tf_op jit(solution)/shard_map/recover/pallas_call | solution.py:268
  (25 shorter events, 0.1 us)
Async XLA Ops:
  0.0 43.6 %copy-start.2 = (s32[64]{0:T(128)S(1)}, s32[64]{0:T(128)}, u32[]{:S(2)}) copy-start(s32[64]{0:T(128)} %param.12) | copy-start | bytes 772
  0.0 43.9 %copy-start.3 = (f32[64]{0:T(128)S(1)}, f32[64]{0:T(128)}, u32[]{:S(2)}) copy-start(f32[64]{0:T(128)} %param.13) | copy-start | bytes 772
  0.0 11.8 %collective-permute-start.1 = (bf16[2,64,1024]{2,1,0:T(8,128)(2,1)}, bf16[2,64,1024]{2,1,0:T(8,128)(2,1)S(1)}, u32[]{:S(2)}, u32[]{:S(2)}) collective-permute-start(bf16[2,64,1024]{2,1,0:T(8,128)(2,1)} %bitcast.12), channel_id=1, source_target_pairs={{0,192},{64,0},{128,64},{192,128},{1,193},{65,1},{129,65},{193,129... | collective-permute-start | bytes 786440 | tf_op jit(solution)/shard_map/ppermute | solution.py:199
  3.3 8.9 %collective-permute-start = (bf16[2,64,1024]{2,1,0:T(8,128)(2,1)}, bf16[2,64,1024]{2,1,0:T(8,128)(2,1)S(1)}, u32[]{:S(2)}, u32[]{:S(2)}) collective-permute-start(bf16[2,64,1024]{2,1,0:T(8,128)(2,1)} %bitcast.13), channel_id=1, source_target_pairs={{0,64},{64,128},{128,192},{192,0},{1,65},{65,129},{129,193},{193,1... | collective-permute-start | bytes 786440 | tf_op jit(solution)/shard_map/ppermute | solution.py:199
  7.9 6.3 %collective-permute-start.2 = (bf16[2,2,64,256]{3,2,1,0:T(8,128)(2,1)}, bf16[2,2,64,256]{3,2,1,0:T(8,128)(2,1)S(1)}, u32[]{:S(2)}, u32[]{:S(2)}) collective-permute-start(bf16[2,2,64,256]{3,2,1,0:T(8,128)(2,1)} %get-tuple-element.17), channel_id=1, source_target_pairs={{0,64},{64,128},{128,192},{192,0},{1,65},{65,129},{129,193},{193,1... | collective-permute-start | bytes 393224 | tf_op jit(solution)/shard_map/ppermute | solution.py:199
  8.1 8.7 %collective-permute-start.3 = (bf16[2,2,64,256]{3,2,1,0:T(8,128)(2,1)}, bf16[2,2,64,256]{3,2,1,0:T(8,128)(2,1)S(1)}, u32[]{:S(2)}, u32[]{:S(2)}) collective-permute-start(bf16[2,2,64,256]{3,2,1,0:T(8,128)(2,1)} %get-tuple-element.18), channel_id=1, source_target_pairs={{0,128},{64,192},{128,0},{192,64},{1,129},{65,193},{129,1},{193,65... | collective-permute-start | bytes 393224 | tf_op jit(solution)/shard_map/ppermute | solution.py:199
  11.8 5.2 %collective-permute-start.4 = (bf16[2,2,64,256]{3,2,1,0:T(8,128)(2,1)}, bf16[2,2,64,256]{3,2,1,0:T(8,128)(2,1)S(1)}, u32[]{:S(2)}, u32[]{:S(2)}) collective-permute-start(bf16[2,2,64,256]{3,2,1,0:T(8,128)(2,1)} %get-tuple-element.19), channel_id=1, source_target_pairs={{0,192},{64,0},{128,64},{192,128},{1,193},{65,1},{129,65},{193,129... | collective-permute-start | bytes 393224 | tf_op jit(solution)/shard_map/ppermute | solution.py:199
  11.8 9.4 %collective-permute-start.6 = (bf16[64,1024]{1,0:T(8,128)(2,1)S(1)}, bf16[64,1024]{1,0:T(8,128)(2,1)S(1)}, u32[]{:S(2)}, u32[]{:S(2)}) collective-permute-start(bf16[64,1024]{1,0:T(8,128)(2,1)S(1)} %slice_bitcast_fusion), channel_id=1, source_target_pairs={{0,192},{64,0},{128,64},{192,128},{1,193},{65,1},{129,65},{193,129... | collective-permute-start | bytes 393224 | tf_op jit(solution)/shard_map/ppermute | solution.py:199
  12.2 9.9 %collective-permute-start.5 = (bf16[64,1024]{1,0:T(8,128)(2,1)S(1)}, bf16[64,1024]{1,0:T(8,128)(2,1)S(1)}, u32[]{:S(2)}, u32[]{:S(2)}) collective-permute-start(bf16[64,1024]{1,0:T(8,128)(2,1)S(1)} %slice_bitcast_fusion.1), channel_id=1, source_target_pairs={{0,64},{64,128},{128,192},{192,0},{1,65},{65,129},{129,193},{193,1... | collective-permute-start | bytes 393224 | tf_op jit(solution)/shard_map/ppermute | solution.py:199
  16.9 5.2 %collective-permute-start.12 = (bf16[2,2,64,256]{3,2,1,0:T(8,128)(2,1)}, bf16[2,2,64,256]{3,2,1,0:T(8,128)(2,1)S(1)}, u32[]{:S(2)}, u32[]{:S(2)}) collective-permute-start(bf16[2,2,64,256]{3,2,1,0:T(8,128)(2,1)} %get-tuple-element.20.own_ref), channel_id=1, source_target_pairs={{0,8},{8,0},{1,9},{9,1},{2,10},{10,2},{3,11},{11,3},{4,12},{12,4},... | collective-permute-start | bytes 393224 | tf_op jit(solution)/shard_map/ppermute | solution.py:202
  20.7 1.9 %collective-permute-start.13 = (bf16[2,2,64,256]{3,2,1,0:T(8,128)(2,1)S(1)}, bf16[2,2,64,256]{3,2,1,0:T(8,128)(2,1)S(1)}, u32[]{:S(2)}, u32[]{:S(2)}) collective-permute-start(bf16[2,2,64,256]{3,2,1,0:T(8,128)(2,1)S(1)} %collective-permute-done.2.refs_9_), channel_id=1, source_target_pairs={{0,8},{8,0},{1,9},{9,1},{2,10},{10,2},{3,11},{11,3},{4,12},{12,4},... | collective-permute-start | bytes 393224 | tf_op jit(solution)/shard_map/ppermute | solution.py:202
  20.7 2.0 %collective-permute-start.14 = (bf16[2,2,64,256]{3,2,1,0:T(8,128)(2,1)S(1)}, bf16[2,2,64,256]{3,2,1,0:T(8,128)(2,1)S(1)}, u32[]{:S(2)}, u32[]{:S(2)}) collective-permute-start(bf16[2,2,64,256]{3,2,1,0:T(8,128)(2,1)S(1)} %collective-permute-done.3.refs_10_), channel_id=1, source_target_pairs={{0,8},{8,0},{1,9},{9,1},{2,10},{10,2},{3,11},{11,3},{4,12},{12,4},... | collective-permute-start | bytes 393224 | tf_op jit(solution)/shard_map/ppermute | solution.py:202
  21.2 2.0 %collective-permute-start.15 = (bf16[2,2,64,256]{3,2,1,0:T(8,128)(2,1)S(1)}, bf16[2,2,64,256]{3,2,1,0:T(8,128)(2,1)S(1)}, u32[]{:S(2)}, u32[]{:S(2)}) collective-permute-start(bf16[2,2,64,256]{3,2,1,0:T(8,128)(2,1)S(1)} %collective-permute-done.4.refs_11_), channel_id=1, source_target_pairs={{0,8},{8,0},{1,9},{9,1},{2,10},{10,2},{3,11},{11,3},{4,12},{12,4},... | collective-permute-start | bytes 393224 | tf_op jit(solution)/shard_map/ppermute | solution.py:202
  22.1 2.8 %collective-permute-start.7 = (bf16[2,64,1024]{2,1,0:T(8,128)(2,1)}, bf16[2,64,1024]{2,1,0:T(8,128)(2,1)S(1)}, u32[]{:S(2)}, u32[]{:S(2)}) collective-permute-start(bf16[2,64,1024]{2,1,0:T(8,128)(2,1)} %bitcast.14), channel_id=1, source_target_pairs={{0,8},{8,0},{1,9},{9,1},{2,10},{10,2},{3,11},{11,3},{4,12},{12,4},... | collective-permute-start | bytes 786440 | tf_op jit(solution)/shard_map/ppermute | solution.py:202
  22.1 2.8 %collective-permute-start.8 = (bf16[2,64,1024]{2,1,0:T(8,128)(2,1)S(1)}, bf16[2,64,1024]{2,1,0:T(8,128)(2,1)S(1)}, u32[]{:S(2)}, u32[]{:S(2)}) collective-permute-start(bf16[2,64,1024]{2,1,0:T(8,128)(2,1)S(1)} %collective-permute-done.refs_0_), channel_id=1, source_target_pairs={{0,8},{8,0},{1,9},{9,1},{2,10},{10,2},{3,11},{11,3},{4,12},{12,4},... | collective-permute-start | bytes 786440 | tf_op jit(solution)/shard_map/ppermute | solution.py:202
  22.6 2.3 %collective-permute-start.11 = (bf16[2,64,1024]{2,1,0:T(8,128)(2,1)S(1)}, bf16[2,64,1024]{2,1,0:T(8,128)(2,1)S(1)}, u32[]{:S(2)}, u32[]{:S(2)}) collective-permute-start(bf16[2,64,1024]{2,1,0:T(8,128)(2,1)S(1)} %collective-permute-done.1.refs_3_), channel_id=1, source_target_pairs={{0,8},{8,0},{1,9},{9,1},{2,10},{10,2},{3,11},{11,3},{4,12},{12,4},... | collective-permute-start | bytes 786440 | tf_op jit(solution)/shard_map/ppermute | solution.py:202
  22.7 2.2 %collective-permute-start.10 = (bf16[64,1024]{1,0:T(8,128)(2,1)S(1)}, bf16[64,1024]{1,0:T(8,128)(2,1)S(1)}, u32[]{:S(2)}, u32[]{:S(2)}) collective-permute-start(bf16[64,1024]{1,0:T(8,128)(2,1)S(1)} %collective-permute-done.6.refs_2_), channel_id=1, source_target_pairs={{0,8},{8,0},{1,9},{9,1},{2,10},{10,2},{3,11},{11,3},{4,12},{12,4},... | collective-permute-start | bytes 393224 | tf_op jit(solution)/shard_map/ppermute | solution.py:202
  23.2 1.8 %collective-permute-start.9 = (bf16[64,1024]{1,0:T(8,128)(2,1)S(1)}, bf16[64,1024]{1,0:T(8,128)(2,1)S(1)}, u32[]{:S(2)}, u32[]{:S(2)}) collective-permute-start(bf16[64,1024]{1,0:T(8,128)(2,1)S(1)} %collective-permute-done.5.refs_1_), channel_id=1, source_target_pairs={{0,8},{8,0},{1,9},{9,1},{2,10},{10,2},{3,11},{11,3},{4,12},{12,4},... | collective-permute-start | bytes 393224 | tf_op jit(solution)/shard_map/ppermute | solution.py:202
  25.0 1.0 %copy-start = (bf16[2,1024,64]{1,2,0:T(8,128)(2,1)S(1)}, bf16[2,1024,64]{1,2,0:T(8,128)(2,1)}, u32[]{:S(2)}) copy-start(bf16[2,1024,64]{1,2,0:T(8,128)(2,1)} %param.8) | copy-start | bytes 786436
  25.9 0.9 %copy-start.1 = (bf16[2,2,64,256]{3,2,1,0:T(8,128)(2,1)S(1)}, bf16[2,2,64,256]{3,2,1,0:T(8,128)(2,1)}, u32[]{:S(2)}) copy-start(bf16[2,2,64,256]{3,2,1,0:T(8,128)(2,1)} %get-tuple-element.20.own_ref) | copy-start | bytes 393220
  30.2 45.6 %all-to-all-start = ((bf16[256,8,256]{2,1,0:T(8,128)(2,1)}), bf16[256,8,256]{2,1,0:T(8,128)(2,1)S(1)}, u32[]{:S(2)}, u32[]{:S(2)}) async-start(bf16[256,8,256]{2,1,0:T(8,128)(2,1)} %bitcast.4), calls=%async_computation | async-start | bytes 2097152 | tf_op jit(solution)/shard_map/all_to_all | solution.py:257

commit v5 on v4

--- a/solution.py
+++ b/solution.py
@@ -21,71 +21,56 @@
     return lax.dot_general(a, b, (((ca,), (cb,)), ((), ())), preferred_element_type=jnp.float32)
 
 
-def focus_kernel(lat_ref, echo_ref, kern_ref, *refs):
-    outs = refs[:-4]
-    echo, kern, echo_sem, kern_sem = refs[-4:]
-    _, _, pulses, cols = outs[0].shape
+def focus_kernel(lat_ref, ver_ref, echo_ref, kern_ref, *outs):
+    _, passes, pulses, _ = echo_ref.shape
+    cols = kern_ref.shape[2]
+    far = len(outs)
     x = lax.axis_index("x")
     c = lax.axis_index("c")
-    numbers = [[(x + s) % len(outs) * 2 + (c + k) % 2 for k in range(2)] for s in range(len(outs))]
-
-    def kern_copy(part):
-        return pltpu.make_async_copy(kern_ref.at[part], kern.at[part], kern_sem.at[part])
-
-    def echo_copy(s, k, part):
-        return pltpu.make_async_copy(
-            echo_ref.at[part, numbers[s][k]], echo.at[part, s, k], echo_sem.at[part, s, k]
+    pairs = [(x + s) % far * 2 for s in range(far)]
+    kr = kern_ref[0]
+    ki = kern_ref[1]
+    er, ei = (
+        jnp.concatenate(
+            [echo_ref[part, pl.ds(pair, 2)].reshape(2 * pulses, -1) for pair in pairs], axis=0
         )
-
-    pieces = [(s, k, part) for s in range(len(outs)) for k in range(2) for part in range(2)]
-    for part in range(2):
-        kern_copy(part).start()
-    for piece in pieces:
-        echo_copy(*piece).start()
-    for part in range(2):
-        kern_copy(part).wait()
-    kr = kern[0]
-    ki = kern[1]
+        for part in range(2)
+    )
+    fr = dot(er, kr, 1, 0) - dot(ei, ki, 1, 0)
+    fi = dot(er, ki, 1, 0) + dot(ei, kr, 1, 0)
     col = lax.broadcasted_iota(jnp.int32, (pulses, cols), 1)
     for s, out in enumerate(outs):
-        for k in range(2):
-            for part in range(2):
-                echo_copy(s, k, part).wait()
-        er = echo[0, s].reshape(2 * pulses, -1)
-        ei = echo[1, s].reshape(2 * pulses, -1)
-        fr = dot(er, kr, 1, 0) - dot(ei, ki, 1, 0)
-        fi = dot(er, ki, 1, 0) + dot(ei, kr, 1, 0)
-        for k in range(2):
-            lag = lat_ref[numbers[s][k]]
+        for p in range(2):
+            lag = lat_ref[pairs[s] + p]
             keep = col >= lag
+            at = (2 * s + p) * pulses
             for part, value in enumerate((fr, fi)):
-                moved = pltpu.roll(value[k * pulses : (k + 1) * pulses], lag, 1)
-                out[k, part] = jnp.where(keep, moved, 0.0).astype(out.dtype)
-
-
-def image_kernel(far, lag_ref, at_ref, own_ref, *refs):
-    out_ref, at_mem, own_mem, out_mem, re_ref, im_ref, at_sem, own_sem, out_sem = refs[-9:]
-    tables = list(refs[:-9])
-    focus_refs = [own_mem] + tables[-2 * far + 1 :]
-    held = tables[: -2 * far + 1]
-    rows = at_mem.shape[2]
+                moved = pltpu.roll(value[at : at + pulses], lag, 1)
+                out[(c + p) % 2, part, 0:pulses] = jnp.where(keep, moved, 0.0).astype(out.dtype)
+    extra = outs[0].shape[2] - pulses
+    row_lag = jnp.full((extra, cols), ver_ref[pairs[0] + c].astype(jnp.float32))
+    for k in range(2):
+        for part in range(2):
+            outs[0][k, part, pulses : pulses + extra] = row_lag.astype(outs[0].dtype)
+
+
+def image_kernel(far, *refs):
+    out_ref, out_mem, re_ref, im_ref, out_sem = refs[-5:]
+    tables = list(refs[:-5])
+    focus_refs = tables[-2 * far :]
+    held = tables[: -2 * far]
+    _, pulses, rows = held[0].shape
     cols = out_ref.shape[1]
-    load_own = pltpu.make_async_copy(own_ref.at[0], own_mem.at[0], own_sem)
-    load = pltpu.make_async_copy(at_ref, at_mem, at_sem)
-    load_own.start()
-    load.start()
-    load_own.wait()
-    fr = jnp.concatenate([ref[i // far, 0] for i, ref in enumerate(focus_refs)], axis=0)
-    fi = jnp.concatenate([ref[i // far, 1] for i, ref in enumerate(focus_refs)], axis=0)
+    fr = jnp.concatenate([ref[i // far, 0, 0:pulses] for i, ref in enumerate(focus_refs)], axis=0)
+    fi = jnp.concatenate([ref[i // far, 1, 0:pulses] for i, ref in enumerate(focus_refs)], axis=0)
+    lag = jnp.max(focus_refs[0][0, 0, pulses:].astype(jnp.float32)).astype(jnp.int32)
     re_ref[0:ROW_MAX] = jnp.zeros((ROW_MAX, cols), jnp.float32)
     im_ref[0:ROW_MAX] = jnp.zeros((ROW_MAX, cols), jnp.float32)
-    lag = lag_ref[0]
     start = ROW_MAX - lag
     base = pl.multiple_of(start // 8 * 8, 8)
     rest = start - base
     step = 128
     sub = lax.broadcasted_iota(jnp.int32, (step // 8, 8, cols), 1)
-    load.wait()
     def planes(refs):
         mine, one, two_r, two_i, three = refs
         return (
@@ -93,8 +78,8 @@
             [mine.at[1], one.at[1], two_i, three.at[1]],
         )
 
-    own = planes([at_mem] + held[:4])
-    sibling = planes(held[4:])
+    own = planes(held[:5])
+    sibling = planes(held[5:])
     real = own[0] + sibling[0]
     imag = own[1] + sibling[1]
 
@@ -207,45 +192,37 @@
     two_re = turn(one[0], 1)
     two_im = turn(three[1], 3)
 
+    spare = 16
+    shapes = [(2, 2, pulses + spare, cols)] + [(2, 2, pulses, cols)] * (nx - 1)
     focus = pl.pallas_call(
         focus_kernel,
-        out_shape=[jax.ShapeDtypeStruct((2, 2, pulses, cols), bf)] * nx,
-        in_specs=[SMEM, HBM, HBM],
+        out_shape=[jax.ShapeDtypeStruct(shape, bf) for shape in shapes],
+        in_specs=[SMEM, SMEM, VMEM, VMEM],
         out_specs=[VMEM] * nx,
-        scratch_shapes=[
-            pltpu.VMEM((2, nx, 2, pulses, freqs), bf),
-            pltpu.VMEM((2, freqs, cols), bf),
-            pltpu.SemaphoreType.DMA((2, nx, 2)),
-            pltpu.SemaphoreType.DMA((2,)),
-        ],
         name="focus",
-    )(lateral, echo, slant)
+    )(lateral, vertical, echo, slant)
     focus = [focus[0]] + [turn(focus[s], s) for s in range(1, nx)]
     at_late, one_late, three_late, *focus = lax.optimization_barrier((at, one, three, *focus))
     focus = focus + [swap(value) for value in focus]
     held = [one, two_re, two_im, three]
-    held = held + [swap(value) for value in (at_late, one_late, two_re, two_im, three_late)]
-
-    number = lax.axis_index("x") * 2 + lax.axis_index("c")
-    lag = jnp.sum(jnp.where(jnp.arange(passes, dtype=jnp.int32) == number, vertical, 0))
+    swapped = [swap(value) for value in (at_late, one_late, two_re, two_im, three_late)]
+    inside = lax.axis_index("x") < nx
+    focus[0] = jnp.where(inside, focus[0], jnp.zeros_like(focus[0]))
+    held = [jnp.where(inside, at_late, jnp.zeros_like(at))] + held + swapped
     return pl.pallas_call(
         functools.partial(image_kernel, nx),
         out_shape=jax.ShapeDtypeStruct((2 * rows, cols), bf),
-        in_specs=[SMEM, HBM, HBM] + [VMEM] * (len(held) + len(focus) - 1),
+        in_specs=[VMEM] * (len(held) + len(focus)),
         out_specs=HBM,
         scratch_shapes=[
-            pltpu.VMEM((2, pulses, rows), bf),
-            pltpu.VMEM((1, 2, pulses, cols), bf),
             pltpu.VMEM((2 * rows, cols), bf),
             pltpu.VMEM((rows + ROW_MAX + 8, cols), jnp.float32),
             pltpu.VMEM((rows + ROW_MAX + 8, cols), jnp.float32),
-            pltpu.SemaphoreType.DMA,
-            pltpu.SemaphoreType.DMA,
             pltpu.SemaphoreType.DMA((rows // 128,)),
         ],
         compiler_params=pltpu.CompilerParams(vmem_limit_bytes=40 << 20),
         name="image",
-    )(lag.reshape(1), at, focus[0], *held, *focus[1:])
+    )(*held, *focus)
 
 
 def body(echo, along, slant, vertical, lateral, survey, spacings):

time: 82 us -> 78.4 us (0.956)
  Pallas kernels: 13.8 us -> 11.4 us
  local copies, waits for them, and re-layouts: 2.25 us -> 0.4 us
  waiting for transfers between devices: 33.9 us -> 35 us
  starting transfers between devices: 28.9 us -> 28 us
    select_n x0 -> x2, other arithmetic: none -> 1.9 us  [the longest x1 0.97 us: partial_image(): held = [jnp.where(inside, at_late, jnp.zeros_like(at))] + held + swapped]
    unnamed x8 -> x4, local copies, waits for them, and re-layouts: 1.86 us -> 0.01 us
    pallas_call x1, Pallas kernels: 4.53 us -> 2.86 us  [partial_image(): pl.pallas_call(focus_kernel, out_shape=[jax.ShapeDtypeStruct(shape, bf) f...]
    reduce_sum x1 -> x0, other arithmetic: 1.37 us -> none  [partial_image(): jnp.sum(jnp.where(jnp.arange(passes, dtype=jnp.int32) == number, vertical...]
    all_to_all x1, starting transfers between devices: 13.4 us -> 12.3 us  [body(): image = lax.all_to_all(image, ('x', 'zh', 'c', 'y', 'zl'), 0, 0, tiled=True)]
    ppermute x7, waiting for transfers between devices: 3.48 us -> 4.44 us  [turn(): return lax.ppermute(value, 'x', [(i, (i + step) % nx) for i in range(nx)])]
  transfers between devices with their start and end apart: 17 -> 17, of which waited for: 4 -> 4; matrix products, arithmetic and copies ran while one was open for 4% -> 5% of each run, Pallas kernels for 6% -> 4%
where the time goes in v5:
time: 78.4 us; the launch traced here: 78.2 us
  waiting for transfers between devices  35 us (45%)
  starting transfers between devices  28 us (36%)
  Pallas kernels  11.4 us (15%)
  other arithmetic  3.29 us (4%)
    all_to_all x1, waiting for transfers between devices, body(): image = lax.all_to_all(image, ('x', 'zh', 'c', 'y', 'zl'), 0, 0, tiled=True)  30.4 us
    all_to_all x1, starting transfers between devices, body(): image = lax.all_to_all(image, ('x', 'zh', 'c', 'y', 'zl'), 0, 0, tiled=True)  12.3 us
    ppermute x7, starting transfers between devices, turn(): return lax.ppermute(value, 'x', [(i, (i + step) % nx) for i in range(nx)])  9.2 us
    ppermute x9, starting transfers between devices, swap(): return lax.ppermute(value, 'c', [(0, 1), (1, 0)])  6.45 us
    pallas_call x1, Pallas kernels, body(): pl.pallas_call(recover_kernel, grid=(own,), out_shape=jax.ShapeDtypeStruc...  5.93 us
    ppermute x7, waiting for transfers between devices, turn(): return lax.ppermute(value, 'x', [(i, (i + step) % nx) for i in range(nx)])  4.44 us
    pallas_call x1, Pallas kernels, partial_image(): pl.pallas_call(focus_kernel, out_shape=[jax.ShapeDtypeStruct(shape, bf) f...  2.86 us
    pallas_call x1, Pallas kernels, partial_image(): pl.pallas_call(functools.partial(image_kernel, nx), out_shape=jax.ShapeDt...  2.65 us
  transfers between devices with their start and end apart: 17, of which 4 were waited for; matrix products, arithmetic and copies ran while one was open for 5% of the time, Pallas kernels for 4%

profile of v5, /device:TPU:1, one launch (start us, length us, event | category | flops | bytes accessed | tf_op | source)
XLA Modules:
  0.0 78.2 jit_solution(323348597073562429)
XLA Ops:
  0.0 3.3 %collective-permute-start.1 = (bf16[2,64,1024]{2,1,0:T(8,128)(2,1)}, bf16[2,64,1024]{2,1,0:T(8,128)(2,1)S(1)}, u32[]{:S(2)}, u32[]{:S(2)}) collective-permute-start(bf16[2,64,1024]{2,1,0:T(8,128)(2,1)} %bitcast.11), channel_id=1, source_target_pairs={{0,192},{64,0},{128,64},{192,128},{1,193},{65,1},{129,65},{193,129... | collective-permute-start | bytes 786440 | tf_op jit(solution)/shard_map/ppermute | solution.py:184
  3.3 2.9 %focus.1 = (bf16[2,2,80,256]{3,2,1,0:T(8,128)(2,1)}, bf16[2,2,64,256]{3,2,1,0:T(8,128)(2,1)}, bf16[2,2,64,256]{3,2,1,0:T(8,128)(2,1)}, bf16[2,2,64,256]{3,2,1,0:T(8,128)(2,1)}) custom-call(s32[8]{0:T(128)} %lat_ref.1, s32[8]{0:T(128)} %ver_ref.1, bf16[2,8,64,512]{3,2,1,0:T(8,128)(2,1)} %echo_ref.1, bf16[2,512,256]{2,1,0:T(8,128)(2,1)} %kern_ref.1), custom_call_target="tpu_custom_call" | custom-call | tf_op jit(solution)/shard_map/focus/pallas_call | solution.py:197
  6.2 0.3 collective-permute-start.2
  6.4 3.7 %collective-permute-start.3 = (bf16[2,2,64,256]{3,2,1,0:T(8,128)(2,1)}, bf16[2,2,64,256]{3,2,1,0:T(8,128)(2,1)S(1)}, u32[]{:S(2)}, u32[]{:S(2)}) collective-permute-start(bf16[2,2,64,256]{3,2,1,0:T(8,128)(2,1)} %get-tuple-element.18), channel_id=1, source_target_pairs={{0,128},{64,192},{128,0},{192,64},{1,129},{65,193},{129,1},{193,65... | collective-permute-start | bytes 393224 | tf_op jit(solution)/shard_map/ppermute | solution.py:184
  10.1 1.9 %collective-permute-start.6 = (bf16[64,1024]{1,0:T(8,128)(2,1)S(1)}, bf16[64,1024]{1,0:T(8,128)(2,1)S(1)}, u32[]{:S(2)}, u32[]{:S(2)}) collective-permute-start(bf16[64,1024]{1,0:T(8,128)(2,1)S(1)} %slice_bitcast_fusion), channel_id=1, source_target_pairs={{0,192},{64,0},{128,64},{192,128},{1,193},{65,1},{129,65},{193,129... | collective-permute-start | bytes 393224 | tf_op jit(solution)/shard_map/ppermute | solution.py:184
  12.0 0.1 collective-permute-start.5
  12.1 3.0 %collective-permute-done.2.refs_11_ = bf16[2,2,64,256]{3,2,1,0:T(8,128)(2,1)S(1)} collective-permute-done((bf16[2,2,64,256]{3,2,1,0:T(8,128)(2,1)}, bf16[2,2,64,256]{3,2,1,0:T(8,128)(2,1)S(1)}, u32[]{:S(2)}, u32[]{:S(2)}) %collective-permute-start.2) | collective-permute-done | bytes 131104 | tf_op jit(solution)/shard_map/ppermute | solution.py:184
  15.1 1.5 %collective-permute-done.3.refs_12_ = bf16[2,2,64,256]{3,2,1,0:T(8,128)(2,1)S(1)} collective-permute-done((bf16[2,2,64,256]{3,2,1,0:T(8,128)(2,1)}, bf16[2,2,64,256]{3,2,1,0:T(8,128)(2,1)S(1)}, u32[]{:S(2)}, u32[]{:S(2)}) %collective-permute-start.3) | collective-permute-done | bytes 131104 | tf_op jit(solution)/shard_map/ppermute | solution.py:184
  16.5 0.0 collective-permute-done.4.refs_13_
  16.5 3.5 %collective-permute-start.13 = (bf16[2,2,64,256]{3,2,1,0:T(8,128)(2,1)S(1)}, bf16[2,2,64,256]{3,2,1,0:T(8,128)(2,1)S(1)}, u32[]{:S(2)}, u32[]{:S(2)}) collective-permute-start(bf16[2,2,64,256]{3,2,1,0:T(8,128)(2,1)S(1)} %collective-permute-done.2.refs_11_), channel_id=1, source_target_pairs={{0,8},{8,0},{1,9},{9,1},{2,10},{10,2},{3,11},{11,3},{4,12},{12,4},... | collective-permute-start | bytes 393224 | tf_op jit(solution)/shard_map/ppermute | solution.py:187
  20.0 0.1 collective-permute-start.14
  20.1 0.4 collective-permute-start.15
  20.5 0.1 collective-permute-start.12
  20.6 1.3 %collective-permute-start.8 = (bf16[2,64,1024]{2,1,0:T(8,128)(2,1)S(1)}, bf16[2,64,1024]{2,1,0:T(8,128)(2,1)S(1)}, u32[]{:S(2)}, u32[]{:S(2)}) collective-permute-start(bf16[2,64,1024]{2,1,0:T(8,128)(2,1)S(1)} %collective-permute-done.refs_1_), channel_id=1, source_target_pairs={{0,8},{8,0},{1,9},{9,1},{2,10},{10,2},{3,11},{11,3},{4,12},{12,4},... | collective-permute-start | bytes 786440 | tf_op jit(solution)/shard_map/ppermute | solution.py:187
  21.9 0.0 collective-permute-start.11
  21.9 0.5 collective-permute-start.7
  22.4 1.0 %broadcast_select_fusion.refs_0_ = bf16[2,64,1024]{2,1,0:T(8,128)(2,1)S(1)} fusion(bf16[2,64,1024]{2,1,0:T(8,128)(2,1)} %bitcast.14, pred[]{:T(512)S(6)} %lt.3), kind=kLoop, calls=%fused_computation.6 | loop fusion | flops 131072 | bytes 524289 | tf_op jit(solution)/shard_map/jit(_where)/select_n | solution.py:211
  23.4 0.2 collective-permute-start.10
  23.6 0.4 collective-permute-start.9
  24.0 0.9 %broadcast_select_fusion.1.refs_10_ = bf16[2,2,80,256]{3,2,1,0:T(8,128)(2,1)S(1)} fusion(bf16[2,2,80,256]{3,2,1,0:T(8,128)(2,1)} %get-tuple-element.23, pred[]{:T(512)S(6)} %lt.3), kind=kLoop, calls=%fused_computation.7 | loop fusion | flops 81920 | bytes 327681 | tf_op jit(solution)/shard_map/jit(_where)/select_n | solution.py:210
  24.9 0.2 collective-permute-done.9.refs_7_
  25.1 2.6 %image.1 = bf16[2048,256]{1,0:T(8,128)(2,1)} custom-call(bf16[2,64,1024]{2,1,0:T(8,128)(2,1)S(1)} %broadcast_select_fusion.refs_0_, bf16[2,64,1024]{2,1,0:T(8,128)(2,1)S(1)} %collective-permute-done.refs_1_, bf16[64,1024]{1,0:T(8,128)(2,1)S(1)} %collective-permute-done.5.refs_2_, bf16[64,1024]{1,0:T(8,128)(2,1)S(1)} %collective-permute-done.6.refs_3_, ...), custom_call_target="tpu_custom_call" | custom-call | tf_op jit(solution)/shard_map/image/pallas_call | solution.py:212
  27.8 12.3 %all-to-all-start = ((bf16[256,8,256]{2,1,0:T(8,128)(2,1)}), bf16[256,8,256]{2,1,0:T(8,128)(2,1)S(1)}, u32[]{:S(2)}, u32[]{:S(2)}) async-start(bf16[256,8,256]{2,1,0:T(8,128)(2,1)} %bitcast.3), calls=%async_computation | async-start | bytes 2097152 | tf_op jit(solution)/shard_map/all_to_all | solution.py:234
  40.1 0.1 reshape.21
  40.2 0.1 copy.10
  40.3 0.1 eq.15
  40.4 0.2 select_reduce_fusion
  40.5 1.0 %fusion.1 = (f32[64,512]{0,1:T(8,128)S(1)}, f32[64,512]{0,1:T(8,128)S(1)}, f32[64,512]{0,1:T(8,128)S(1)}) fusion(f32[512]{0:T(512)S(1)} %convert_add_fusion, f32[64]{0:T(128)S(1)} %broadcast_multiply_fusion), kind=kLoop, calls=%fused_computation.10 | loop fusion | flops 65536 | bytes 395520 | tf_op jit(solution)/shard_map/neg | solution.py:239
  41.5 0.2 fusion
  41.8 0.1 copy.11.g_ref
  41.9 30.4 %all-to-all-done = bf16[256,8,256]{2,1,0:T(8,128)(2,1)S(1)} async-done(((bf16[256,8,256]{2,1,0:T(8,128)(2,1)}), bf16[256,8,256]{2,1,0:T(8,128)(2,1)S(1)}, u32[]{:S(2)}, u32[]{:S(2)}) %all-to-all-start) | async-done | bytes 1048608 | tf_op jit(solution)/shard_map/all_to_all | solution.py:234
  72.3 5.9 %recover.1 = f32[2,4,256,512]{3,2,1,0:T(8,128)} custom-call(bf16[4,4,16,8,256]{4,3,2,1,0:T(8,128)(2,1)S(1)} %bitcast.10, bf16[128,1024]{1,0:T(8,128)(2,1)S(1)} %copy.11.g_ref, bf16[1024,128]{1,0:T(8,128)(2,1)S(1)} %get-tuple-element.27.h_ref), custom_call_target="tpu_custom_call" | custom-call | tf_op jit(solution)/shard_map/recover/pallas_call | solution.py:245
  (22 shorter events, 0.1 us)
Async XLA Ops:
  0.0 10.1 %collective-permute-start.1 = (bf16[2,64,1024]{2,1,0:T(8,128)(2,1)}, bf16[2,64,1024]{2,1,0:T(8,128)(2,1)S(1)}, u32[]{:S(2)}, u32[]{:S(2)}) collective-permute-start(bf16[2,64,1024]{2,1,0:T(8,128)(2,1)} %bitcast.11), channel_id=1, source_target_pairs={{0,192},{64,0},{128,64},{192,128},{1,193},{65,1},{129,65},{193,129... | collective-permute-start | bytes 786440 | tf_op jit(solution)/shard_map/ppermute | solution.py:184
  3.3 8.7 %collective-permute-start = (bf16[2,64,1024]{2,1,0:T(8,128)(2,1)}, bf16[2,64,1024]{2,1,0:T(8,128)(2,1)S(1)}, u32[]{:S(2)}, u32[]{:S(2)}) collective-permute-start(bf16[2,64,1024]{2,1,0:T(8,128)(2,1)} %bitcast.12), channel_id=1, source_target_pairs={{0,64},{64,128},{128,192},{192,0},{1,65},{65,129},{129,193},{193,1... | collective-permute-start | bytes 786440 | tf_op jit(solution)/shard_map/ppermute | solution.py:184
  6.2 33.9 %copy-start = (s32[64]{0:T(128)S(1)}, s32[64]{0:T(128)}, u32[]{:S(2)}) copy-start(s32[64]{0:T(128)} %param.12) | copy-start | bytes 772
  6.2 34.2 %copy-start.1 = (f32[64]{0:T(128)S(1)}, f32[64]{0:T(128)}, u32[]{:S(2)}) copy-start(f32[64]{0:T(128)} %param.13) | copy-start | bytes 772
  6.2 8.9 %collective-permute-start.2 = (bf16[2,2,64,256]{3,2,1,0:T(8,128)(2,1)}, bf16[2,2,64,256]{3,2,1,0:T(8,128)(2,1)S(1)}, u32[]{:S(2)}, u32[]{:S(2)}) collective-permute-start(bf16[2,2,64,256]{3,2,1,0:T(8,128)(2,1)} %get-tuple-element.17), channel_id=1, source_target_pairs={{0,64},{64,128},{128,192},{192,0},{1,65},{65,129},{129,193},{193,1... | collective-permute-start | bytes 393224 | tf_op jit(solution)/shard_map/ppermute | solution.py:184
  6.4 10.1 %collective-permute-start.3 = (bf16[2,2,64,256]{3,2,1,0:T(8,128)(2,1)}, bf16[2,2,64,256]{3,2,1,0:T(8,128)(2,1)S(1)}, u32[]{:S(2)}, u32[]{:S(2)}) collective-permute-start(bf16[2,2,64,256]{3,2,1,0:T(8,128)(2,1)} %get-tuple-element.18), channel_id=1, source_target_pairs={{0,128},{64,192},{128,0},{192,64},{1,129},{65,193},{129,1},{193,65... | collective-permute-start | bytes 393224 | tf_op jit(solution)/shard_map/ppermute | solution.py:184
  10.1 6.4 %collective-permute-start.4 = (bf16[2,2,64,256]{3,2,1,0:T(8,128)(2,1)}, bf16[2,2,64,256]{3,2,1,0:T(8,128)(2,1)S(1)}, u32[]{:S(2)}, u32[]{:S(2)}) collective-permute-start(bf16[2,2,64,256]{3,2,1,0:T(8,128)(2,1)} %get-tuple-element.19), channel_id=1, source_target_pairs={{0,192},{64,0},{128,64},{192,128},{1,193},{65,1},{129,65},{193,129... | collective-permute-start | bytes 393224 | tf_op jit(solution)/shard_map/ppermute | solution.py:184
  10.1 10.4 %collective-permute-start.6 = (bf16[64,1024]{1,0:T(8,128)(2,1)S(1)}, bf16[64,1024]{1,0:T(8,128)(2,1)S(1)}, u32[]{:S(2)}, u32[]{:S(2)}) collective-permute-start(bf16[64,1024]{1,0:T(8,128)(2,1)S(1)} %slice_bitcast_fusion), channel_id=1, source_target_pairs={{0,192},{64,0},{128,64},{192,128},{1,193},{65,1},{129,65},{193,129... | collective-permute-start | bytes 393224 | tf_op jit(solution)/shard_map/ppermute | solution.py:184
  12.0 8.6 %collective-permute-start.5 = (bf16[64,1024]{1,0:T(8,128)(2,1)S(1)}, bf16[64,1024]{1,0:T(8,128)(2,1)S(1)}, u32[]{:S(2)}, u32[]{:S(2)}) collective-permute-start(bf16[64,1024]{1,0:T(8,128)(2,1)S(1)} %slice_bitcast_fusion.1), channel_id=1, source_target_pairs={{0,64},{64,128},{128,192},{192,0},{1,65},{65,129},{129,193},{193,1... | collective-permute-start | bytes 393224 | tf_op jit(solution)/shard_map/ppermute | solution.py:184
  16.5 5.4 %collective-permute-start.13 = (bf16[2,2,64,256]{3,2,1,0:T(8,128)(2,1)S(1)}, bf16[2,2,64,256]{3,2,1,0:T(8,128)(2,1)S(1)}, u32[]{:S(2)}, u32[]{:S(2)}) collective-permute-start(bf16[2,2,64,256]{3,2,1,0:T(8,128)(2,1)S(1)} %collective-permute-done.2.refs_11_), channel_id=1, source_target_pairs={{0,8},{8,0},{1,9},{9,1},{2,10},{10,2},{3,11},{11,3},{4,12},{12,4},... | collective-permute-start | bytes 393224 | tf_op jit(solution)/shard_map/ppermute | solution.py:187
  20.0 1.9 %collective-permute-start.14 = (bf16[2,2,64,256]{3,2,1,0:T(8,128)(2,1)S(1)}, bf16[2,2,64,256]{3,2,1,0:T(8,128)(2,1)S(1)}, u32[]{:S(2)}, u32[]{:S(2)}) collective-permute-start(bf16[2,2,64,256]{3,2,1,0:T(8,128)(2,1)S(1)} %collective-permute-done.3.refs_12_), channel_id=1, source_target_pairs={{0,8},{8,0},{1,9},{9,1},{2,10},{10,2},{3,11},{11,3},{4,12},{12,4},... | collective-permute-start | bytes 393224 | tf_op jit(solution)/shard_map/ppermute | solution.py:187
  20.1 3.3 %collective-permute-start.15 = (bf16[2,2,64,256]{3,2,1,0:T(8,128)(2,1)S(1)}, bf16[2,2,64,256]{3,2,1,0:T(8,128)(2,1)S(1)}, u32[]{:S(2)}, u32[]{:S(2)}) collective-permute-start(bf16[2,2,64,256]{3,2,1,0:T(8,128)(2,1)S(1)} %collective-permute-done.4.refs_13_), channel_id=1, source_target_pairs={{0,8},{8,0},{1,9},{9,1},{2,10},{10,2},{3,11},{11,3},{4,12},{12,4},... | collective-permute-start | bytes 393224 | tf_op jit(solution)/shard_map/ppermute | solution.py:187
  20.5 3.0 %collective-permute-start.12 = (bf16[2,2,80,256]{3,2,1,0:T(8,128)(2,1)}, bf16[2,2,80,256]{3,2,1,0:T(8,128)(2,1)S(1)}, u32[]{:S(2)}, u32[]{:S(2)}) collective-permute-start(bf16[2,2,80,256]{3,2,1,0:T(8,128)(2,1)} %get-tuple-element.23), channel_id=1, source_target_pairs={{0,8},{8,0},{1,9},{9,1},{2,10},{10,2},{3,11},{11,3},{4,12},{12,4},... | collective-permute-start | bytes 491528 | tf_op jit(solution)/shard_map/ppermute | solution.py:187
  20.6 4.5 %collective-permute-start.8 = (bf16[2,64,1024]{2,1,0:T(8,128)(2,1)S(1)}, bf16[2,64,1024]{2,1,0:T(8,128)(2,1)S(1)}, u32[]{:S(2)}, u32[]{:S(2)}) collective-permute-start(bf16[2,64,1024]{2,1,0:T(8,128)(2,1)S(1)} %collective-permute-done.refs_1_), channel_id=1, source_target_pairs={{0,8},{8,0},{1,9},{9,1},{2,10},{10,2},{3,11},{11,3},{4,12},{12,4},... | collective-permute-start | bytes 786440 | tf_op jit(solution)/shard_map/ppermute | solution.py:187
  21.9 3.2 %collective-permute-start.11 = (bf16[2,64,1024]{2,1,0:T(8,128)(2,1)S(1)}, bf16[2,64,1024]{2,1,0:T(8,128)(2,1)S(1)}, u32[]{:S(2)}, u32[]{:S(2)}) collective-permute-start(bf16[2,64,1024]{2,1,0:T(8,128)(2,1)S(1)} %collective-permute-done.1.refs_4_), channel_id=1, source_target_pairs={{0,8},{8,0},{1,9},{9,1},{2,10},{10,2},{3,11},{11,3},{4,12},{12,4},... | collective-permute-start | bytes 786440 | tf_op jit(solution)/shard_map/ppermute | solution.py:187
  21.9 3.2 %collective-permute-start.7 = (bf16[2,64,1024]{2,1,0:T(8,128)(2,1)}, bf16[2,64,1024]{2,1,0:T(8,128)(2,1)S(1)}, u32[]{:S(2)}, u32[]{:S(2)}) collective-permute-start(bf16[2,64,1024]{2,1,0:T(8,128)(2,1)} %bitcast.13), channel_id=1, source_target_pairs={{0,8},{8,0},{1,9},{9,1},{2,10},{10,2},{3,11},{11,3},{4,12},{12,4},... | collective-permute-start | bytes 786440 | tf_op jit(solution)/shard_map/ppermute | solution.py:187
  23.4 1.5 %collective-permute-start.10 = (bf16[64,1024]{1,0:T(8,128)(2,1)S(1)}, bf16[64,1024]{1,0:T(8,128)(2,1)S(1)}, u32[]{:S(2)}, u32[]{:S(2)}) collective-permute-start(bf16[64,1024]{1,0:T(8,128)(2,1)S(1)} %collective-permute-done.6.refs_3_), channel_id=1, source_target_pairs={{0,8},{8,0},{1,9},{9,1},{2,10},{10,2},{3,11},{11,3},{4,12},{12,4},... | collective-permute-start | bytes 393224 | tf_op jit(solution)/shard_map/ppermute | solution.py:187
  23.6 1.5 %collective-permute-start.9 = (bf16[64,1024]{1,0:T(8,128)(2,1)S(1)}, bf16[64,1024]{1,0:T(8,128)(2,1)S(1)}, u32[]{:S(2)}, u32[]{:S(2)}) collective-permute-start(bf16[64,1024]{1,0:T(8,128)(2,1)S(1)} %collective-permute-done.5.refs_2_), channel_id=1, source_target_pairs={{0,8},{8,0},{1,9},{9,1},{2,10},{10,2},{3,11},{11,3},{4,12},{12,4},... | collective-permute-start | bytes 393224 | tf_op jit(solution)/shard_map/ppermute | solution.py:187
  27.8 44.5 %all-to-all-start = ((bf16[256,8,256]{2,1,0:T(8,128)(2,1)}), bf16[256,8,256]{2,1,0:T(8,128)(2,1)S(1)}, u32[]{:S(2)}, u32[]{:S(2)}) async-start(bf16[256,8,256]{2,1,0:T(8,128)(2,1)} %bitcast.3), calls=%async_computation | async-start | bytes 2097152 | tf_op jit(solution)/shard_map/all_to_all | solution.py:234

commit v6 on v5

--- a/solution.py
+++ b/solution.py
@@ -202,13 +202,17 @@
         name="focus",
     )(lateral, vertical, echo, slant)
     focus = [focus[0]] + [turn(focus[s], s) for s in range(1, nx)]
-    at_late, one_late, three_late, *focus = lax.optimization_barrier((at, one, three, *focus))
+    inside = lax.axis_index("x") < nx
+    own = jnp.where(inside, at, jnp.zeros_like(at))
+    own_focus = jnp.where(inside, focus[0], jnp.zeros_like(focus[0]))
+    at_late, one_late, three_late, own, own_focus, *focus = lax.optimization_barrier(
+        (at, one, three, own, own_focus, *focus)
+    )
     focus = focus + [swap(value) for value in focus]
     held = [one, two_re, two_im, three]
     swapped = [swap(value) for value in (at_late, one_late, two_re, two_im, three_late)]
-    inside = lax.axis_index("x") < nx
-    focus[0] = jnp.where(inside, focus[0], jnp.zeros_like(focus[0]))
-    held = [jnp.where(inside, at_late, jnp.zeros_like(at))] + held + swapped
+    focus[0] = own_focus
+    held = [own] + held + swapped
     return pl.pallas_call(
         functools.partial(image_kernel, nx),
         out_shape=jax.ShapeDtypeStruct((2 * rows, cols), bf),

time: 78.4 us -> 77.9 us (level)
    ppermute x7, waiting for transfers between devices: 4.44 us -> 2.83 us  [turn(): return lax.ppermute(value, 'x', [(i, (i + step) % nx) for i in range(nx)])]
    ppermute x9, waiting for transfers between devices: 0.2 us -> 1.27 us  [swap(): return lax.ppermute(value, 'c', [(0, 1), (1, 0)])]
  transfers between devices with their start and end apart: 17 -> 17, of which waited for: 4 -> 5; matrix products, arithmetic and copies ran while one was open for 5% -> 5% of each run, Pallas kernels for 4% -> 4%
where the time goes in v6:
time: 77.9 us; the launch traced here: 77.7 us
  waiting for transfers between devices  34.5 us (44%)
  starting transfers between devices  27.9 us (36%)
  Pallas kernels  11.4 us (15%)
  other arithmetic  3.29 us (4%)
    all_to_all x1, waiting for transfers between devices, body(): image = lax.all_to_all(image, ('x', 'zh', 'c', 'y', 'zl'), 0, 0, tiled=True)  30.4 us
    all_to_all x1, starting transfers between devices, body(): image = lax.all_to_all(image, ('x', 'zh', 'c', 'y', 'zl'), 0, 0, tiled=True)  12.7 us
    ppermute x7, starting transfers between devices, turn(): return lax.ppermute(value, 'x', [(i, (i + step) % nx) for i in range(nx)])  8.88 us
    ppermute x9, starting transfers between devices, swap(): return lax.ppermute(value, 'c', [(0, 1), (1, 0)])  6.36 us
    pallas_call x1, Pallas kernels, body(): pl.pallas_call(recover_kernel, grid=(own,), out_shape=jax.ShapeDtypeStruc...  5.93 us
    pallas_call x1, Pallas kernels, partial_image(): pl.pallas_call(focus_kernel, out_shape=[jax.ShapeDtypeStruct(shape, bf) f...  2.86 us
    ppermute x7, waiting for transfers between devices, turn(): return lax.ppermute(value, 'x', [(i, (i + step) % nx) for i in range(nx)])  2.83 us
    pallas_call x1, Pallas kernels, partial_image(): pl.pallas_call(functools.partial(image_kernel, nx), out_shape=jax.ShapeDt...  2.64 us
  transfers between devices with their start and end apart: 17, of which 5 were waited for; matrix products, arithmetic and copies ran while one was open for 5% of the time, Pallas kernels for 4%

profile of v6, /device:TPU:1, one launch (start us, length us, event | category | flops | bytes accessed | tf_op | source)
XLA Modules:
  0.0 77.7 jit_solution(18353735514204071603)
XLA Ops:
  0.0 3.3 %collective-permute-start.1 = (bf16[2,64,1024]{2,1,0:T(8,128)(2,1)}, bf16[2,64,1024]{2,1,0:T(8,128)(2,1)S(1)}, u32[]{:S(2)}, u32[]{:S(2)}) collective-permute-start(bf16[2,64,1024]{2,1,0:T(8,128)(2,1)} %bitcast.12), channel_id=1, source_target_pairs={{0,192},{64,0},{128,64},{192,128},{1,193},{65,1},{129,65},{193,129... | collective-permute-start | bytes 786440 | tf_op jit(solution)/shard_map/ppermute | solution.py:184
  3.3 2.9 %focus.1 = (bf16[2,2,80,256]{3,2,1,0:T(8,128)(2,1)}, bf16[2,2,64,256]{3,2,1,0:T(8,128)(2,1)}, bf16[2,2,64,256]{3,2,1,0:T(8,128)(2,1)}, bf16[2,2,64,256]{3,2,1,0:T(8,128)(2,1)}) custom-call(s32[8]{0:T(128)} %lat_ref.1, s32[8]{0:T(128)} %ver_ref.1, bf16[2,8,64,512]{3,2,1,0:T(8,128)(2,1)} %echo_ref.1, bf16[2,512,256]{2,1,0:T(8,128)(2,1)} %kern_ref.1), custom_call_target="tpu_custom_call" | custom-call | tf_op jit(solution)/shard_map/focus/pallas_call | solution.py:197
  6.2 0.3 collective-permute-start.2
  6.4 3.7 %collective-permute-start.3 = (bf16[2,2,64,256]{3,2,1,0:T(8,128)(2,1)}, bf16[2,2,64,256]{3,2,1,0:T(8,128)(2,1)S(1)}, u32[]{:S(2)}, u32[]{:S(2)}) collective-permute-start(bf16[2,2,64,256]{3,2,1,0:T(8,128)(2,1)} %get-tuple-element.20), channel_id=1, source_target_pairs={{0,128},{64,192},{128,0},{192,64},{1,129},{65,193},{129,1},{193,65... | collective-permute-start | bytes 393224 | tf_op jit(solution)/shard_map/ppermute | solution.py:184
  10.1 1.0 %broadcast_select_fusion.refs_0_ = bf16[2,64,1024]{2,1,0:T(8,128)(2,1)S(1)} fusion(pred[]{:T(512)S(6)} %lt.3, bf16[2,1024,64]{1,2,0:T(8,128)(2,1)} %param.8), kind=kLoop, calls=%fused_computation.6 | loop fusion | flops 131072 | bytes 524289 | tf_op jit(solution)/shard_map/jit(_where)/select_n | solution.py:206
  11.1 0.9 %broadcast_select_fusion.1.refs_10_ = bf16[2,2,80,256]{3,2,1,0:T(8,128)(2,1)S(1)} fusion(bf16[2,2,80,256]{3,2,1,0:T(8,128)(2,1)} %get-tuple-element.30, pred[]{:T(512)S(6)} %lt.3), kind=kLoop, calls=%fused_computation.7 | loop fusion | flops 81920 | bytes 327681 | tf_op jit(solution)/shard_map/jit(_where)/select_n | solution.py:207
  12.0 0.4 collective-permute-start.6
  12.4 1.3 %collective-permute-start.5 = (bf16[64,1024]{1,0:T(8,128)(2,1)S(1)}, bf16[64,1024]{1,0:T(8,128)(2,1)S(1)}, u32[]{:S(2)}, u32[]{:S(2)}) collective-permute-start(bf16[64,1024]{1,0:T(8,128)(2,1)S(1)} %slice_bitcast_fusion.1), channel_id=1, source_target_pairs={{0,64},{64,128},{128,192},{192,0},{1,65},{65,129},{129,193},{193,1... | collective-permute-start | bytes 393224 | tf_op jit(solution)/shard_map/ppermute | solution.py:184
  13.7 1.4 %collective-permute-done.2.refs_11_ = bf16[2,2,64,256]{3,2,1,0:T(8,128)(2,1)S(1)} collective-permute-done((bf16[2,2,64,256]{3,2,1,0:T(8,128)(2,1)}, bf16[2,2,64,256]{3,2,1,0:T(8,128)(2,1)S(1)}, u32[]{:S(2)}, u32[]{:S(2)}) %collective-permute-start.2) | collective-permute-done | bytes 131104 | tf_op jit(solution)/shard_map/ppermute | solution.py:184
  15.1 1.5 %collective-permute-done.3.refs_12_ = bf16[2,2,64,256]{3,2,1,0:T(8,128)(2,1)S(1)} collective-permute-done((bf16[2,2,64,256]{3,2,1,0:T(8,128)(2,1)}, bf16[2,2,64,256]{3,2,1,0:T(8,128)(2,1)S(1)}, u32[]{:S(2)}, u32[]{:S(2)}) %collective-permute-start.3) | collective-permute-done | bytes 131104 | tf_op jit(solution)/shard_map/ppermute | solution.py:184
  16.5 3.3 %collective-permute-start.13 = (bf16[2,2,64,256]{3,2,1,0:T(8,128)(2,1)S(1)}, bf16[2,2,64,256]{3,2,1,0:T(8,128)(2,1)S(1)}, u32[]{:S(2)}, u32[]{:S(2)}) collective-permute-start(bf16[2,2,64,256]{3,2,1,0:T(8,128)(2,1)S(1)} %collective-permute-done.2.refs_11_), channel_id=1, source_target_pairs={{0,8},{8,0},{1,9},{9,1},{2,10},{10,2},{3,11},{11,3},{4,12},{12,4},... | collective-permute-start | bytes 393224 | tf_op jit(solution)/shard_map/ppermute | solution.py:187
  19.9 0.1 collective-permute-start.14
  20.0 0.4 collective-permute-start.12
  20.4 0.1 collective-permute-start.15
  20.5 1.4 %collective-permute-start.7 = (bf16[2,64,1024]{2,1,0:T(8,128)(2,1)}, bf16[2,64,1024]{2,1,0:T(8,128)(2,1)S(1)}, u32[]{:S(2)}, u32[]{:S(2)}) collective-permute-start(bf16[2,64,1024]{2,1,0:T(8,128)(2,1)} %bitcast.14), channel_id=1, source_target_pairs={{0,8},{8,0},{1,9},{9,1},{2,10},{10,2},{3,11},{11,3},{4,12},{12,4},... | collective-permute-start | bytes 786440 | tf_op jit(solution)/shard_map/ppermute | solution.py:187
  21.9 0.0 collective-permute-start.8
  21.9 0.5 collective-permute-start.11
  22.4 0.1 collective-permute-start.10
  22.5 0.4 collective-permute-start.9
  22.9 1.1 %collective-permute-done.10.refs_8_ = bf16[64,1024]{1,0:T(8,128)(2,1)S(1)} collective-permute-done((bf16[64,1024]{1,0:T(8,128)(2,1)S(1)}, bf16[64,1024]{1,0:T(8,128)(2,1)S(1)}, u32[]{:S(2)}, u32[]{:S(2)}) %collective-permute-start.10) | collective-permute-done | bytes 131104 | tf_op jit(solution)/shard_map/ppermute | solution.py:187
  24.0 0.2 collective-permute-done.9.refs_7_
  24.2 2.6 %image.1 = bf16[2048,256]{1,0:T(8,128)(2,1)} custom-call(bf16[2,64,1024]{2,1,0:T(8,128)(2,1)S(1)} %broadcast_select_fusion.refs_0_, bf16[2,64,1024]{2,1,0:T(8,128)(2,1)S(1)} %collective-permute-done.refs_1_, bf16[64,1024]{1,0:T(8,128)(2,1)S(1)} %collective-permute-done.5.refs_2_, bf16[64,1024]{1,0:T(8,128)(2,1)S(1)} %collective-permute-done.6.refs_3_, ...), custom_call_target="tpu_custom_call" | custom-call | tf_op jit(solution)/shard_map/image/pallas_call | solution.py:216
  26.8 12.7 %all-to-all-start = ((bf16[256,8,256]{2,1,0:T(8,128)(2,1)}), bf16[256,8,256]{2,1,0:T(8,128)(2,1)S(1)}, u32[]{:S(2)}, u32[]{:S(2)}) async-start(bf16[256,8,256]{2,1,0:T(8,128)(2,1)} %bitcast.3), calls=%async_computation | async-start | bytes 2097152 | tf_op jit(solution)/shard_map/all_to_all | solution.py:238
  39.6 0.1 reshape.21
  39.6 0.1 copy.10
  39.7 0.1 eq.15
  39.8 0.2 select_reduce_fusion
  40.0 1.0 %fusion.1 = (f32[64,512]{0,1:T(8,128)S(1)}, f32[64,512]{0,1:T(8,128)S(1)}, f32[64,512]{0,1:T(8,128)S(1)}) fusion(f32[512]{0:T(512)S(1)} %convert_add_fusion, f32[64]{0:T(128)S(1)} %broadcast_multiply_fusion), kind=kLoop, calls=%fused_computation.10 | loop fusion | flops 65536 | bytes 395520 | tf_op jit(solution)/shard_map/neg | solution.py:243
  41.0 0.2 fusion
  41.2 0.1 copy.11.g_ref
  41.4 30.4 %all-to-all-done = bf16[256,8,256]{2,1,0:T(8,128)(2,1)S(1)} async-done(((bf16[256,8,256]{2,1,0:T(8,128)(2,1)}), bf16[256,8,256]{2,1,0:T(8,128)(2,1)S(1)}, u32[]{:S(2)}, u32[]{:S(2)}) %all-to-all-start) | async-done | bytes 1048608 | tf_op jit(solution)/shard_map/all_to_all | solution.py:238
  71.7 5.9 %recover.1 = f32[2,4,256,512]{3,2,1,0:T(8,128)} custom-call(bf16[4,4,16,8,256]{4,3,2,1,0:T(8,128)(2,1)S(1)} %bitcast.11, bf16[128,1024]{1,0:T(8,128)(2,1)S(1)} %copy.11.g_ref, bf16[1024,128]{1,0:T(8,128)(2,1)S(1)} %get-tuple-element.31.h_ref), custom_call_target="tpu_custom_call" | custom-call | tf_op jit(solution)/shard_map/recover/pallas_call | solution.py:249
  (22 shorter events, 0.1 us)
Async XLA Ops:
  0.0 12.0 %collective-permute-start.1 = (bf16[2,64,1024]{2,1,0:T(8,128)(2,1)}, bf16[2,64,1024]{2,1,0:T(8,128)(2,1)S(1)}, u32[]{:S(2)}, u32[]{:S(2)}) collective-permute-start(bf16[2,64,1024]{2,1,0:T(8,128)(2,1)} %bitcast.12), channel_id=1, source_target_pairs={{0,192},{64,0},{128,64},{192,128},{1,193},{65,1},{129,65},{193,129... | collective-permute-start | bytes 786440 | tf_op jit(solution)/shard_map/ppermute | solution.py:184
  3.3 9.1 %collective-permute-start = (bf16[2,64,1024]{2,1,0:T(8,128)(2,1)}, bf16[2,64,1024]{2,1,0:T(8,128)(2,1)S(1)}, u32[]{:S(2)}, u32[]{:S(2)}) collective-permute-start(bf16[2,64,1024]{2,1,0:T(8,128)(2,1)} %bitcast.13), channel_id=1, source_target_pairs={{0,64},{64,128},{128,192},{192,0},{1,65},{65,129},{129,193},{193,1... | collective-permute-start | bytes 786440 | tf_op jit(solution)/shard_map/ppermute | solution.py:184
  6.2 33.4 %copy-start = (s32[64]{0:T(128)S(1)}, s32[64]{0:T(128)}, u32[]{:S(2)}) copy-start(s32[64]{0:T(128)} %param.12) | copy-start | bytes 772
  6.2 33.6 %copy-start.1 = (f32[64]{0:T(128)S(1)}, f32[64]{0:T(128)}, u32[]{:S(2)}) copy-start(f32[64]{0:T(128)} %param.13) | copy-start | bytes 772
  6.2 8.9 %collective-permute-start.2 = (bf16[2,2,64,256]{3,2,1,0:T(8,128)(2,1)}, bf16[2,2,64,256]{3,2,1,0:T(8,128)(2,1)S(1)}, u32[]{:S(2)}, u32[]{:S(2)}) collective-permute-start(bf16[2,2,64,256]{3,2,1,0:T(8,128)(2,1)} %get-tuple-element.19), channel_id=1, source_target_pairs={{0,64},{64,128},{128,192},{192,0},{1,65},{65,129},{129,193},{193,1... | collective-permute-start | bytes 393224 | tf_op jit(solution)/shard_map/ppermute | solution.py:184
  6.4 10.1 %collective-permute-start.3 = (bf16[2,2,64,256]{3,2,1,0:T(8,128)(2,1)}, bf16[2,2,64,256]{3,2,1,0:T(8,128)(2,1)S(1)}, u32[]{:S(2)}, u32[]{:S(2)}) collective-permute-start(bf16[2,2,64,256]{3,2,1,0:T(8,128)(2,1)} %get-tuple-element.20), channel_id=1, source_target_pairs={{0,128},{64,192},{128,0},{192,64},{1,129},{65,193},{129,1},{193,65... | collective-permute-start | bytes 393224 | tf_op jit(solution)/shard_map/ppermute | solution.py:184
  10.1 6.4 %collective-permute-start.4 = (bf16[2,2,64,256]{3,2,1,0:T(8,128)(2,1)}, bf16[2,2,64,256]{3,2,1,0:T(8,128)(2,1)S(1)}, u32[]{:S(2)}, u32[]{:S(2)}) collective-permute-start(bf16[2,2,64,256]{3,2,1,0:T(8,128)(2,1)} %get-tuple-element.21), channel_id=1, source_target_pairs={{0,192},{64,0},{128,64},{192,128},{1,193},{65,1},{129,65},{193,129... | collective-permute-start | bytes 393224 | tf_op jit(solution)/shard_map/ppermute | solution.py:184
  12.0 8.3 %collective-permute-start.6 = (bf16[64,1024]{1,0:T(8,128)(2,1)S(1)}, bf16[64,1024]{1,0:T(8,128)(2,1)S(1)}, u32[]{:S(2)}, u32[]{:S(2)}) collective-permute-start(bf16[64,1024]{1,0:T(8,128)(2,1)S(1)} %slice_bitcast_fusion), channel_id=1, source_target_pairs={{0,192},{64,0},{128,64},{192,128},{1,193},{65,1},{129,65},{193,129... | collective-permute-start | bytes 393224 | tf_op jit(solution)/shard_map/ppermute | solution.py:184
  12.4 8.0 %collective-permute-start.5 = (bf16[64,1024]{1,0:T(8,128)(2,1)S(1)}, bf16[64,1024]{1,0:T(8,128)(2,1)S(1)}, u32[]{:S(2)}, u32[]{:S(2)}) collective-permute-start(bf16[64,1024]{1,0:T(8,128)(2,1)S(1)} %slice_bitcast_fusion.1), channel_id=1, source_target_pairs={{0,64},{64,128},{128,192},{192,0},{1,65},{65,129},{129,193},{193,1... | collective-permute-start | bytes 393224 | tf_op jit(solution)/shard_map/ppermute | solution.py:184
  16.5 5.4 %collective-permute-start.13 = (bf16[2,2,64,256]{3,2,1,0:T(8,128)(2,1)S(1)}, bf16[2,2,64,256]{3,2,1,0:T(8,128)(2,1)S(1)}, u32[]{:S(2)}, u32[]{:S(2)}) collective-permute-start(bf16[2,2,64,256]{3,2,1,0:T(8,128)(2,1)S(1)} %collective-permute-done.2.refs_11_), channel_id=1, source_target_pairs={{0,8},{8,0},{1,9},{9,1},{2,10},{10,2},{3,11},{11,3},{4,12},{12,4},... | collective-permute-start | bytes 393224 | tf_op jit(solution)/shard_map/ppermute | solution.py:187
  19.9 2.0 %collective-permute-start.14 = (bf16[2,2,64,256]{3,2,1,0:T(8,128)(2,1)S(1)}, bf16[2,2,64,256]{3,2,1,0:T(8,128)(2,1)S(1)}, u32[]{:S(2)}, u32[]{:S(2)}) collective-permute-start(bf16[2,2,64,256]{3,2,1,0:T(8,128)(2,1)S(1)} %collective-permute-done.3.refs_12_), channel_id=1, source_target_pairs={{0,8},{8,0},{1,9},{9,1},{2,10},{10,2},{3,11},{11,3},{4,12},{12,4},... | collective-permute-start | bytes 393224 | tf_op jit(solution)/shard_map/ppermute | solution.py:187
  20.0 2.5 %collective-permute-start.12 = (bf16[2,2,80,256]{3,2,1,0:T(8,128)(2,1)}, bf16[2,2,80,256]{3,2,1,0:T(8,128)(2,1)S(1)}, u32[]{:S(2)}, u32[]{:S(2)}) collective-permute-start(bf16[2,2,80,256]{3,2,1,0:T(8,128)(2,1)} %get-tuple-element.30), channel_id=1, source_target_pairs={{0,8},{8,0},{1,9},{9,1},{2,10},{10,2},{3,11},{11,3},{4,12},{12,4},... | collective-permute-start | bytes 491528 | tf_op jit(solution)/shard_map/ppermute | solution.py:187
  20.4 2.0 %collective-permute-start.15 = (bf16[2,2,64,256]{3,2,1,0:T(8,128)(2,1)S(1)}, bf16[2,2,64,256]{3,2,1,0:T(8,128)(2,1)S(1)}, u32[]{:S(2)}, u32[]{:S(2)}) collective-permute-start(bf16[2,2,64,256]{3,2,1,0:T(8,128)(2,1)S(1)} %collective-permute-done.4.refs_13_), channel_id=1, source_target_pairs={{0,8},{8,0},{1,9},{9,1},{2,10},{10,2},{3,11},{11,3},{4,12},{12,4},... | collective-permute-start | bytes 393224 | tf_op jit(solution)/shard_map/ppermute | solution.py:187
  20.5 3.7 %collective-permute-start.7 = (bf16[2,64,1024]{2,1,0:T(8,128)(2,1)}, bf16[2,64,1024]{2,1,0:T(8,128)(2,1)S(1)}, u32[]{:S(2)}, u32[]{:S(2)}) collective-permute-start(bf16[2,64,1024]{2,1,0:T(8,128)(2,1)} %bitcast.14), channel_id=1, source_target_pairs={{0,8},{8,0},{1,9},{9,1},{2,10},{10,2},{3,11},{11,3},{4,12},{12,4},... | collective-permute-start | bytes 786440 | tf_op jit(solution)/shard_map/ppermute | solution.py:187
  21.9 2.3 %collective-permute-start.8 = (bf16[2,64,1024]{2,1,0:T(8,128)(2,1)S(1)}, bf16[2,64,1024]{2,1,0:T(8,128)(2,1)S(1)}, u32[]{:S(2)}, u32[]{:S(2)}) collective-permute-start(bf16[2,64,1024]{2,1,0:T(8,128)(2,1)S(1)} %collective-permute-done.refs_1_), channel_id=1, source_target_pairs={{0,8},{8,0},{1,9},{9,1},{2,10},{10,2},{3,11},{11,3},{4,12},{12,4},... | collective-permute-start | bytes 786440 | tf_op jit(solution)/shard_map/ppermute | solution.py:187
  21.9 2.3 %collective-permute-start.11 = (bf16[2,64,1024]{2,1,0:T(8,128)(2,1)S(1)}, bf16[2,64,1024]{2,1,0:T(8,128)(2,1)S(1)}, u32[]{:S(2)}, u32[]{:S(2)}) collective-permute-start(bf16[2,64,1024]{2,1,0:T(8,128)(2,1)S(1)} %collective-permute-done.1.refs_4_), channel_id=1, source_target_pairs={{0,8},{8,0},{1,9},{9,1},{2,10},{10,2},{3,11},{11,3},{4,12},{12,4},... | collective-permute-start | bytes 786440 | tf_op jit(solution)/shard_map/ppermute | solution.py:187
  22.4 1.6 %collective-permute-start.10 = (bf16[64,1024]{1,0:T(8,128)(2,1)S(1)}, bf16[64,1024]{1,0:T(8,128)(2,1)S(1)}, u32[]{:S(2)}, u32[]{:S(2)}) collective-permute-start(bf16[64,1024]{1,0:T(8,128)(2,1)S(1)} %collective-permute-done.6.refs_3_), channel_id=1, source_target_pairs={{0,8},{8,0},{1,9},{9,1},{2,10},{10,2},{3,11},{11,3},{4,12},{12,4},... | collective-permute-start | bytes 393224 | tf_op jit(solution)/shard_map/ppermute | solution.py:187
  22.5 1.7 %collective-permute-start.9 = (bf16[64,1024]{1,0:T(8,128)(2,1)S(1)}, bf16[64,1024]{1,0:T(8,128)(2,1)S(1)}, u32[]{:S(2)}, u32[]{:S(2)}) collective-permute-start(bf16[64,1024]{1,0:T(8,128)(2,1)S(1)} %collective-permute-done.5.refs_2_), channel_id=1, source_target_pairs={{0,8},{8,0},{1,9},{9,1},{2,10},{10,2},{3,11},{11,3},{4,12},{12,4},... | collective-permute-start | bytes 393224 | tf_op jit(solution)/shard_map/ppermute | solution.py:187
  26.8 44.9 %all-to-all-start = ((bf16[256,8,256]{2,1,0:T(8,128)(2,1)}), bf16[256,8,256]{2,1,0:T(8,128)(2,1)S(1)}, u32[]{:S(2)}, u32[]{:S(2)}) async-start(bf16[256,8,256]{2,1,0:T(8,128)(2,1)} %bitcast.3), calls=%async_computation | async-start | bytes 2097152 | tf_op jit(solution)/shard_map/all_to_all | solution.py:238

commit v7 on v6

--- a/solution.py
+++ b/solution.py
@@ -189,8 +189,9 @@
     at = jnp.transpose(along, (0, 2, 1))
     one = turn(at, 1)
     three = turn(at, 3)
-    two_re = turn(one[0], 1)
-    two_im = turn(three[1], 3)
+    pass_re, pass_im = one[0], three[1]
+    two_re = turn(pass_re, 1)
+    two_im = turn(pass_im, 3)
 
     spare = 16
     shapes = [(2, 2, pulses + spare, cols)] + [(2, 2, pulses, cols)] * (nx - 1)
@@ -203,8 +204,9 @@
     )(lateral, vertical, echo, slant)
     focus = [focus[0]] + [turn(focus[s], s) for s in range(1, nx)]
     inside = lax.axis_index("x") < nx
-    own = jnp.where(inside, at, jnp.zeros_like(at))
-    own_focus = jnp.where(inside, focus[0], jnp.zeros_like(focus[0]))
+    at_here, focus_here, _, _ = lax.optimization_barrier((at, focus[0], pass_re, pass_im))
+    own = jnp.where(inside, at_here, jnp.zeros_like(at))
+    own_focus = jnp.where(inside, focus_here, jnp.zeros_like(focus[0]))
     at_late, one_late, three_late, own, own_focus, *focus = lax.optimization_barrier(
         (at, one, three, own, own_focus, *focus)
     )

time: 77.9 us -> 77.7 us (level)
  no operation moved by 1% of the time
where the time goes in v7:
time: 77.7 us; the launch traced here: 77.5 us
  waiting for transfers between devices  34.2 us (44%)
  starting transfers between devices  28.1 us (36%)
  Pallas kernels  11.4 us (15%)
  other arithmetic  3.3 us (4%)
    all_to_all x1, waiting for transfers between devices, body(): image = lax.all_to_all(image, ('x', 'zh', 'c', 'y', 'zl'), 0, 0, tiled=True)  30.4 us
    all_to_all x1, starting transfers between devices, body(): image = lax.all_to_all(image, ('x', 'zh', 'c', 'y', 'zl'), 0, 0, tiled=True)  12.5 us
    ppermute x7, starting transfers between devices, turn(): return lax.ppermute(value, 'x', [(i, (i + step) % nx) for i in range(nx)])  9.2 us
    ppermute x9, starting transfers between devices, swap(): return lax.ppermute(value, 'c', [(0, 1), (1, 0)])  6.36 us
    pallas_call x1, Pallas kernels, body(): pl.pallas_call(recover_kernel, grid=(own,), out_shape=jax.ShapeDtypeStruc...  5.94 us
    pallas_call x1, Pallas kernels, partial_image(): pl.pallas_call(focus_kernel, out_shape=[jax.ShapeDtypeStruct(shape, bf) f...  2.86 us
    pallas_call x1, Pallas kernels, partial_image(): pl.pallas_call(functools.partial(image_kernel, nx), out_shape=jax.ShapeDt...  2.64 us
    ppermute x7, waiting for transfers between devices, turn(): return lax.ppermute(value, 'x', [(i, (i + step) % nx) for i in range(nx)])  2.51 us
  transfers between devices with their start and end apart: 17, of which 5 were waited for; matrix products, arithmetic and copies ran while one was open for 5% of the time, Pallas kernels for 4%

profile of v7, /device:TPU:1, one launch (start us, length us, event | category | flops | bytes accessed | tf_op | source)
XLA Modules:
  0.0 77.5 jit_solution(5110012201404588107)
XLA Ops:
  0.0 3.3 %collective-permute-start.1 = (bf16[2,64,1024]{2,1,0:T(8,128)(2,1)}, bf16[2,64,1024]{2,1,0:T(8,128)(2,1)S(1)}, u32[]{:S(2)}, u32[]{:S(2)}) collective-permute-start(bf16[2,64,1024]{2,1,0:T(8,128)(2,1)} %bitcast.11), channel_id=1, source_target_pairs={{0,192},{64,0},{128,64},{192,128},{1,193},{65,1},{129,65},{193,129... | collective-permute-start | bytes 786440 | tf_op jit(solution)/shard_map/ppermute | solution.py:184
  3.3 2.9 %focus.1 = (bf16[2,2,80,256]{3,2,1,0:T(8,128)(2,1)}, bf16[2,2,64,256]{3,2,1,0:T(8,128)(2,1)}, bf16[2,2,64,256]{3,2,1,0:T(8,128)(2,1)}, bf16[2,2,64,256]{3,2,1,0:T(8,128)(2,1)}) custom-call(s32[8]{0:T(128)} %lat_ref.1, s32[8]{0:T(128)} %ver_ref.1, bf16[2,8,64,512]{3,2,1,0:T(8,128)(2,1)} %echo_ref.1, bf16[2,512,256]{2,1,0:T(8,128)(2,1)} %kern_ref.1), custom_call_target="tpu_custom_call" | custom-call | tf_op jit(solution)/shard_map/focus/pallas_call | solution.py:198
  6.2 0.3 collective-permute-start.2
  6.4 3.7 %collective-permute-start.3 = (bf16[2,2,64,256]{3,2,1,0:T(8,128)(2,1)}, bf16[2,2,64,256]{3,2,1,0:T(8,128)(2,1)S(1)}, u32[]{:S(2)}, u32[]{:S(2)}) collective-permute-start(bf16[2,2,64,256]{3,2,1,0:T(8,128)(2,1)} %get-tuple-element.24), channel_id=1, source_target_pairs={{0,128},{64,192},{128,0},{192,64},{1,129},{65,193},{129,1},{193,65... | collective-permute-start | bytes 393224 | tf_op jit(solution)/shard_map/ppermute | solution.py:184
  10.1 1.9 %collective-permute-start.6 = (bf16[64,1024]{1,0:T(8,128)(2,1)S(1)}, bf16[64,1024]{1,0:T(8,128)(2,1)S(1)}, u32[]{:S(2)}, u32[]{:S(2)}) collective-permute-start(bf16[64,1024]{1,0:T(8,128)(2,1)S(1)} %slice_bitcast_fusion), channel_id=1, source_target_pairs={{0,192},{64,0},{128,64},{192,128},{1,193},{65,1},{129,65},{193,129... | collective-permute-start | bytes 393224 | tf_op jit(solution)/shard_map/ppermute | solution.py:184
  12.0 0.1 collective-permute-start.5
  12.1 1.0 %broadcast_select_fusion.refs_0_ = bf16[2,64,1024]{2,1,0:T(8,128)(2,1)S(1)} fusion(bf16[2,64,1024]{2,1,0:T(8,128)(2,1)} %bitcast.13, pred[]{:T(512)S(6)} %lt.3), kind=kLoop, calls=%fused_computation.6 | loop fusion | flops 131072 | bytes 524289 | tf_op jit(solution)/shard_map/jit(_where)/select_n | solution.py:208
  13.1 0.9 %broadcast_select_fusion.1.refs_10_ = bf16[2,2,80,256]{3,2,1,0:T(8,128)(2,1)S(1)} fusion(bf16[2,2,80,256]{3,2,1,0:T(8,128)(2,1)} %get-tuple-element.34, pred[]{:T(512)S(6)} %lt.3), kind=kLoop, calls=%fused_computation.7 | loop fusion | flops 81920 | bytes 327681 | tf_op jit(solution)/shard_map/jit(_where)/select_n | solution.py:209
  14.0 1.0 %collective-permute-done.2.refs_11_ = bf16[2,2,64,256]{3,2,1,0:T(8,128)(2,1)S(1)} collective-permute-done((bf16[2,2,64,256]{3,2,1,0:T(8,128)(2,1)}, bf16[2,2,64,256]{3,2,1,0:T(8,128)(2,1)S(1)}, u32[]{:S(2)}, u32[]{:S(2)}) %collective-permute-start.2) | collective-permute-done | bytes 131104 | tf_op jit(solution)/shard_map/ppermute | solution.py:184
  15.1 1.5 %collective-permute-done.3.refs_12_ = bf16[2,2,64,256]{3,2,1,0:T(8,128)(2,1)S(1)} collective-permute-done((bf16[2,2,64,256]{3,2,1,0:T(8,128)(2,1)}, bf16[2,2,64,256]{3,2,1,0:T(8,128)(2,1)S(1)}, u32[]{:S(2)}, u32[]{:S(2)}) %collective-permute-start.3) | collective-permute-done | bytes 131104 | tf_op jit(solution)/shard_map/ppermute | solution.py:184
  16.5 3.5 %collective-permute-start.13 = (bf16[2,2,64,256]{3,2,1,0:T(8,128)(2,1)S(1)}, bf16[2,2,64,256]{3,2,1,0:T(8,128)(2,1)S(1)}, u32[]{:S(2)}, u32[]{:S(2)}) collective-permute-start(bf16[2,2,64,256]{3,2,1,0:T(8,128)(2,1)S(1)} %collective-permute-done.2.refs_11_), channel_id=1, source_target_pairs={{0,8},{8,0},{1,9},{9,1},{2,10},{10,2},{3,11},{11,3},{4,12},{12,4},... | collective-permute-start | bytes 393224 | tf_op jit(solution)/shard_map/ppermute | solution.py:187
  20.0 0.1 collective-permute-start.14
  20.1 0.4 collective-permute-start.12
  20.5 0.1 collective-permute-start.15
  20.6 1.3 %collective-permute-start.7 = (bf16[2,64,1024]{2,1,0:T(8,128)(2,1)}, bf16[2,64,1024]{2,1,0:T(8,128)(2,1)S(1)}, u32[]{:S(2)}, u32[]{:S(2)}) collective-permute-start(bf16[2,64,1024]{2,1,0:T(8,128)(2,1)} %bitcast.14), channel_id=1, source_target_pairs={{0,8},{8,0},{1,9},{9,1},{2,10},{10,2},{3,11},{11,3},{4,12},{12,4},... | collective-permute-start | bytes 786440 | tf_op jit(solution)/shard_map/ppermute | solution.py:187
  21.9 0.0 collective-permute-start.8
  21.9 0.5 collective-permute-start.11
  22.4 0.1 collective-permute-start.10
  22.5 0.4 collective-permute-start.9
  22.9 1.1 %collective-permute-done.10.refs_8_ = bf16[64,1024]{1,0:T(8,128)(2,1)S(1)} collective-permute-done((bf16[64,1024]{1,0:T(8,128)(2,1)S(1)}, bf16[64,1024]{1,0:T(8,128)(2,1)S(1)}, u32[]{:S(2)}, u32[]{:S(2)}) %collective-permute-start.10) | collective-permute-done | bytes 131104 | tf_op jit(solution)/shard_map/ppermute | solution.py:187
  24.0 0.2 collective-permute-done.9.refs_7_
  24.2 2.6 %image.1 = bf16[2048,256]{1,0:T(8,128)(2,1)} custom-call(bf16[2,64,1024]{2,1,0:T(8,128)(2,1)S(1)} %broadcast_select_fusion.refs_0_, bf16[2,64,1024]{2,1,0:T(8,128)(2,1)S(1)} %collective-permute-done.refs_1_, bf16[64,1024]{1,0:T(8,128)(2,1)S(1)} %collective-permute-done.5.refs_2_, bf16[64,1024]{1,0:T(8,128)(2,1)S(1)} %collective-permute-done.6.refs_3_, ...), custom_call_target="tpu_custom_call" | custom-call | tf_op jit(solution)/shard_map/image/pallas_call | solution.py:218
  26.8 12.5 %all-to-all-start = ((bf16[256,8,256]{2,1,0:T(8,128)(2,1)}), bf16[256,8,256]{2,1,0:T(8,128)(2,1)S(1)}, u32[]{:S(2)}, u32[]{:S(2)}) async-start(bf16[256,8,256]{2,1,0:T(8,128)(2,1)} %bitcast.3), calls=%async_computation | async-start | bytes 2097152 | tf_op jit(solution)/shard_map/all_to_all | solution.py:240
  39.3 0.1 reshape.21
  39.4 0.1 copy.10
  39.5 0.1 eq.15
  39.6 0.2 select_reduce_fusion
  39.8 1.0 %fusion.1 = (f32[64,512]{0,1:T(8,128)S(1)}, f32[64,512]{0,1:T(8,128)S(1)}, f32[64,512]{0,1:T(8,128)S(1)}) fusion(f32[512]{0:T(512)S(1)} %convert_add_fusion, f32[64]{0:T(128)S(1)} %broadcast_multiply_fusion), kind=kLoop, calls=%fused_computation.10 | loop fusion | flops 65536 | bytes 395520 | tf_op jit(solution)/shard_map/neg | solution.py:245
  40.8 0.2 fusion
  41.0 0.1 copy.11.g_ref
  41.2 30.4 %all-to-all-done = bf16[256,8,256]{2,1,0:T(8,128)(2,1)S(1)} async-done(((bf16[256,8,256]{2,1,0:T(8,128)(2,1)}), bf16[256,8,256]{2,1,0:T(8,128)(2,1)S(1)}, u32[]{:S(2)}, u32[]{:S(2)}) %all-to-all-start) | async-done | bytes 1048608 | tf_op jit(solution)/shard_map/all_to_all | solution.py:240
  71.5 5.9 %recover.1 = f32[2,4,256,512]{3,2,1,0:T(8,128)} custom-call(bf16[4,4,16,8,256]{4,3,2,1,0:T(8,128)(2,1)S(1)} %bitcast.10, bf16[128,1024]{1,0:T(8,128)(2,1)S(1)} %copy.11.g_ref, bf16[1024,128]{1,0:T(8,128)(2,1)S(1)} %get-tuple-element.35.h_ref), custom_call_target="tpu_custom_call" | custom-call | tf_op jit(solution)/shard_map/recover/pallas_call | solution.py:251
  (22 shorter events, 0.1 us)
Async XLA Ops:
  0.0 10.1 %collective-permute-start.1 = (bf16[2,64,1024]{2,1,0:T(8,128)(2,1)}, bf16[2,64,1024]{2,1,0:T(8,128)(2,1)S(1)}, u32[]{:S(2)}, u32[]{:S(2)}) collective-permute-start(bf16[2,64,1024]{2,1,0:T(8,128)(2,1)} %bitcast.11), channel_id=1, source_target_pairs={{0,192},{64,0},{128,64},{192,128},{1,193},{65,1},{129,65},{193,129... | collective-permute-start | bytes 786440 | tf_op jit(solution)/shard_map/ppermute | solution.py:184
  3.3 8.7 %collective-permute-start = (bf16[2,64,1024]{2,1,0:T(8,128)(2,1)}, bf16[2,64,1024]{2,1,0:T(8,128)(2,1)S(1)}, u32[]{:S(2)}, u32[]{:S(2)}) collective-permute-start(bf16[2,64,1024]{2,1,0:T(8,128)(2,1)} %bitcast.12), channel_id=1, source_target_pairs={{0,64},{64,128},{128,192},{192,0},{1,65},{65,129},{129,193},{193,1... | collective-permute-start | bytes 786440 | tf_op jit(solution)/shard_map/ppermute | solution.py:184
  6.2 33.2 %copy-start = (s32[64]{0:T(128)S(1)}, s32[64]{0:T(128)}, u32[]{:S(2)}) copy-start(s32[64]{0:T(128)} %param.12) | copy-start | bytes 772
  6.2 33.4 %copy-start.1 = (f32[64]{0:T(128)S(1)}, f32[64]{0:T(128)}, u32[]{:S(2)}) copy-start(f32[64]{0:T(128)} %param.13) | copy-start | bytes 772
  6.2 8.9 %collective-permute-start.2 = (bf16[2,2,64,256]{3,2,1,0:T(8,128)(2,1)}, bf16[2,2,64,256]{3,2,1,0:T(8,128)(2,1)S(1)}, u32[]{:S(2)}, u32[]{:S(2)}) collective-permute-start(bf16[2,2,64,256]{3,2,1,0:T(8,128)(2,1)} %get-tuple-element.23), channel_id=1, source_target_pairs={{0,64},{64,128},{128,192},{192,0},{1,65},{65,129},{129,193},{193,1... | collective-permute-start | bytes 393224 | tf_op jit(solution)/shard_map/ppermute | solution.py:184
  6.4 10.1 %collective-permute-start.3 = (bf16[2,2,64,256]{3,2,1,0:T(8,128)(2,1)}, bf16[2,2,64,256]{3,2,1,0:T(8,128)(2,1)S(1)}, u32[]{:S(2)}, u32[]{:S(2)}) collective-permute-start(bf16[2,2,64,256]{3,2,1,0:T(8,128)(2,1)} %get-tuple-element.24), channel_id=1, source_target_pairs={{0,128},{64,192},{128,0},{192,64},{1,129},{65,193},{129,1},{193,65... | collective-permute-start | bytes 393224 | tf_op jit(solution)/shard_map/ppermute | solution.py:184
  10.1 6.4 %collective-permute-start.4 = (bf16[2,2,64,256]{3,2,1,0:T(8,128)(2,1)}, bf16[2,2,64,256]{3,2,1,0:T(8,128)(2,1)S(1)}, u32[]{:S(2)}, u32[]{:S(2)}) collective-permute-start(bf16[2,2,64,256]{3,2,1,0:T(8,128)(2,1)} %get-tuple-element.25), channel_id=1, source_target_pairs={{0,192},{64,0},{128,64},{192,128},{1,193},{65,1},{129,65},{193,129... | collective-permute-start | bytes 393224 | tf_op jit(solution)/shard_map/ppermute | solution.py:184
  10.1 10.4 %collective-permute-start.6 = (bf16[64,1024]{1,0:T(8,128)(2,1)S(1)}, bf16[64,1024]{1,0:T(8,128)(2,1)S(1)}, u32[]{:S(2)}, u32[]{:S(2)}) collective-permute-start(bf16[64,1024]{1,0:T(8,128)(2,1)S(1)} %slice_bitcast_fusion), channel_id=1, source_target_pairs={{0,192},{64,0},{128,64},{192,128},{1,193},{65,1},{129,65},{193,129... | collective-permute-start | bytes 393224 | tf_op jit(solution)/shard_map/ppermute | solution.py:184
  12.0 8.6 %collective-permute-start.5 = (bf16[64,1024]{1,0:T(8,128)(2,1)S(1)}, bf16[64,1024]{1,0:T(8,128)(2,1)S(1)}, u32[]{:S(2)}, u32[]{:S(2)}) collective-permute-start(bf16[64,1024]{1,0:T(8,128)(2,1)S(1)} %slice_bitcast_fusion.1), channel_id=1, source_target_pairs={{0,64},{64,128},{128,192},{192,0},{1,65},{65,129},{129,193},{193,1... | collective-permute-start | bytes 393224 | tf_op jit(solution)/shard_map/ppermute | solution.py:184
  16.5 5.4 %collective-permute-start.13 = (bf16[2,2,64,256]{3,2,1,0:T(8,128)(2,1)S(1)}, bf16[2,2,64,256]{3,2,1,0:T(8,128)(2,1)S(1)}, u32[]{:S(2)}, u32[]{:S(2)}) collective-permute-start(bf16[2,2,64,256]{3,2,1,0:T(8,128)(2,1)S(1)} %collective-permute-done.2.refs_11_), channel_id=1, source_target_pairs={{0,8},{8,0},{1,9},{9,1},{2,10},{10,2},{3,11},{11,3},{4,12},{12,4},... | collective-permute-start | bytes 393224 | tf_op jit(solution)/shard_map/ppermute | solution.py:187
  20.0 1.9 %collective-permute-start.14 = (bf16[2,2,64,256]{3,2,1,0:T(8,128)(2,1)S(1)}, bf16[2,2,64,256]{3,2,1,0:T(8,128)(2,1)S(1)}, u32[]{:S(2)}, u32[]{:S(2)}) collective-permute-start(bf16[2,2,64,256]{3,2,1,0:T(8,128)(2,1)S(1)} %collective-permute-done.3.refs_12_), channel_id=1, source_target_pairs={{0,8},{8,0},{1,9},{9,1},{2,10},{10,2},{3,11},{11,3},{4,12},{12,4},... | collective-permute-start | bytes 393224 | tf_op jit(solution)/shard_map/ppermute | solution.py:187
  20.1 2.4 %collective-permute-start.12 = (bf16[2,2,80,256]{3,2,1,0:T(8,128)(2,1)}, bf16[2,2,80,256]{3,2,1,0:T(8,128)(2,1)S(1)}, u32[]{:S(2)}, u32[]{:S(2)}) collective-permute-start(bf16[2,2,80,256]{3,2,1,0:T(8,128)(2,1)} %get-tuple-element.34), channel_id=1, source_target_pairs={{0,8},{8,0},{1,9},{9,1},{2,10},{10,2},{3,11},{11,3},{4,12},{12,4},... | collective-permute-start | bytes 491528 | tf_op jit(solution)/shard_map/ppermute | solution.py:187
  20.5 1.9 %collective-permute-start.15 = (bf16[2,2,64,256]{3,2,1,0:T(8,128)(2,1)S(1)}, bf16[2,2,64,256]{3,2,1,0:T(8,128)(2,1)S(1)}, u32[]{:S(2)}, u32[]{:S(2)}) collective-permute-start(bf16[2,2,64,256]{3,2,1,0:T(8,128)(2,1)S(1)} %collective-permute-done.4.refs_13_), channel_id=1, source_target_pairs={{0,8},{8,0},{1,9},{9,1},{2,10},{10,2},{3,11},{11,3},{4,12},{12,4},... | collective-permute-start | bytes 393224 | tf_op jit(solution)/shard_map/ppermute | solution.py:187
  20.6 3.5 %collective-permute-start.7 = (bf16[2,64,1024]{2,1,0:T(8,128)(2,1)}, bf16[2,64,1024]{2,1,0:T(8,128)(2,1)S(1)}, u32[]{:S(2)}, u32[]{:S(2)}) collective-permute-start(bf16[2,64,1024]{2,1,0:T(8,128)(2,1)} %bitcast.14), channel_id=1, source_target_pairs={{0,8},{8,0},{1,9},{9,1},{2,10},{10,2},{3,11},{11,3},{4,12},{12,4},... | collective-permute-start | bytes 786440 | tf_op jit(solution)/shard_map/ppermute | solution.py:187
  21.9 2.3 %collective-permute-start.8 = (bf16[2,64,1024]{2,1,0:T(8,128)(2,1)S(1)}, bf16[2,64,1024]{2,1,0:T(8,128)(2,1)S(1)}, u32[]{:S(2)}, u32[]{:S(2)}) collective-permute-start(bf16[2,64,1024]{2,1,0:T(8,128)(2,1)S(1)} %collective-permute-done.refs_1_), channel_id=1, source_target_pairs={{0,8},{8,0},{1,9},{9,1},{2,10},{10,2},{3,11},{11,3},{4,12},{12,4},... | collective-permute-start | bytes 786440 | tf_op jit(solution)/shard_map/ppermute | solution.py:187
  21.9 2.3 %collective-permute-start.11 = (bf16[2,64,1024]{2,1,0:T(8,128)(2,1)S(1)}, bf16[2,64,1024]{2,1,0:T(8,128)(2,1)S(1)}, u32[]{:S(2)}, u32[]{:S(2)}) collective-permute-start(bf16[2,64,1024]{2,1,0:T(8,128)(2,1)S(1)} %collective-permute-done.1.refs_4_), channel_id=1, source_target_pairs={{0,8},{8,0},{1,9},{9,1},{2,10},{10,2},{3,11},{11,3},{4,12},{12,4},... | collective-permute-start | bytes 786440 | tf_op jit(solution)/shard_map/ppermute | solution.py:187
  22.4 1.6 %collective-permute-start.10 = (bf16[64,1024]{1,0:T(8,128)(2,1)S(1)}, bf16[64,1024]{1,0:T(8,128)(2,1)S(1)}, u32[]{:S(2)}, u32[]{:S(2)}) collective-permute-start(bf16[64,1024]{1,0:T(8,128)(2,1)S(1)} %collective-permute-done.6.refs_3_), channel_id=1, source_target_pairs={{0,8},{8,0},{1,9},{9,1},{2,10},{10,2},{3,11},{11,3},{4,12},{12,4},... | collective-permute-start | bytes 393224 | tf_op jit(solution)/shard_map/ppermute | solution.py:187
  22.5 1.7 %collective-permute-start.9 = (bf16[64,1024]{1,0:T(8,128)(2,1)S(1)}, bf16[64,1024]{1,0:T(8,128)(2,1)S(1)}, u32[]{:S(2)}, u32[]{:S(2)}) collective-permute-start(bf16[64,1024]{1,0:T(8,128)(2,1)S(1)} %collective-permute-done.5.refs_2_), channel_id=1, source_target_pairs={{0,8},{8,0},{1,9},{9,1},{2,10},{10,2},{3,11},{11,3},{4,12},{12,4},... | collective-permute-start | bytes 393224 | tf_op jit(solution)/shard_map/ppermute | solution.py:187
  26.8 44.7 %all-to-all-start = ((bf16[256,8,256]{2,1,0:T(8,128)(2,1)}), bf16[256,8,256]{2,1,0:T(8,128)(2,1)S(1)}, u32[]{:S(2)}, u32[]{:S(2)}) async-start(bf16[256,8,256]{2,1,0:T(8,128)(2,1)} %bitcast.3), calls=%async_computation | async-start | bytes 2097152 | tf_op jit(solution)/shard_map/all_to_all | solution.py:240

commit v8 on v7

--- a/solution.py
+++ b/solution.py
@@ -186,13 +186,6 @@
     def swap(value):
         return lax.ppermute(value, "c", [(0, 1), (1, 0)])
 
-    at = jnp.transpose(along, (0, 2, 1))
-    one = turn(at, 1)
-    three = turn(at, 3)
-    pass_re, pass_im = one[0], three[1]
-    two_re = turn(pass_re, 1)
-    two_im = turn(pass_im, 3)
-
     spare = 16
     shapes = [(2, 2, pulses + spare, cols)] + [(2, 2, pulses, cols)] * (nx - 1)
     focus = pl.pallas_call(
@@ -202,6 +195,12 @@
         out_specs=[VMEM] * nx,
         name="focus",
     )(lateral, vertical, echo, slant)
+    at, _ = lax.optimization_barrier((jnp.transpose(along, (0, 2, 1)), focus[0]))
+    one = turn(at, 1)
+    three = turn(at, 3)
+    pass_re, pass_im = one[0], three[1]
+    two_re = turn(pass_re, 1)
+    two_im = turn(pass_im, 3)
     focus = [focus[0]] + [turn(focus[s], s) for s in range(1, nx)]
     inside = lax.axis_index("x") < nx
     at_here, focus_here, _, _ = lax.optimization_barrier((at, focus[0], pass_re, pass_im))

time: 77.7 us -> 82.4 us (1.060)
  starting transfers between devices: 28.1 us -> 32.3 us
    ppermute x9, starting transfers between devices: 6.36 us -> 9.09 us  [swap(): return lax.ppermute(value, 'c', [(0, 1), (1, 0)])]
    ppermute x7, starting transfers between devices: 9.2 us -> 11.1 us  [turn(): return lax.ppermute(value, 'x', [(i, (i + step) % nx) for i in range(nx)])]
  transfers between devices with their start and end apart: 17 -> 17, of which waited for: 5 -> 5; matrix products, arithmetic and copies ran while one was open for 5% -> 4% of each run, Pallas kernels for 4% -> 0%
where the time goes in v8:
time: 82.4 us; the launch traced here: 82.2 us
  waiting for transfers between devices  34.6 us (42%)
  starting transfers between devices  32.3 us (39%)
  Pallas kernels  11.4 us (14%)
  other arithmetic  3.3 us (4%)
    all_to_all x1, waiting for transfers between devices, body(): image = lax.all_to_all(image, ('x', 'zh', 'c', 'y', 'zl'), 0, 0, tiled=True)  30.4 us
    all_to_all x1, starting transfers between devices, body(): image = lax.all_to_all(image, ('x', 'zh', 'c', 'y', 'zl'), 0, 0, tiled=True)  12.1 us
    ppermute x7, starting transfers between devices, turn(): return lax.ppermute(value, 'x', [(i, (i + step) % nx) for i in range(nx)])  11.1 us
    ppermute x9, starting transfers between devices, swap(): return lax.ppermute(value, 'c', [(0, 1), (1, 0)])  9.09 us
    pallas_call x1, Pallas kernels, body(): pl.pallas_call(recover_kernel, grid=(own,), out_shape=jax.ShapeDtypeStruc...  5.93 us
    ppermute x7, waiting for transfers between devices, turn(): return lax.ppermute(value, 'x', [(i, (i + step) % nx) for i in range(nx)])  2.94 us
    pallas_call x1, Pallas kernels, partial_image(): pl.pallas_call(focus_kernel, out_shape=[jax.ShapeDtypeStruct(shape, bf) f...  2.86 us
    pallas_call x1, Pallas kernels, partial_image(): pl.pallas_call(functools.partial(image_kernel, nx), out_shape=jax.ShapeDt...  2.65 us
  transfers between devices with their start and end apart: 17, of which 5 were waited for; matrix products, arithmetic and copies ran while one was open for 4% of the time, Pallas kernels for 0%

profile of v8, /device:TPU:1, one launch (start us, length us, event | category | flops | bytes accessed | tf_op | source)
XLA Modules:
  0.0 82.2 jit_solution(2920033749325067000)
XLA Ops:
  0.0 2.9 %focus.1 = (bf16[2,2,80,256]{3,2,1,0:T(8,128)(2,1)}, bf16[2,2,64,256]{3,2,1,0:T(8,128)(2,1)}, bf16[2,2,64,256]{3,2,1,0:T(8,128)(2,1)}, bf16[2,2,64,256]{3,2,1,0:T(8,128)(2,1)}) custom-call(s32[8]{0:T(128)} %lat_ref.1, s32[8]{0:T(128)} %ver_ref.1, bf16[2,8,64,512]{3,2,1,0:T(8,128)(2,1)} %echo_ref.1, bf16[2,512,256]{2,1,0:T(8,128)(2,1)} %kern_ref.1), custom_call_target="tpu_custom_call" | custom-call | tf_op jit(solution)/shard_map/focus/pallas_call | solution.py:191
  2.9 3.4 %collective-permute-start.1 = (bf16[2,64,1024]{2,1,0:T(8,128)(2,1)}, bf16[2,64,1024]{2,1,0:T(8,128)(2,1)S(1)}, u32[]{:S(2)}, u32[]{:S(2)}) collective-permute-start(bf16[2,64,1024]{2,1,0:T(8,128)(2,1)} %bitcast.11), channel_id=1, source_target_pairs={{0,192},{64,0},{128,64},{192,128},{1,193},{65,1},{129,65},{193,129... | collective-permute-start | bytes 786440 | tf_op jit(solution)/shard_map/ppermute | solution.py:184
  6.2 0.2 collective-permute-start.2
  6.4 3.7 %collective-permute-start.3 = (bf16[2,2,64,256]{3,2,1,0:T(8,128)(2,1)}, bf16[2,2,64,256]{3,2,1,0:T(8,128)(2,1)S(1)}, u32[]{:S(2)}, u32[]{:S(2)}) collective-permute-start(bf16[2,2,64,256]{3,2,1,0:T(8,128)(2,1)} %get-tuple-element.26), channel_id=1, source_target_pairs={{0,128},{64,192},{128,0},{192,64},{1,129},{65,193},{129,1},{193,65... | collective-permute-start | bytes 393224 | tf_op jit(solution)/shard_map/ppermute | solution.py:184
  10.1 2.3 %collective-permute-done.1.refs_4_ = bf16[2,64,1024]{2,1,0:T(8,128)(2,1)S(1)} collective-permute-done((bf16[2,64,1024]{2,1,0:T(8,128)(2,1)}, bf16[2,64,1024]{2,1,0:T(8,128)(2,1)S(1)}, u32[]{:S(2)}, u32[]{:S(2)}) %collective-permute-start.1) | collective-permute-done | bytes 262176 | tf_op jit(solution)/shard_map/ppermute | solution.py:184
  12.4 3.8 %collective-permute-start.6 = (bf16[64,1024]{1,0:T(8,128)(2,1)S(1)}, bf16[64,1024]{1,0:T(8,128)(2,1)S(1)}, u32[]{:S(2)}, u32[]{:S(2)}) collective-permute-start(bf16[64,1024]{1,0:T(8,128)(2,1)S(1)} %slice_bitcast_fusion), channel_id=1, source_target_pairs={{0,192},{64,0},{128,64},{192,128},{1,193},{65,1},{129,65},{193,129... | collective-permute-start | bytes 393224 | tf_op jit(solution)/shard_map/ppermute | solution.py:184
  16.3 0.1 collective-permute-start.5
  16.4 1.0 %broadcast_select_fusion.refs_0_ = bf16[2,64,1024]{2,1,0:T(8,128)(2,1)S(1)} fusion(bf16[2,64,1024]{2,1,0:T(8,128)(2,1)} %bitcast.13, pred[]{:T(512)S(6)} %lt.3), kind=kLoop, calls=%fused_computation.6 | loop fusion | flops 131072 | bytes 524289 | tf_op jit(solution)/shard_map/jit(_where)/select_n | solution.py:207
  17.3 0.9 %broadcast_select_fusion.1.refs_10_ = bf16[2,2,80,256]{3,2,1,0:T(8,128)(2,1)S(1)} fusion(bf16[2,2,80,256]{3,2,1,0:T(8,128)(2,1)} %get-tuple-element.36, pred[]{:T(512)S(6)} %lt.3), kind=kLoop, calls=%fused_computation.7 | loop fusion | flops 81920 | bytes 327681 | tf_op jit(solution)/shard_map/jit(_where)/select_n | solution.py:208
  18.3 0.6 collective-permute-done.3.refs_12_
  18.9 4.0 %collective-permute-start.13 = (bf16[2,2,64,256]{3,2,1,0:T(8,128)(2,1)S(1)}, bf16[2,2,64,256]{3,2,1,0:T(8,128)(2,1)S(1)}, u32[]{:S(2)}, u32[]{:S(2)}) collective-permute-start(bf16[2,2,64,256]{3,2,1,0:T(8,128)(2,1)S(1)} %collective-permute-done.2.refs_11_), channel_id=1, source_target_pairs={{0,8},{8,0},{1,9},{9,1},{2,10},{10,2},{3,11},{11,3},{4,12},{12,4},... | collective-permute-start | bytes 393224 | tf_op jit(solution)/shard_map/ppermute | solution.py:187
  22.9 0.1 collective-permute-start.14
  23.0 0.4 collective-permute-start.12
  23.4 0.1 collective-permute-start.15
  23.5 3.5 %collective-permute-start.7 = (bf16[2,64,1024]{2,1,0:T(8,128)(2,1)}, bf16[2,64,1024]{2,1,0:T(8,128)(2,1)S(1)}, u32[]{:S(2)}, u32[]{:S(2)}) collective-permute-start(bf16[2,64,1024]{2,1,0:T(8,128)(2,1)} %bitcast.14), channel_id=1, source_target_pairs={{0,8},{8,0},{1,9},{9,1},{2,10},{10,2},{3,11},{11,3},{4,12},{12,4},... | collective-permute-start | bytes 786440 | tf_op jit(solution)/shard_map/ppermute | solution.py:187
  27.0 0.0 collective-permute-start.8
  27.0 0.5 collective-permute-start.11
  27.5 0.1 collective-permute-start.10
  27.6 0.4 collective-permute-start.9
  28.0 1.1 %collective-permute-done.10.refs_8_ = bf16[64,1024]{1,0:T(8,128)(2,1)S(1)} collective-permute-done((bf16[64,1024]{1,0:T(8,128)(2,1)S(1)}, bf16[64,1024]{1,0:T(8,128)(2,1)S(1)}, u32[]{:S(2)}, u32[]{:S(2)}) %collective-permute-start.10) | collective-permute-done | bytes 131104 | tf_op jit(solution)/shard_map/ppermute | solution.py:187
  29.1 0.2 collective-permute-done.9.refs_7_
  29.3 2.6 %image.1 = bf16[2048,256]{1,0:T(8,128)(2,1)} custom-call(bf16[2,64,1024]{2,1,0:T(8,128)(2,1)S(1)} %broadcast_select_fusion.refs_0_, bf16[2,64,1024]{2,1,0:T(8,128)(2,1)S(1)} %collective-permute-done.refs_1_, bf16[64,1024]{1,0:T(8,128)(2,1)S(1)} %collective-permute-done.5.refs_2_, bf16[64,1024]{1,0:T(8,128)(2,1)S(1)} %collective-permute-done.6.refs_3_, ...), custom_call_target="tpu_custom_call" | custom-call | tf_op jit(solution)/shard_map/image/pallas_call | solution.py:217
  31.9 12.1 %all-to-all-start = ((bf16[256,8,256]{2,1,0:T(8,128)(2,1)}), bf16[256,8,256]{2,1,0:T(8,128)(2,1)S(1)}, u32[]{:S(2)}, u32[]{:S(2)}) async-start(bf16[256,8,256]{2,1,0:T(8,128)(2,1)} %bitcast.3), calls=%async_computation | async-start | bytes 2097152 | tf_op jit(solution)/shard_map/all_to_all | solution.py:239
  44.0 0.1 reshape.21
  44.1 0.1 copy.10
  44.2 0.1 eq.15
  44.3 0.2 select_reduce_fusion
  44.5 1.0 %fusion.1 = (f32[64,512]{0,1:T(8,128)S(1)}, f32[64,512]{0,1:T(8,128)S(1)}, f32[64,512]{0,1:T(8,128)S(1)}) fusion(f32[512]{0:T(512)S(1)} %convert_add_fusion, f32[64]{0:T(128)S(1)} %broadcast_multiply_fusion), kind=kLoop, calls=%fused_computation.10 | loop fusion | flops 65536 | bytes 395520 | tf_op jit(solution)/shard_map/neg | solution.py:244
  45.5 0.2 fusion
  45.7 0.1 copy.11.g_ref
  45.8 30.4 %all-to-all-done = bf16[256,8,256]{2,1,0:T(8,128)(2,1)S(1)} async-done(((bf16[256,8,256]{2,1,0:T(8,128)(2,1)}), bf16[256,8,256]{2,1,0:T(8,128)(2,1)S(1)}, u32[]{:S(2)}, u32[]{:S(2)}) %all-to-all-start) | async-done | bytes 1048608 | tf_op jit(solution)/shard_map/all_to_all | solution.py:239
  76.2 5.9 %recover.1 = f32[2,4,256,512]{3,2,1,0:T(8,128)} custom-call(bf16[4,4,16,8,256]{4,3,2,1,0:T(8,128)(2,1)S(1)} %bitcast.10, bf16[128,1024]{1,0:T(8,128)(2,1)S(1)} %copy.11.g_ref, bf16[1024,128]{1,0:T(8,128)(2,1)S(1)} %get-tuple-element.37.h_ref), custom_call_target="tpu_custom_call" | custom-call | tf_op jit(solution)/shard_map/recover/pallas_call | solution.py:250
  (22 shorter events, 0.1 us)
Async XLA Ops:
  2.9 41.2 %copy-start = (s32[64]{0:T(128)S(1)}, s32[64]{0:T(128)}, u32[]{:S(2)}) copy-start(s32[64]{0:T(128)} %param.12) | copy-start | bytes 772
  2.9 41.4 %copy-start.1 = (f32[64]{0:T(128)S(1)}, f32[64]{0:T(128)}, u32[]{:S(2)}) copy-start(f32[64]{0:T(128)} %param.13) | copy-start | bytes 772
  2.9 9.6 %collective-permute-start.1 = (bf16[2,64,1024]{2,1,0:T(8,128)(2,1)}, bf16[2,64,1024]{2,1,0:T(8,128)(2,1)S(1)}, u32[]{:S(2)}, u32[]{:S(2)}) collective-permute-start(bf16[2,64,1024]{2,1,0:T(8,128)(2,1)} %bitcast.11), channel_id=1, source_target_pairs={{0,192},{64,0},{128,64},{192,128},{1,193},{65,1},{129,65},{193,129... | collective-permute-start | bytes 786440 | tf_op jit(solution)/shard_map/ppermute | solution.py:184
  6.2 10.0 %collective-permute-start = (bf16[2,64,1024]{2,1,0:T(8,128)(2,1)}, bf16[2,64,1024]{2,1,0:T(8,128)(2,1)S(1)}, u32[]{:S(2)}, u32[]{:S(2)}) collective-permute-start(bf16[2,64,1024]{2,1,0:T(8,128)(2,1)} %bitcast.12), channel_id=1, source_target_pairs={{0,64},{64,128},{128,192},{192,0},{1,65},{65,129},{129,193},{193,1... | collective-permute-start | bytes 786440 | tf_op jit(solution)/shard_map/ppermute | solution.py:184
  6.2 12.0 %collective-permute-start.2 = (bf16[2,2,64,256]{3,2,1,0:T(8,128)(2,1)}, bf16[2,2,64,256]{3,2,1,0:T(8,128)(2,1)S(1)}, u32[]{:S(2)}, u32[]{:S(2)}) collective-permute-start(bf16[2,2,64,256]{3,2,1,0:T(8,128)(2,1)} %get-tuple-element.25), channel_id=1, source_target_pairs={{0,64},{64,128},{128,192},{192,0},{1,65},{65,129},{129,193},{193,1... | collective-permute-start | bytes 393224 | tf_op jit(solution)/shard_map/ppermute | solution.py:184
  6.4 12.5 %collective-permute-start.3 = (bf16[2,2,64,256]{3,2,1,0:T(8,128)(2,1)}, bf16[2,2,64,256]{3,2,1,0:T(8,128)(2,1)S(1)}, u32[]{:S(2)}, u32[]{:S(2)}) collective-permute-start(bf16[2,2,64,256]{3,2,1,0:T(8,128)(2,1)} %get-tuple-element.26), channel_id=1, source_target_pairs={{0,128},{64,192},{128,0},{192,64},{1,129},{65,193},{129,1},{193,65... | collective-permute-start | bytes 393224 | tf_op jit(solution)/shard_map/ppermute | solution.py:184
  10.1 8.8 %collective-permute-start.4 = (bf16[2,2,64,256]{3,2,1,0:T(8,128)(2,1)}, bf16[2,2,64,256]{3,2,1,0:T(8,128)(2,1)S(1)}, u32[]{:S(2)}, u32[]{:S(2)}) collective-permute-start(bf16[2,2,64,256]{3,2,1,0:T(8,128)(2,1)} %get-tuple-element.27), channel_id=1, source_target_pairs={{0,192},{64,0},{128,64},{192,128},{1,193},{65,1},{129,65},{193,129... | collective-permute-start | bytes 393224 | tf_op jit(solution)/shard_map/ppermute | solution.py:184
  12.4 10.9 %collective-permute-start.6 = (bf16[64,1024]{1,0:T(8,128)(2,1)S(1)}, bf16[64,1024]{1,0:T(8,128)(2,1)S(1)}, u32[]{:S(2)}, u32[]{:S(2)}) collective-permute-start(bf16[64,1024]{1,0:T(8,128)(2,1)S(1)} %slice_bitcast_fusion), channel_id=1, source_target_pairs={{0,192},{64,0},{128,64},{192,128},{1,193},{65,1},{129,65},{193,129... | collective-permute-start | bytes 393224 | tf_op jit(solution)/shard_map/ppermute | solution.py:184
  16.3 7.2 %collective-permute-start.5 = (bf16[64,1024]{1,0:T(8,128)(2,1)S(1)}, bf16[64,1024]{1,0:T(8,128)(2,1)S(1)}, u32[]{:S(2)}, u32[]{:S(2)}) collective-permute-start(bf16[64,1024]{1,0:T(8,128)(2,1)S(1)} %slice_bitcast_fusion.1), channel_id=1, source_target_pairs={{0,64},{64,128},{128,192},{192,0},{1,65},{65,129},{129,193},{193,1... | collective-permute-start | bytes 393224 | tf_op jit(solution)/shard_map/ppermute | solution.py:184
  18.9 8.1 %collective-permute-start.13 = (bf16[2,2,64,256]{3,2,1,0:T(8,128)(2,1)S(1)}, bf16[2,2,64,256]{3,2,1,0:T(8,128)(2,1)S(1)}, u32[]{:S(2)}, u32[]{:S(2)}) collective-permute-start(bf16[2,2,64,256]{3,2,1,0:T(8,128)(2,1)S(1)} %collective-permute-done.2.refs_11_), channel_id=1, source_target_pairs={{0,8},{8,0},{1,9},{9,1},{2,10},{10,2},{3,11},{11,3},{4,12},{12,4},... | collective-permute-start | bytes 393224 | tf_op jit(solution)/shard_map/ppermute | solution.py:187
  22.9 4.1 %collective-permute-start.14 = (bf16[2,2,64,256]{3,2,1,0:T(8,128)(2,1)S(1)}, bf16[2,2,64,256]{3,2,1,0:T(8,128)(2,1)S(1)}, u32[]{:S(2)}, u32[]{:S(2)}) collective-permute-start(bf16[2,2,64,256]{3,2,1,0:T(8,128)(2,1)S(1)} %collective-permute-done.3.refs_12_), channel_id=1, source_target_pairs={{0,8},{8,0},{1,9},{9,1},{2,10},{10,2},{3,11},{11,3},{4,12},{12,4},... | collective-permute-start | bytes 393224 | tf_op jit(solution)/shard_map/ppermute | solution.py:187
  23.0 4.6 %collective-permute-start.12 = (bf16[2,2,80,256]{3,2,1,0:T(8,128)(2,1)}, bf16[2,2,80,256]{3,2,1,0:T(8,128)(2,1)S(1)}, u32[]{:S(2)}, u32[]{:S(2)}) collective-permute-start(bf16[2,2,80,256]{3,2,1,0:T(8,128)(2,1)} %get-tuple-element.36), channel_id=1, source_target_pairs={{0,8},{8,0},{1,9},{9,1},{2,10},{10,2},{3,11},{11,3},{4,12},{12,4},... | collective-permute-start | bytes 491528 | tf_op jit(solution)/shard_map/ppermute | solution.py:187
  23.4 4.1 %collective-permute-start.15 = (bf16[2,2,64,256]{3,2,1,0:T(8,128)(2,1)S(1)}, bf16[2,2,64,256]{3,2,1,0:T(8,128)(2,1)S(1)}, u32[]{:S(2)}, u32[]{:S(2)}) collective-permute-start(bf16[2,2,64,256]{3,2,1,0:T(8,128)(2,1)S(1)} %collective-permute-done.4.refs_13_), channel_id=1, source_target_pairs={{0,8},{8,0},{1,9},{9,1},{2,10},{10,2},{3,11},{11,3},{4,12},{12,4},... | collective-permute-start | bytes 393224 | tf_op jit(solution)/shard_map/ppermute | solution.py:187
  23.5 5.8 %collective-permute-start.7 = (bf16[2,64,1024]{2,1,0:T(8,128)(2,1)}, bf16[2,64,1024]{2,1,0:T(8,128)(2,1)S(1)}, u32[]{:S(2)}, u32[]{:S(2)}) collective-permute-start(bf16[2,64,1024]{2,1,0:T(8,128)(2,1)} %bitcast.14), channel_id=1, source_target_pairs={{0,8},{8,0},{1,9},{9,1},{2,10},{10,2},{3,11},{11,3},{4,12},{12,4},... | collective-permute-start | bytes 786440 | tf_op jit(solution)/shard_map/ppermute | solution.py:187
  27.0 2.3 %collective-permute-start.8 = (bf16[2,64,1024]{2,1,0:T(8,128)(2,1)S(1)}, bf16[2,64,1024]{2,1,0:T(8,128)(2,1)S(1)}, u32[]{:S(2)}, u32[]{:S(2)}) collective-permute-start(bf16[2,64,1024]{2,1,0:T(8,128)(2,1)S(1)} %collective-permute-done.refs_1_), channel_id=1, source_target_pairs={{0,8},{8,0},{1,9},{9,1},{2,10},{10,2},{3,11},{11,3},{4,12},{12,4},... | collective-permute-start | bytes 786440 | tf_op jit(solution)/shard_map/ppermute | solution.py:187
  27.0 2.3 %collective-permute-start.11 = (bf16[2,64,1024]{2,1,0:T(8,128)(2,1)S(1)}, bf16[2,64,1024]{2,1,0:T(8,128)(2,1)S(1)}, u32[]{:S(2)}, u32[]{:S(2)}) collective-permute-start(bf16[2,64,1024]{2,1,0:T(8,128)(2,1)S(1)} %collective-permute-done.1.refs_4_), channel_id=1, source_target_pairs={{0,8},{8,0},{1,9},{9,1},{2,10},{10,2},{3,11},{11,3},{4,12},{12,4},... | collective-permute-start | bytes 786440 | tf_op jit(solution)/shard_map/ppermute | solution.py:187
  27.5 1.6 %collective-permute-start.10 = (bf16[64,1024]{1,0:T(8,128)(2,1)S(1)}, bf16[64,1024]{1,0:T(8,128)(2,1)S(1)}, u32[]{:S(2)}, u32[]{:S(2)}) collective-permute-start(bf16[64,1024]{1,0:T(8,128)(2,1)S(1)} %collective-permute-done.6.refs_3_), channel_id=1, source_target_pairs={{0,8},{8,0},{1,9},{9,1},{2,10},{10,2},{3,11},{11,3},{4,12},{12,4},... | collective-permute-start | bytes 393224 | tf_op jit(solution)/shard_map/ppermute | solution.py:187
  27.6 1.7 %collective-permute-start.9 = (bf16[64,1024]{1,0:T(8,128)(2,1)S(1)}, bf16[64,1024]{1,0:T(8,128)(2,1)S(1)}, u32[]{:S(2)}, u32[]{:S(2)}) collective-permute-start(bf16[64,1024]{1,0:T(8,128)(2,1)S(1)} %collective-permute-done.5.refs_2_), channel_id=1, source_target_pairs={{0,8},{8,0},{1,9},{9,1},{2,10},{10,2},{3,11},{11,3},{4,12},{12,4},... | collective-permute-start | bytes 393224 | tf_op jit(solution)/shard_map/ppermute | solution.py:187
  31.9 44.3 %all-to-all-start = ((bf16[256,8,256]{2,1,0:T(8,128)(2,1)}), bf16[256,8,256]{2,1,0:T(8,128)(2,1)S(1)}, u32[]{:S(2)}, u32[]{:S(2)}) async-start(bf16[256,8,256]{2,1,0:T(8,128)(2,1)} %bitcast.3), calls=%async_computation | async-start | bytes 2097152 | tf_op jit(solution)/shard_map/all_to_all | solution.py:239

commit v9 on v7

--- a/solution.py
+++ b/solution.py
@@ -252,11 +252,7 @@
         recover_kernel,
         grid=(own,),
         out_shape=jax.ShapeDtypeStruct((2, own, cols, BINS), jnp.float32),
-        in_specs=[
-            pl.BlockSpec(image.shape, lambda i: (0, 0, 0, 0, 0)),
-            pl.BlockSpec(gb.shape, lambda i: (0, 0)),
-            pl.BlockSpec(hb.shape, lambda i: (0, 0)),
-        ],
+        in_specs=[VMEM] * 3,
         out_specs=pl.BlockSpec((2, 1, cols, BINS), lambda i: (0, i, 0, 0)),
         scratch_shapes=[pltpu.VMEM((cols // 128, total * 2 * own, 128), jnp.float32)],
         compiler_params=pltpu.CompilerParams(vmem_limit_bytes=40 << 20),

time: 77.7 us -> 77.7 us (level)
  no operation moved by 1% of the time
where the time goes in v9:
time: 77.7 us; the launch traced here: 77.5 us
  waiting for transfers between devices  34.2 us (44%)
  starting transfers between devices  28.1 us (36%)
  Pallas kernels  11.4 us (15%)
  other arithmetic  3.3 us (4%)
    all_to_all x1, waiting for transfers between devices, body(): image = lax.all_to_all(image, ('x', 'zh', 'c', 'y', 'zl'), 0, 0, tiled=True)  30.4 us
    all_to_all x1, starting transfers between devices, body(): image = lax.all_to_all(image, ('x', 'zh', 'c', 'y', 'zl'), 0, 0, tiled=True)  12.5 us
    ppermute x7, starting transfers between devices, turn(): return lax.ppermute(value, 'x', [(i, (i + step) % nx) for i in range(nx)])  9.2 us
    ppermute x9, starting transfers between devices, swap(): return lax.ppermute(value, 'c', [(0, 1), (1, 0)])  6.36 us
    pallas_call x1, Pallas kernels, body(): pl.pallas_call(recover_kernel, grid=(own,), out_shape=jax.ShapeDtypeStruc...  5.94 us
    pallas_call x1, Pallas kernels, partial_image(): pl.pallas_call(focus_kernel, out_shape=[jax.ShapeDtypeStruct(shape, bf) f...  2.86 us
    pallas_call x1, Pallas kernels, partial_image(): pl.pallas_call(functools.partial(image_kernel, nx), out_shape=jax.ShapeDt...  2.64 us
    ppermute x7, waiting for transfers between devices, turn(): return lax.ppermute(value, 'x', [(i, (i + step) % nx) for i in range(nx)])  2.51 us
  transfers between devices with their start and end apart: 17, of which 5 were waited for; matrix products, arithmetic and copies ran while one was open for 5% of the time, Pallas kernels for 4%

profile of v9, /device:TPU:1, one launch (start us, length us, event | category | flops | bytes accessed | tf_op | source)
XLA Modules:
  0.0 77.5 jit_solution(5110012201404588107)
XLA Ops:
  0.0 3.3 %collective-permute-start.1 = (bf16[2,64,1024]{2,1,0:T(8,128)(2,1)}, bf16[2,64,1024]{2,1,0:T(8,128)(2,1)S(1)}, u32[]{:S(2)}, u32[]{:S(2)}) collective-permute-start(bf16[2,64,1024]{2,1,0:T(8,128)(2,1)} %bitcast.11), channel_id=1, source_target_pairs={{0,192},{64,0},{128,64},{192,128},{1,193},{65,1},{129,65},{193,129... | collective-permute-start | bytes 786440 | tf_op jit(solution)/shard_map/ppermute | solution.py:184
  3.3 2.9 %focus.1 = (bf16[2,2,80,256]{3,2,1,0:T(8,128)(2,1)}, bf16[2,2,64,256]{3,2,1,0:T(8,128)(2,1)}, bf16[2,2,64,256]{3,2,1,0:T(8,128)(2,1)}, bf16[2,2,64,256]{3,2,1,0:T(8,128)(2,1)}) custom-call(s32[8]{0:T(128)} %lat_ref.1, s32[8]{0:T(128)} %ver_ref.1, bf16[2,8,64,512]{3,2,1,0:T(8,128)(2,1)} %echo_ref.1, bf16[2,512,256]{2,1,0:T(8,128)(2,1)} %kern_ref.1), custom_call_target="tpu_custom_call" | custom-call | tf_op jit(solution)/shard_map/focus/pallas_call | solution.py:198
  6.2 0.3 collective-permute-start.2
  6.4 3.7 %collective-permute-start.3 = (bf16[2,2,64,256]{3,2,1,0:T(8,128)(2,1)}, bf16[2,2,64,256]{3,2,1,0:T(8,128)(2,1)S(1)}, u32[]{:S(2)}, u32[]{:S(2)}) collective-permute-start(bf16[2,2,64,256]{3,2,1,0:T(8,128)(2,1)} %get-tuple-element.24), channel_id=1, source_target_pairs={{0,128},{64,192},{128,0},{192,64},{1,129},{65,193},{129,1},{193,65... | collective-permute-start | bytes 393224 | tf_op jit(solution)/shard_map/ppermute | solution.py:184
  10.1 1.9 %collective-permute-start.6 = (bf16[64,1024]{1,0:T(8,128)(2,1)S(1)}, bf16[64,1024]{1,0:T(8,128)(2,1)S(1)}, u32[]{:S(2)}, u32[]{:S(2)}) collective-permute-start(bf16[64,1024]{1,0:T(8,128)(2,1)S(1)} %slice_bitcast_fusion), channel_id=1, source_target_pairs={{0,192},{64,0},{128,64},{192,128},{1,193},{65,1},{129,65},{193,129... | collective-permute-start | bytes 393224 | tf_op jit(solution)/shard_map/ppermute | solution.py:184
  12.0 0.1 collective-permute-start.5
  12.1 1.0 %broadcast_select_fusion.refs_0_ = bf16[2,64,1024]{2,1,0:T(8,128)(2,1)S(1)} fusion(bf16[2,64,1024]{2,1,0:T(8,128)(2,1)} %bitcast.13, pred[]{:T(512)S(6)} %lt.3), kind=kLoop, calls=%fused_computation.6 | loop fusion | flops 131072 | bytes 524289 | tf_op jit(solution)/shard_map/jit(_where)/select_n | solution.py:208
  13.1 0.9 %broadcast_select_fusion.1.refs_10_ = bf16[2,2,80,256]{3,2,1,0:T(8,128)(2,1)S(1)} fusion(bf16[2,2,80,256]{3,2,1,0:T(8,128)(2,1)} %get-tuple-element.34, pred[]{:T(512)S(6)} %lt.3), kind=kLoop, calls=%fused_computation.7 | loop fusion | flops 81920 | bytes 327681 | tf_op jit(solution)/shard_map/jit(_where)/select_n | solution.py:209
  14.0 1.0 %collective-permute-done.2.refs_11_ = bf16[2,2,64,256]{3,2,1,0:T(8,128)(2,1)S(1)} collective-permute-done((bf16[2,2,64,256]{3,2,1,0:T(8,128)(2,1)}, bf16[2,2,64,256]{3,2,1,0:T(8,128)(2,1)S(1)}, u32[]{:S(2)}, u32[]{:S(2)}) %collective-permute-start.2) | collective-permute-done | bytes 131104 | tf_op jit(solution)/shard_map/ppermute | solution.py:184
  15.1 1.5 %collective-permute-done.3.refs_12_ = bf16[2,2,64,256]{3,2,1,0:T(8,128)(2,1)S(1)} collective-permute-done((bf16[2,2,64,256]{3,2,1,0:T(8,128)(2,1)}, bf16[2,2,64,256]{3,2,1,0:T(8,128)(2,1)S(1)}, u32[]{:S(2)}, u32[]{:S(2)}) %collective-permute-start.3) | collective-permute-done | bytes 131104 | tf_op jit(solution)/shard_map/ppermute | solution.py:184
  16.5 3.5 %collective-permute-start.13 = (bf16[2,2,64,256]{3,2,1,0:T(8,128)(2,1)S(1)}, bf16[2,2,64,256]{3,2,1,0:T(8,128)(2,1)S(1)}, u32[]{:S(2)}, u32[]{:S(2)}) collective-permute-start(bf16[2,2,64,256]{3,2,1,0:T(8,128)(2,1)S(1)} %collective-permute-done.2.refs_11_), channel_id=1, source_target_pairs={{0,8},{8,0},{1,9},{9,1},{2,10},{10,2},{3,11},{11,3},{4,12},{12,4},... | collective-permute-start | bytes 393224 | tf_op jit(solution)/shard_map/ppermute | solution.py:187
  20.0 0.1 collective-permute-start.14
  20.1 0.4 collective-permute-start.12
  20.5 0.1 collective-permute-start.15
  20.6 1.3 %collective-permute-start.7 = (bf16[2,64,1024]{2,1,0:T(8,128)(2,1)}, bf16[2,64,1024]{2,1,0:T(8,128)(2,1)S(1)}, u32[]{:S(2)}, u32[]{:S(2)}) collective-permute-start(bf16[2,64,1024]{2,1,0:T(8,128)(2,1)} %bitcast.14), channel_id=1, source_target_pairs={{0,8},{8,0},{1,9},{9,1},{2,10},{10,2},{3,11},{11,3},{4,12},{12,4},... | collective-permute-start | bytes 786440 | tf_op jit(solution)/shard_map/ppermute | solution.py:187
  21.9 0.0 collective-permute-start.8
  21.9 0.5 collective-permute-start.11
  22.4 0.1 collective-permute-start.10
  22.5 0.4 collective-permute-start.9
  22.9 1.1 %collective-permute-done.10.refs_8_ = bf16[64,1024]{1,0:T(8,128)(2,1)S(1)} collective-permute-done((bf16[64,1024]{1,0:T(8,128)(2,1)S(1)}, bf16[64,1024]{1,0:T(8,128)(2,1)S(1)}, u32[]{:S(2)}, u32[]{:S(2)}) %collective-permute-start.10) | collective-permute-done | bytes 131104 | tf_op jit(solution)/shard_map/ppermute | solution.py:187
  24.0 0.2 collective-permute-done.9.refs_7_
  24.2 2.6 %image.1 = bf16[2048,256]{1,0:T(8,128)(2,1)} custom-call(bf16[2,64,1024]{2,1,0:T(8,128)(2,1)S(1)} %broadcast_select_fusion.refs_0_, bf16[2,64,1024]{2,1,0:T(8,128)(2,1)S(1)} %collective-permute-done.refs_1_, bf16[64,1024]{1,0:T(8,128)(2,1)S(1)} %collective-permute-done.5.refs_2_, bf16[64,1024]{1,0:T(8,128)(2,1)S(1)} %collective-permute-done.6.refs_3_, ...), custom_call_target="tpu_custom_call" | custom-call | tf_op jit(solution)/shard_map/image/pallas_call | solution.py:218
  26.8 12.5 %all-to-all-start = ((bf16[256,8,256]{2,1,0:T(8,128)(2,1)}), bf16[256,8,256]{2,1,0:T(8,128)(2,1)S(1)}, u32[]{:S(2)}, u32[]{:S(2)}) async-start(bf16[256,8,256]{2,1,0:T(8,128)(2,1)} %bitcast.3), calls=%async_computation | async-start | bytes 2097152 | tf_op jit(solution)/shard_map/all_to_all | solution.py:240
  39.3 0.1 reshape.21
  39.4 0.1 copy.10
  39.5 0.1 eq.15
  39.6 0.2 select_reduce_fusion
  39.8 1.0 %fusion.1 = (f32[64,512]{0,1:T(8,128)S(1)}, f32[64,512]{0,1:T(8,128)S(1)}, f32[64,512]{0,1:T(8,128)S(1)}) fusion(f32[512]{0:T(512)S(1)} %convert_add_fusion, f32[64]{0:T(128)S(1)} %broadcast_multiply_fusion), kind=kLoop, calls=%fused_computation.10 | loop fusion | flops 65536 | bytes 395520 | tf_op jit(solution)/shard_map/neg | solution.py:245
  40.8 0.2 fusion
  41.0 0.1 copy.11.g_ref
  41.2 30.4 %all-to-all-done = bf16[256,8,256]{2,1,0:T(8,128)(2,1)S(1)} async-done(((bf16[256,8,256]{2,1,0:T(8,128)(2,1)}), bf16[256,8,256]{2,1,0:T(8,128)(2,1)S(1)}, u32[]{:S(2)}, u32[]{:S(2)}) %all-to-all-start) | async-done | bytes 1048608 | tf_op jit(solution)/shard_map/all_to_all | solution.py:240
  71.5 5.9 %recover.1 = f32[2,4,256,512]{3,2,1,0:T(8,128)} custom-call(bf16[4,4,16,8,256]{4,3,2,1,0:T(8,128)(2,1)S(1)} %bitcast.10, bf16[128,1024]{1,0:T(8,128)(2,1)S(1)} %copy.11.g_ref, bf16[1024,128]{1,0:T(8,128)(2,1)S(1)} %get-tuple-element.35.h_ref), custom_call_target="tpu_custom_call" | custom-call | tf_op jit(solution)/shard_map/recover/pallas_call | solution.py:251
  (22 shorter events, 0.1 us)
Async XLA Ops:
  0.0 10.1 %collective-permute-start.1 = (bf16[2,64,1024]{2,1,0:T(8,128)(2,1)}, bf16[2,64,1024]{2,1,0:T(8,128)(2,1)S(1)}, u32[]{:S(2)}, u32[]{:S(2)}) collective-permute-start(bf16[2,64,1024]{2,1,0:T(8,128)(2,1)} %bitcast.11), channel_id=1, source_target_pairs={{0,192},{64,0},{128,64},{192,128},{1,193},{65,1},{129,65},{193,129... | collective-permute-start | bytes 786440 | tf_op jit(solution)/shard_map/ppermute | solution.py:184
  3.3 8.7 %collective-permute-start = (bf16[2,64,1024]{2,1,0:T(8,128)(2,1)}, bf16[2,64,1024]{2,1,0:T(8,128)(2,1)S(1)}, u32[]{:S(2)}, u32[]{:S(2)}) collective-permute-start(bf16[2,64,1024]{2,1,0:T(8,128)(2,1)} %bitcast.12), channel_id=1, source_target_pairs={{0,64},{64,128},{128,192},{192,0},{1,65},{65,129},{129,193},{193,1... | collective-permute-start | bytes 786440 | tf_op jit(solution)/shard_map/ppermute | solution.py:184
  6.2 33.2 %copy-start = (s32[64]{0:T(128)S(1)}, s32[64]{0:T(128)}, u32[]{:S(2)}) copy-start(s32[64]{0:T(128)} %param.12) | copy-start | bytes 772
  6.2 33.4 %copy-start.1 = (f32[64]{0:T(128)S(1)}, f32[64]{0:T(128)}, u32[]{:S(2)}) copy-start(f32[64]{0:T(128)} %param.13) | copy-start | bytes 772
  6.2 8.9 %collective-permute-start.2 = (bf16[2,2,64,256]{3,2,1,0:T(8,128)(2,1)}, bf16[2,2,64,256]{3,2,1,0:T(8,128)(2,1)S(1)}, u32[]{:S(2)}, u32[]{:S(2)}) collective-permute-start(bf16[2,2,64,256]{3,2,1,0:T(8,128)(2,1)} %get-tuple-element.23), channel_id=1, source_target_pairs={{0,64},{64,128},{128,192},{192,0},{1,65},{65,129},{129,193},{193,1... | collective-permute-start | bytes 393224 | tf_op jit(solution)/shard_map/ppermute | solution.py:184
  6.4 10.1 %collective-permute-start.3 = (bf16[2,2,64,256]{3,2,1,0:T(8,128)(2,1)}, bf16[2,2,64,256]{3,2,1,0:T(8,128)(2,1)S(1)}, u32[]{:S(2)}, u32[]{:S(2)}) collective-permute-start(bf16[2,2,64,256]{3,2,1,0:T(8,128)(2,1)} %get-tuple-element.24), channel_id=1, source_target_pairs={{0,128},{64,192},{128,0},{192,64},{1,129},{65,193},{129,1},{193,65... | collective-permute-start | bytes 393224 | tf_op jit(solution)/shard_map/ppermute | solution.py:184
  10.1 6.4 %collective-permute-start.4 = (bf16[2,2,64,256]{3,2,1,0:T(8,128)(2,1)}, bf16[2,2,64,256]{3,2,1,0:T(8,128)(2,1)S(1)}, u32[]{:S(2)}, u32[]{:S(2)}) collective-permute-start(bf16[2,2,64,256]{3,2,1,0:T(8,128)(2,1)} %get-tuple-element.25), channel_id=1, source_target_pairs={{0,192},{64,0},{128,64},{192,128},{1,193},{65,1},{129,65},{193,129... | collective-permute-start | bytes 393224 | tf_op jit(solution)/shard_map/ppermute | solution.py:184
  10.1 10.4 %collective-permute-start.6 = (bf16[64,1024]{1,0:T(8,128)(2,1)S(1)}, bf16[64,1024]{1,0:T(8,128)(2,1)S(1)}, u32[]{:S(2)}, u32[]{:S(2)}) collective-permute-start(bf16[64,1024]{1,0:T(8,128)(2,1)S(1)} %slice_bitcast_fusion), channel_id=1, source_target_pairs={{0,192},{64,0},{128,64},{192,128},{1,193},{65,1},{129,65},{193,129... | collective-permute-start | bytes 393224 | tf_op jit(solution)/shard_map/ppermute | solution.py:184
  12.0 8.6 %collective-permute-start.5 = (bf16[64,1024]{1,0:T(8,128)(2,1)S(1)}, bf16[64,1024]{1,0:T(8,128)(2,1)S(1)}, u32[]{:S(2)}, u32[]{:S(2)}) collective-permute-start(bf16[64,1024]{1,0:T(8,128)(2,1)S(1)} %slice_bitcast_fusion.1), channel_id=1, source_target_pairs={{0,64},{64,128},{128,192},{192,0},{1,65},{65,129},{129,193},{193,1... | collective-permute-start | bytes 393224 | tf_op jit(solution)/shard_map/ppermute | solution.py:184
  16.5 5.4 %collective-permute-start.13 = (bf16[2,2,64,256]{3,2,1,0:T(8,128)(2,1)S(1)}, bf16[2,2,64,256]{3,2,1,0:T(8,128)(2,1)S(1)}, u32[]{:S(2)}, u32[]{:S(2)}) collective-permute-start(bf16[2,2,64,256]{3,2,1,0:T(8,128)(2,1)S(1)} %collective-permute-done.2.refs_11_), channel_id=1, source_target_pairs={{0,8},{8,0},{1,9},{9,1},{2,10},{10,2},{3,11},{11,3},{4,12},{12,4},... | collective-permute-start | bytes 393224 | tf_op jit(solution)/shard_map/ppermute | solution.py:187
  20.0 1.9 %collective-permute-start.14 = (bf16[2,2,64,256]{3,2,1,0:T(8,128)(2,1)S(1)}, bf16[2,2,64,256]{3,2,1,0:T(8,128)(2,1)S(1)}, u32[]{:S(2)}, u32[]{:S(2)}) collective-permute-start(bf16[2,2,64,256]{3,2,1,0:T(8,128)(2,1)S(1)} %collective-permute-done.3.refs_12_), channel_id=1, source_target_pairs={{0,8},{8,0},{1,9},{9,1},{2,10},{10,2},{3,11},{11,3},{4,12},{12,4},... | collective-permute-start | bytes 393224 | tf_op jit(solution)/shard_map/ppermute | solution.py:187
  20.1 2.4 %collective-permute-start.12 = (bf16[2,2,80,256]{3,2,1,0:T(8,128)(2,1)}, bf16[2,2,80,256]{3,2,1,0:T(8,128)(2,1)S(1)}, u32[]{:S(2)}, u32[]{:S(2)}) collective-permute-start(bf16[2,2,80,256]{3,2,1,0:T(8,128)(2,1)} %get-tuple-element.34), channel_id=1, source_target_pairs={{0,8},{8,0},{1,9},{9,1},{2,10},{10,2},{3,11},{11,3},{4,12},{12,4},... | collective-permute-start | bytes 491528 | tf_op jit(solution)/shard_map/ppermute | solution.py:187
  20.5 1.9 %collective-permute-start.15 = (bf16[2,2,64,256]{3,2,1,0:T(8,128)(2,1)S(1)}, bf16[2,2,64,256]{3,2,1,0:T(8,128)(2,1)S(1)}, u32[]{:S(2)}, u32[]{:S(2)}) collective-permute-start(bf16[2,2,64,256]{3,2,1,0:T(8,128)(2,1)S(1)} %collective-permute-done.4.refs_13_), channel_id=1, source_target_pairs={{0,8},{8,0},{1,9},{9,1},{2,10},{10,2},{3,11},{11,3},{4,12},{12,4},... | collective-permute-start | bytes 393224 | tf_op jit(solution)/shard_map/ppermute | solution.py:187
  20.6 3.5 %collective-permute-start.7 = (bf16[2,64,1024]{2,1,0:T(8,128)(2,1)}, bf16[2,64,1024]{2,1,0:T(8,128)(2,1)S(1)}, u32[]{:S(2)}, u32[]{:S(2)}) collective-permute-start(bf16[2,64,1024]{2,1,0:T(8,128)(2,1)} %bitcast.14), channel_id=1, source_target_pairs={{0,8},{8,0},{1,9},{9,1},{2,10},{10,2},{3,11},{11,3},{4,12},{12,4},... | collective-permute-start | bytes 786440 | tf_op jit(solution)/shard_map/ppermute | solution.py:187
  21.9 2.3 %collective-permute-start.8 = (bf16[2,64,1024]{2,1,0:T(8,128)(2,1)S(1)}, bf16[2,64,1024]{2,1,0:T(8,128)(2,1)S(1)}, u32[]{:S(2)}, u32[]{:S(2)}) collective-permute-start(bf16[2,64,1024]{2,1,0:T(8,128)(2,1)S(1)} %collective-permute-done.refs_1_), channel_id=1, source_target_pairs={{0,8},{8,0},{1,9},{9,1},{2,10},{10,2},{3,11},{11,3},{4,12},{12,4},... | collective-permute-start | bytes 786440 | tf_op jit(solution)/shard_map/ppermute | solution.py:187
  21.9 2.3 %collective-permute-start.11 = (bf16[2,64,1024]{2,1,0:T(8,128)(2,1)S(1)}, bf16[2,64,1024]{2,1,0:T(8,128)(2,1)S(1)}, u32[]{:S(2)}, u32[]{:S(2)}) collective-permute-start(bf16[2,64,1024]{2,1,0:T(8,128)(2,1)S(1)} %collective-permute-done.1.refs_4_), channel_id=1, source_target_pairs={{0,8},{8,0},{1,9},{9,1},{2,10},{10,2},{3,11},{11,3},{4,12},{12,4},... | collective-permute-start | bytes 786440 | tf_op jit(solution)/shard_map/ppermute | solution.py:187
  22.4 1.6 %collective-permute-start.10 = (bf16[64,1024]{1,0:T(8,128)(2,1)S(1)}, bf16[64,1024]{1,0:T(8,128)(2,1)S(1)}, u32[]{:S(2)}, u32[]{:S(2)}) collective-permute-start(bf16[64,1024]{1,0:T(8,128)(2,1)S(1)} %collective-permute-done.6.refs_3_), channel_id=1, source_target_pairs={{0,8},{8,0},{1,9},{9,1},{2,10},{10,2},{3,11},{11,3},{4,12},{12,4},... | collective-permute-start | bytes 393224 | tf_op jit(solution)/shard_map/ppermute | solution.py:187
  22.5 1.7 %collective-permute-start.9 = (bf16[64,1024]{1,0:T(8,128)(2,1)S(1)}, bf16[64,1024]{1,0:T(8,128)(2,1)S(1)}, u32[]{:S(2)}, u32[]{:S(2)}) collective-permute-start(bf16[64,1024]{1,0:T(8,128)(2,1)S(1)} %collective-permute-done.5.refs_2_), channel_id=1, source_target_pairs={{0,8},{8,0},{1,9},{9,1},{2,10},{10,2},{3,11},{11,3},{4,12},{12,4},... | collective-permute-start | bytes 393224 | tf_op jit(solution)/shard_map/ppermute | solution.py:187
  26.8 44.7 %all-to-all-start = ((bf16[256,8,256]{2,1,0:T(8,128)(2,1)}), bf16[256,8,256]{2,1,0:T(8,128)(2,1)S(1)}, u32[]{:S(2)}, u32[]{:S(2)}) async-start(bf16[256,8,256]{2,1,0:T(8,128)(2,1)} %bitcast.3), calls=%async_computation | async-start | bytes 2097152 | tf_op jit(solution)/shard_map/all_to_all | solution.py:240

commit v10 on v7

--- a/solution.py
+++ b/solution.py
@@ -202,7 +202,10 @@
         out_specs=[VMEM] * nx,
         name="focus",
     )(lateral, vertical, echo, slant)
-    focus = [focus[0]] + [turn(focus[s], s) for s in range(1, nx)]
+    moved = {s: turn(focus[s], s) for s in (1, nx - 1)}
+    far_piece, _ = lax.optimization_barrier((focus[2], pass_re))
+    moved[2] = turn(far_piece, 2)
+    focus = [focus[0]] + [moved[s] for s in range(1, nx)]
     inside = lax.axis_index("x") < nx
     at_here, focus_here, _, _ = lax.optimization_barrier((at, focus[0], pass_re, pass_im))
     own = jnp.where(inside, at_here, jnp.zeros_like(at))

time: 77.7 us -> 80.4 us (1.035)
  starting transfers between devices: 28.1 us -> 31.7 us
  waiting for transfers between devices: 34.2 us -> 33.3 us
    ppermute x9, starting transfers between devices: 6.36 us -> 8.87 us  [swap(): return lax.ppermute(value, 'c', [(0, 1), (1, 0)])]
    ppermute x7, waiting for transfers between devices: 2.51 us -> 1.11 us  [turn(): return lax.ppermute(value, 'x', [(i, (i + step) % nx) for i in range(nx)])]
    ppermute x7, starting transfers between devices: 9.2 us -> 10.4 us  [turn(): return lax.ppermute(value, 'x', [(i, (i + step) % nx) for i in range(nx)])]
  transfers between devices with their start and end apart: 17 -> 17, of which waited for: 5 -> 6; matrix products, arithmetic and copies ran while one was open for 5% -> 5% of each run, Pallas kernels for 4% -> 4%
where the time goes in v10:
time: 80.4 us; the launch traced here: 80.2 us
  waiting for transfers between devices  33.3 us (41%)
  starting transfers between devices  31.7 us (39%)
  Pallas kernels  11.4 us (14%)
  other arithmetic  3.29 us (4%)
    all_to_all x1, waiting for transfers between devices, body(): image = lax.all_to_all(image, ('x', 'zh', 'c', 'y', 'zl'), 0, 0, tiled=True)  30.4 us
    all_to_all x1, starting transfers between devices, body(): image = lax.all_to_all(image, ('x', 'zh', 'c', 'y', 'zl'), 0, 0, tiled=True)  12.4 us
    ppermute x7, starting transfers between devices, turn(): return lax.ppermute(value, 'x', [(i, (i + step) % nx) for i in range(nx)])  10.4 us
    ppermute x9, starting transfers between devices, swap(): return lax.ppermute(value, 'c', [(0, 1), (1, 0)])  8.87 us
    pallas_call x1, Pallas kernels, body(): pl.pallas_call(recover_kernel, grid=(own,), out_shape=jax.ShapeDtypeStruc...  5.93 us
    pallas_call x1, Pallas kernels, partial_image(): pl.pallas_call(focus_kernel, out_shape=[jax.ShapeDtypeStruct(shape, bf) f...  2.86 us
    pallas_call x1, Pallas kernels, partial_image(): pl.pallas_call(functools.partial(image_kernel, nx), out_shape=jax.ShapeDt...  2.65 us
    ppermute x9, waiting for transfers between devices, swap(): return lax.ppermute(value, 'c', [(0, 1), (1, 0)])  1.8 us
  transfers between devices with their start and end apart: 17, of which 6 were waited for; matrix products, arithmetic and copies ran while one was open for 5% of the time, Pallas kernels for 4%

profile of v10, /device:TPU:1, one launch (start us, length us, event | category | flops | bytes accessed | tf_op | source)
XLA Modules:
  0.0 80.2 jit_solution(3877829688687698937)
XLA Ops:
  0.0 3.3 %collective-permute-start.1 = (bf16[2,64,1024]{2,1,0:T(8,128)(2,1)}, bf16[2,64,1024]{2,1,0:T(8,128)(2,1)S(1)}, u32[]{:S(2)}, u32[]{:S(2)}) collective-permute-start(bf16[2,64,1024]{2,1,0:T(8,128)(2,1)} %bitcast.11), channel_id=1, source_target_pairs={{0,192},{64,0},{128,64},{192,128},{1,193},{65,1},{129,65},{193,129... | collective-permute-start | bytes 786440 | tf_op jit(solution)/shard_map/ppermute | solution.py:184
  3.3 2.9 %focus.1 = (bf16[2,2,80,256]{3,2,1,0:T(8,128)(2,1)}, bf16[2,2,64,256]{3,2,1,0:T(8,128)(2,1)}, bf16[2,2,64,256]{3,2,1,0:T(8,128)(2,1)}, bf16[2,2,64,256]{3,2,1,0:T(8,128)(2,1)}) custom-call(s32[8]{0:T(128)} %lat_ref.1, s32[8]{0:T(128)} %ver_ref.1, bf16[2,8,64,512]{3,2,1,0:T(8,128)(2,1)} %echo_ref.1, bf16[2,512,256]{2,1,0:T(8,128)(2,1)} %kern_ref.1), custom_call_target="tpu_custom_call" | custom-call | tf_op jit(solution)/shard_map/focus/pallas_call | solution.py:198
  6.2 0.3 collective-permute-start.2
  6.4 2.6 %collective-permute-start.4 = (bf16[2,2,64,256]{3,2,1,0:T(8,128)(2,1)}, bf16[2,2,64,256]{3,2,1,0:T(8,128)(2,1)S(1)}, u32[]{:S(2)}, u32[]{:S(2)}) collective-permute-start(bf16[2,2,64,256]{3,2,1,0:T(8,128)(2,1)} %get-tuple-element.27), channel_id=1, source_target_pairs={{0,192},{64,0},{128,64},{192,128},{1,193},{65,1},{129,65},{193,129... | collective-permute-start | bytes 393224 | tf_op jit(solution)/shard_map/ppermute | solution.py:184
  9.0 3.0 %collective-permute-start.6 = (bf16[64,1024]{1,0:T(8,128)(2,1)S(1)}, bf16[64,1024]{1,0:T(8,128)(2,1)S(1)}, u32[]{:S(2)}, u32[]{:S(2)}) collective-permute-start(bf16[64,1024]{1,0:T(8,128)(2,1)S(1)} %slice_bitcast_fusion), channel_id=1, source_target_pairs={{0,192},{64,0},{128,64},{192,128},{1,193},{65,1},{129,65},{193,129... | collective-permute-start | bytes 393224 | tf_op jit(solution)/shard_map/ppermute | solution.py:184
  12.0 0.1 collective-permute-start.5
  12.1 1.2 %collective-permute-start.3 = (bf16[2,2,64,256]{3,2,1,0:T(8,128)(2,1)}, bf16[2,2,64,256]{3,2,1,0:T(8,128)(2,1)S(1)}, u32[]{:S(2)}, u32[]{:S(2)}) collective-permute-start(bf16[2,2,64,256]{3,2,1,0:T(8,128)(2,1)} %get-tuple-element.26), channel_id=1, source_target_pairs={{0,128},{64,192},{128,0},{192,64},{1,129},{65,193},{129,1},{193,65... | collective-permute-start | bytes 393224 | tf_op jit(solution)/shard_map/ppermute | solution.py:184
  13.3 1.0 %broadcast_select_fusion.refs_0_ = bf16[2,64,1024]{2,1,0:T(8,128)(2,1)S(1)} fusion(bf16[2,64,1024]{2,1,0:T(8,128)(2,1)} %bitcast.13, pred[]{:T(512)S(6)} %lt.3), kind=kLoop, calls=%fused_computation.6 | loop fusion | flops 131072 | bytes 524289 | tf_op jit(solution)/shard_map/jit(_where)/select_n | solution.py:211
  14.3 1.0 %collective-permute-done.6.refs_3_ = bf16[64,1024]{1,0:T(8,128)(2,1)S(1)} collective-permute-done((bf16[64,1024]{1,0:T(8,128)(2,1)S(1)}, bf16[64,1024]{1,0:T(8,128)(2,1)S(1)}, u32[]{:S(2)}, u32[]{:S(2)}) %collective-permute-start.6) | collective-permute-done | bytes 131104 | tf_op jit(solution)/shard_map/ppermute | solution.py:184
  15.3 3.1 %collective-permute-start.10 = (bf16[64,1024]{1,0:T(8,128)(2,1)S(1)}, bf16[64,1024]{1,0:T(8,128)(2,1)S(1)}, u32[]{:S(2)}, u32[]{:S(2)}) collective-permute-start(bf16[64,1024]{1,0:T(8,128)(2,1)S(1)} %collective-permute-done.6.refs_3_), channel_id=1, source_target_pairs={{0,8},{8,0},{1,9},{9,1},{2,10},{10,2},{3,11},{11,3},{4,12},{12,4},... | collective-permute-start | bytes 393224 | tf_op jit(solution)/shard_map/ppermute | solution.py:187
  18.4 4.1 %collective-permute-start.9 = (bf16[64,1024]{1,0:T(8,128)(2,1)S(1)}, bf16[64,1024]{1,0:T(8,128)(2,1)S(1)}, u32[]{:S(2)}, u32[]{:S(2)}) collective-permute-start(bf16[64,1024]{1,0:T(8,128)(2,1)S(1)} %collective-permute-done.5.refs_2_), channel_id=1, source_target_pairs={{0,8},{8,0},{1,9},{9,1},{2,10},{10,2},{3,11},{11,3},{4,12},{12,4},... | collective-permute-start | bytes 393224 | tf_op jit(solution)/shard_map/ppermute | solution.py:187
  22.5 0.9 %broadcast_select_fusion.1.refs_10_ = bf16[2,2,80,256]{3,2,1,0:T(8,128)(2,1)S(1)} fusion(bf16[2,2,80,256]{3,2,1,0:T(8,128)(2,1)} %get-tuple-element.36, pred[]{:T(512)S(6)} %lt.3), kind=kLoop, calls=%fused_computation.7 | loop fusion | flops 81920 | bytes 327681 | tf_op jit(solution)/shard_map/jit(_where)/select_n | solution.py:212
  23.5 0.1 collective-permute-start.13
  23.6 0.5 collective-permute-start.14
  24.1 0.1 collective-permute-start.7
  24.2 0.4 collective-permute-start.8
  24.6 0.1 collective-permute-start.11
  24.7 0.2 collective-permute-done.13.refs_15_
  24.9 0.2 collective-permute-start.12
  25.1 0.3 collective-permute-start.15
  25.4 1.3 %collective-permute-done.15.refs_17_ = bf16[2,2,64,256]{3,2,1,0:T(8,128)(2,1)S(1)} collective-permute-done((bf16[2,2,64,256]{3,2,1,0:T(8,128)(2,1)S(1)}, bf16[2,2,64,256]{3,2,1,0:T(8,128)(2,1)S(1)}, u32[]{:S(2)}, u32[]{:S(2)}) %collective-permute-start.15) | collective-permute-done | bytes 131104 | tf_op jit(solution)/shard_map/ppermute | solution.py:187
  26.8 0.3 collective-permute-done.12.refs_14_
  27.0 2.6 %image.1 = bf16[2048,256]{1,0:T(8,128)(2,1)} custom-call(bf16[2,64,1024]{2,1,0:T(8,128)(2,1)S(1)} %broadcast_select_fusion.refs_0_, bf16[2,64,1024]{2,1,0:T(8,128)(2,1)S(1)} %collective-permute-done.refs_1_, bf16[64,1024]{1,0:T(8,128)(2,1)S(1)} %collective-permute-done.5.refs_2_, bf16[64,1024]{1,0:T(8,128)(2,1)S(1)} %collective-permute-done.6.refs_3_, ...), custom_call_target="tpu_custom_call" | custom-call | tf_op jit(solution)/shard_map/image/pallas_call | solution.py:221
  29.7 12.4 %all-to-all-start = ((bf16[256,8,256]{2,1,0:T(8,128)(2,1)}), bf16[256,8,256]{2,1,0:T(8,128)(2,1)S(1)}, u32[]{:S(2)}, u32[]{:S(2)}) async-start(bf16[256,8,256]{2,1,0:T(8,128)(2,1)} %bitcast.3), calls=%async_computation | async-start | bytes 2097152 | tf_op jit(solution)/shard_map/all_to_all | solution.py:243
  42.1 0.1 reshape.21
  42.3 0.1 eq.15
  42.4 0.2 select_reduce_fusion
  42.6 1.0 %fusion.1 = (f32[64,512]{0,1:T(8,128)S(1)}, f32[64,512]{0,1:T(8,128)S(1)}, f32[64,512]{0,1:T(8,128)S(1)}) fusion(f32[512]{0:T(512)S(1)} %convert_add_fusion, f32[64]{0:T(128)S(1)} %broadcast_multiply_fusion), kind=kLoop, calls=%fused_computation.10 | loop fusion | flops 65536 | bytes 395520 | tf_op jit(solution)/shard_map/neg | solution.py:248
  43.6 0.2 fusion
  43.8 0.1 copy.11.g_ref
  43.9 30.4 %all-to-all-done = bf16[256,8,256]{2,1,0:T(8,128)(2,1)S(1)} async-done(((bf16[256,8,256]{2,1,0:T(8,128)(2,1)}), bf16[256,8,256]{2,1,0:T(8,128)(2,1)S(1)}, u32[]{:S(2)}, u32[]{:S(2)}) %all-to-all-start) | async-done | bytes 1048608 | tf_op jit(solution)/shard_map/all_to_all | solution.py:243
  74.3 5.9 %recover.1 = f32[2,4,256,512]{3,2,1,0:T(8,128)} custom-call(bf16[4,4,16,8,256]{4,3,2,1,0:T(8,128)(2,1)S(1)} %bitcast.10, bf16[128,1024]{1,0:T(8,128)(2,1)S(1)} %copy.11.g_ref, bf16[1024,128]{1,0:T(8,128)(2,1)S(1)} %get-tuple-element.37.h_ref), custom_call_target="tpu_custom_call" | custom-call | tf_op jit(solution)/shard_map/recover/pallas_call | solution.py:254
  (22 shorter events, 0.2 us)
Async XLA Ops:
  0.0 9.0 %collective-permute-start.1 = (bf16[2,64,1024]{2,1,0:T(8,128)(2,1)}, bf16[2,64,1024]{2,1,0:T(8,128)(2,1)S(1)}, u32[]{:S(2)}, u32[]{:S(2)}) collective-permute-start(bf16[2,64,1024]{2,1,0:T(8,128)(2,1)} %bitcast.11), channel_id=1, source_target_pairs={{0,192},{64,0},{128,64},{192,128},{1,193},{65,1},{129,65},{193,129... | collective-permute-start | bytes 786440 | tf_op jit(solution)/shard_map/ppermute | solution.py:184
  3.3 8.7 %collective-permute-start = (bf16[2,64,1024]{2,1,0:T(8,128)(2,1)}, bf16[2,64,1024]{2,1,0:T(8,128)(2,1)S(1)}, u32[]{:S(2)}, u32[]{:S(2)}) collective-permute-start(bf16[2,64,1024]{2,1,0:T(8,128)(2,1)} %bitcast.12), channel_id=1, source_target_pairs={{0,64},{64,128},{128,192},{192,0},{1,65},{65,129},{129,193},{193,1... | collective-permute-start | bytes 786440 | tf_op jit(solution)/shard_map/ppermute | solution.py:184
  6.2 35.9 %copy-start = (s32[64]{0:T(128)S(1)}, s32[64]{0:T(128)}, u32[]{:S(2)}) copy-start(s32[64]{0:T(128)} %param.12) | copy-start | bytes 772
  6.2 36.2 %copy-start.1 = (f32[64]{0:T(128)S(1)}, f32[64]{0:T(128)}, u32[]{:S(2)}) copy-start(f32[64]{0:T(128)} %param.13) | copy-start | bytes 772
  6.2 17.3 %collective-permute-start.2 = (bf16[2,2,64,256]{3,2,1,0:T(8,128)(2,1)}, bf16[2,2,64,256]{3,2,1,0:T(8,128)(2,1)S(1)}, u32[]{:S(2)}, u32[]{:S(2)}) collective-permute-start(bf16[2,2,64,256]{3,2,1,0:T(8,128)(2,1)} %get-tuple-element.24), channel_id=1, source_target_pairs={{0,64},{64,128},{128,192},{192,0},{1,65},{65,129},{129,193},{193,1... | collective-permute-start | bytes 393224 | tf_op jit(solution)/shard_map/ppermute | solution.py:184
  6.4 17.0 %collective-permute-start.4 = (bf16[2,2,64,256]{3,2,1,0:T(8,128)(2,1)}, bf16[2,2,64,256]{3,2,1,0:T(8,128)(2,1)S(1)}, u32[]{:S(2)}, u32[]{:S(2)}) collective-permute-start(bf16[2,2,64,256]{3,2,1,0:T(8,128)(2,1)} %get-tuple-element.27), channel_id=1, source_target_pairs={{0,192},{64,0},{128,64},{192,128},{1,193},{65,1},{129,65},{193,129... | collective-permute-start | bytes 393224 | tf_op jit(solution)/shard_map/ppermute | solution.py:184
  9.0 6.3 %collective-permute-start.6 = (bf16[64,1024]{1,0:T(8,128)(2,1)S(1)}, bf16[64,1024]{1,0:T(8,128)(2,1)S(1)}, u32[]{:S(2)}, u32[]{:S(2)}) collective-permute-start(bf16[64,1024]{1,0:T(8,128)(2,1)S(1)} %slice_bitcast_fusion), channel_id=1, source_target_pairs={{0,192},{64,0},{128,64},{192,128},{1,193},{65,1},{129,65},{193,129... | collective-permute-start | bytes 393224 | tf_op jit(solution)/shard_map/ppermute | solution.py:184
  12.0 6.4 %collective-permute-start.5 = (bf16[64,1024]{1,0:T(8,128)(2,1)S(1)}, bf16[64,1024]{1,0:T(8,128)(2,1)S(1)}, u32[]{:S(2)}, u32[]{:S(2)}) collective-permute-start(bf16[64,1024]{1,0:T(8,128)(2,1)S(1)} %slice_bitcast_fusion.1), channel_id=1, source_target_pairs={{0,64},{64,128},{128,192},{192,0},{1,65},{65,129},{129,193},{193,1... | collective-permute-start | bytes 393224 | tf_op jit(solution)/shard_map/ppermute | solution.py:184
  12.1 11.4 %collective-permute-start.3 = (bf16[2,2,64,256]{3,2,1,0:T(8,128)(2,1)}, bf16[2,2,64,256]{3,2,1,0:T(8,128)(2,1)S(1)}, u32[]{:S(2)}, u32[]{:S(2)}) collective-permute-start(bf16[2,2,64,256]{3,2,1,0:T(8,128)(2,1)} %get-tuple-element.26), channel_id=1, source_target_pairs={{0,128},{64,192},{128,0},{192,64},{1,129},{65,193},{129,1},{193,65... | collective-permute-start | bytes 393224 | tf_op jit(solution)/shard_map/ppermute | solution.py:184
  15.3 8.9 %collective-permute-start.10 = (bf16[64,1024]{1,0:T(8,128)(2,1)S(1)}, bf16[64,1024]{1,0:T(8,128)(2,1)S(1)}, u32[]{:S(2)}, u32[]{:S(2)}) collective-permute-start(bf16[64,1024]{1,0:T(8,128)(2,1)S(1)} %collective-permute-done.6.refs_3_), channel_id=1, source_target_pairs={{0,8},{8,0},{1,9},{9,1},{2,10},{10,2},{3,11},{11,3},{4,12},{12,4},... | collective-permute-start | bytes 393224 | tf_op jit(solution)/shard_map/ppermute | solution.py:187
  18.4 6.2 %collective-permute-start.9 = (bf16[64,1024]{1,0:T(8,128)(2,1)S(1)}, bf16[64,1024]{1,0:T(8,128)(2,1)S(1)}, u32[]{:S(2)}, u32[]{:S(2)}) collective-permute-start(bf16[64,1024]{1,0:T(8,128)(2,1)S(1)} %collective-permute-done.5.refs_2_), channel_id=1, source_target_pairs={{0,8},{8,0},{1,9},{9,1},{2,10},{10,2},{3,11},{11,3},{4,12},{12,4},... | collective-permute-start | bytes 393224 | tf_op jit(solution)/shard_map/ppermute | solution.py:187
  23.5 1.4 %collective-permute-start.13 = (bf16[2,2,64,256]{3,2,1,0:T(8,128)(2,1)S(1)}, bf16[2,2,64,256]{3,2,1,0:T(8,128)(2,1)S(1)}, u32[]{:S(2)}, u32[]{:S(2)}) collective-permute-start(bf16[2,2,64,256]{3,2,1,0:T(8,128)(2,1)S(1)} %collective-permute-done.2.refs_11_), channel_id=1, source_target_pairs={{0,8},{8,0},{1,9},{9,1},{2,10},{10,2},{3,11},{11,3},{4,12},{12,4},... | collective-permute-start | bytes 393224 | tf_op jit(solution)/shard_map/ppermute | solution.py:187
  23.6 1.5 %collective-permute-start.14 = (bf16[2,2,64,256]{3,2,1,0:T(8,128)(2,1)S(1)}, bf16[2,2,64,256]{3,2,1,0:T(8,128)(2,1)S(1)}, u32[]{:S(2)}, u32[]{:S(2)}) collective-permute-start(bf16[2,2,64,256]{3,2,1,0:T(8,128)(2,1)S(1)} %collective-permute-done.3.refs_12_), channel_id=1, source_target_pairs={{0,8},{8,0},{1,9},{9,1},{2,10},{10,2},{3,11},{11,3},{4,12},{12,4},... | collective-permute-start | bytes 393224 | tf_op jit(solution)/shard_map/ppermute | solution.py:187
  24.1 2.9 %collective-permute-start.7 = (bf16[2,64,1024]{2,1,0:T(8,128)(2,1)}, bf16[2,64,1024]{2,1,0:T(8,128)(2,1)S(1)}, u32[]{:S(2)}, u32[]{:S(2)}) collective-permute-start(bf16[2,64,1024]{2,1,0:T(8,128)(2,1)} %bitcast.14), channel_id=1, source_target_pairs={{0,8},{8,0},{1,9},{9,1},{2,10},{10,2},{3,11},{11,3},{4,12},{12,4},... | collective-permute-start | bytes 786440 | tf_op jit(solution)/shard_map/ppermute | solution.py:187
  24.2 2.8 %collective-permute-start.8 = (bf16[2,64,1024]{2,1,0:T(8,128)(2,1)S(1)}, bf16[2,64,1024]{2,1,0:T(8,128)(2,1)S(1)}, u32[]{:S(2)}, u32[]{:S(2)}) collective-permute-start(bf16[2,64,1024]{2,1,0:T(8,128)(2,1)S(1)} %collective-permute-done.refs_1_), channel_id=1, source_target_pairs={{0,8},{8,0},{1,9},{9,1},{2,10},{10,2},{3,11},{11,3},{4,12},{12,4},... | collective-permute-start | bytes 786440 | tf_op jit(solution)/shard_map/ppermute | solution.py:187
  24.6 2.4 %collective-permute-start.11 = (bf16[2,64,1024]{2,1,0:T(8,128)(2,1)S(1)}, bf16[2,64,1024]{2,1,0:T(8,128)(2,1)S(1)}, u32[]{:S(2)}, u32[]{:S(2)}) collective-permute-start(bf16[2,64,1024]{2,1,0:T(8,128)(2,1)S(1)} %collective-permute-done.1.refs_4_), channel_id=1, source_target_pairs={{0,8},{8,0},{1,9},{9,1},{2,10},{10,2},{3,11},{11,3},{4,12},{12,4},... | collective-permute-start | bytes 786440 | tf_op jit(solution)/shard_map/ppermute | solution.py:187
  24.9 2.1 %collective-permute-start.12 = (bf16[2,2,80,256]{3,2,1,0:T(8,128)(2,1)}, bf16[2,2,80,256]{3,2,1,0:T(8,128)(2,1)S(1)}, u32[]{:S(2)}, u32[]{:S(2)}) collective-permute-start(bf16[2,2,80,256]{3,2,1,0:T(8,128)(2,1)} %get-tuple-element.36), channel_id=1, source_target_pairs={{0,8},{8,0},{1,9},{9,1},{2,10},{10,2},{3,11},{11,3},{4,12},{12,4},... | collective-permute-start | bytes 491528 | tf_op jit(solution)/shard_map/ppermute | solution.py:187
  25.1 1.6 %collective-permute-start.15 = (bf16[2,2,64,256]{3,2,1,0:T(8,128)(2,1)S(1)}, bf16[2,2,64,256]{3,2,1,0:T(8,128)(2,1)S(1)}, u32[]{:S(2)}, u32[]{:S(2)}) collective-permute-start(bf16[2,2,64,256]{3,2,1,0:T(8,128)(2,1)S(1)} %collective-permute-done.4.refs_13_), channel_id=1, source_target_pairs={{0,8},{8,0},{1,9},{9,1},{2,10},{10,2},{3,11},{11,3},{4,12},{12,4},... | collective-permute-start | bytes 393224 | tf_op jit(solution)/shard_map/ppermute | solution.py:187
  29.7 44.6 %all-to-all-start = ((bf16[256,8,256]{2,1,0:T(8,128)(2,1)}), bf16[256,8,256]{2,1,0:T(8,128)(2,1)S(1)}, u32[]{:S(2)}, u32[]{:S(2)}) async-start(bf16[256,8,256]{2,1,0:T(8,128)(2,1)} %bitcast.3), calls=%async_computation | async-start | bytes 2097152 | tf_op jit(solution)/shard_map/all_to_all | solution.py:243

commit v11 on v9

--- a/solution.py
+++ b/solution.py
@@ -117,45 +117,52 @@
         copy(r0).wait()
 
 
-def recover_kernel(img_ref, g_ref, h_ref, out_ref, y_ref):
-    i = pl.program_id(0)
+def recover_kernel(img_ref, g_ref, h_ref, out_ref, y_ref, out_mem, out_sem):
     outer, parts, inner, eight, cols = img_ref.shape
     passes = outer * inner
-
-    @pl.when(i == 0)
-    def _():
-        some = 1
-        for k in range(0, outer, some):
-            acc = img_ref[k : k + some, 0].astype(jnp.float32)
-            for z in range(1, parts):
-                acc = acc + img_ref[k : k + some, z].astype(jnp.float32)
-            acc = acc.reshape(some * inner * eight, cols)
-            at = k * inner * eight
-            for c in range(cols // 128):
-                y_ref[c, at : at + some * inner * eight] = acc[:, c * 128 : c * 128 + 128]
+    own = eight // 2
+    for k in range(outer):
+        acc = img_ref[k, 0].astype(jnp.float32)
+        for z in range(1, parts):
+            acc = acc + img_ref[k, z].astype(jnp.float32)
+        acc = acc.reshape(inner * eight, cols)
+        at = k * inner * eight
+        for c in range(cols // 128):
+            y_ref[c, at : at + inner * eight] = acc[:, c * 128 : c * 128 + 128]
 
     g = g_ref[...]
     h = h_ref[...]
-    chains = []
-    for c in range(cols // 128):
-        re = y_ref.at[c][pl.ds(i, passes, stride=eight), :]
-        im = y_ref.at[c][pl.ds(eight // 2 + i, passes, stride=eight), :]
-        y = jnp.concatenate([re, im], axis=0).T.astype(jnp.bfloat16)
-        chains += [y[:64], y[64:]]
-    wide = [y.astype(jnp.float32) for y in chains]
 
     def shrink(v):
         return v - jnp.clip(v, -LEVEL, LEVEL)
 
-    us = [shrink(dot(y, g, 1, 0)) for y in chains]
-    for _ in range(ITERS - 1):
-        resids = [
-            (y - dot(u.astype(jnp.bfloat16), h, 1, 0)).astype(jnp.bfloat16) for y, u in zip(wide, us)
-        ]
-        us = [shrink(u + dot(r, g, 1, 0)) for u, r in zip(us, resids)]
-    for k, u in enumerate(us):
-        out_ref[0, 0, k * 64 : k * 64 + 64] = u[:, :BINS]
-        out_ref[1, 0, k * 64 : k * 64 + 64] = u[:, BINS:]
+    def copy(i, c):
+        piece = pl.ds(c * 128, 128)
+        return pltpu.make_async_copy(out_mem.at[:, i, piece], out_ref.at[:, i, piece], out_sem.at[i, c])
+
+    for i in range(own):
+        chains = []
+        for c in range(cols // 128):
+            re = y_ref.at[c][pl.ds(i, passes, stride=eight), :]
+            im = y_ref.at[c][pl.ds(own + i, passes, stride=eight), :]
+            y = jnp.concatenate([re, im], axis=0).T.astype(jnp.bfloat16)
+            chains += [y[:64], y[64:]]
+        wide = [y.astype(jnp.float32) for y in chains]
+        us = [shrink(dot(y, g, 1, 0)) for y in chains]
+        for _ in range(ITERS - 1):
+            resids = [
+                (y - dot(u.astype(jnp.bfloat16), h, 1, 0)).astype(jnp.bfloat16)
+                for y, u in zip(wide, us)
+            ]
+            us = [shrink(u + dot(r, g, 1, 0)) for u, r in zip(us, resids)]
+        for k, u in enumerate(us):
+            out_mem[0, i, k * 64 : k * 64 + 64] = u[:, :BINS]
+            out_mem[1, i, k * 64 : k * 64 + 64] = u[:, BINS:]
+            if k % 2 == 1:
+                copy(i, k // 2).start()
+    for i in range(own):
+        for c in range(cols // 128):
+            copy(i, c).wait()
 
 
 def steering(normal_spacings, source):
@@ -250,11 +257,14 @@
     image = image.reshape(nx, nz, nc * ny * nl, 2 * own, cols)
     return pl.pallas_call(
         recover_kernel,
-        grid=(own,),
         out_shape=jax.ShapeDtypeStruct((2, own, cols, BINS), jnp.float32),
         in_specs=[VMEM] * 3,
-        out_specs=pl.BlockSpec((2, 1, cols, BINS), lambda i: (0, i, 0, 0)),
-        scratch_shapes=[pltpu.VMEM((cols // 128, total * 2 * own, 128), jnp.float32)],
+        out_specs=HBM,
+        scratch_shapes=[
+            pltpu.VMEM((cols // 128, total * 2 * own, 128), jnp.float32),
+            pltpu.VMEM((2, own, cols, BINS), jnp.float32),
+            pltpu.SemaphoreType.DMA((own, cols // 128)),
+        ],
         compiler_params=pltpu.CompilerParams(vmem_limit_bytes=40 << 20),
         name="recover",
     )(image, gb, hb)

time: 77.7 us -> 77.1 us (level)
  no operation moved by 1% of the time
where the time goes in v11:
time: 77.1 us; the launch traced here: 76.9 us
  waiting for transfers between devices  34.2 us (44%)
  starting transfers between devices  28.1 us (36%)
  Pallas kernels  10.7 us (14%)
  other arithmetic  3.3 us (4%)
    all_to_all x1, waiting for transfers between devices, body(): image = lax.all_to_all(image, ('x', 'zh', 'c', 'y', 'zl'), 0, 0, tiled=True)  30.4 us
    all_to_all x1, starting transfers between devices, body(): image = lax.all_to_all(image, ('x', 'zh', 'c', 'y', 'zl'), 0, 0, tiled=True)  12.5 us
    ppermute x7, starting transfers between devices, turn(): return lax.ppermute(value, 'x', [(i, (i + step) % nx) for i in range(nx)])  9.2 us
    ppermute x9, starting transfers between devices, swap(): return lax.ppermute(value, 'c', [(0, 1), (1, 0)])  6.36 us
    pallas_call x1, Pallas kernels, body(): pl.pallas_call(recover_kernel, out_shape=jax.ShapeDtypeStruct((2, own, co...  5.18 us
    pallas_call x1, Pallas kernels, partial_image(): pl.pallas_call(focus_kernel, out_shape=[jax.ShapeDtypeStruct(shape, bf) f...  2.86 us
    pallas_call x1, Pallas kernels, partial_image(): pl.pallas_call(functools.partial(image_kernel, nx), out_shape=jax.ShapeDt...  2.65 us
    ppermute x7, waiting for transfers between devices, turn(): return lax.ppermute(value, 'x', [(i, (i + step) % nx) for i in range(nx)])  2.51 us
  transfers between devices with their start and end apart: 17, of which 5 were waited for; matrix products, arithmetic and copies ran while one was open for 5% of the time, Pallas kernels for 4%

profile of v11, /device:TPU:1, one launch (start us, length us, event | category | flops | bytes accessed | tf_op | source)
XLA Modules:
  0.0 76.9 jit_solution(17858868702083444134)
XLA Ops:
  0.0 3.3 %collective-permute-start.1 = (bf16[2,64,1024]{2,1,0:T(8,128)(2,1)}, bf16[2,64,1024]{2,1,0:T(8,128)(2,1)S(1)}, u32[]{:S(2)}, u32[]{:S(2)}) collective-permute-start(bf16[2,64,1024]{2,1,0:T(8,128)(2,1)} %bitcast.11), channel_id=1, source_target_pairs={{0,192},{64,0},{128,64},{192,128},{1,193},{65,1},{129,65},{193,129... | collective-permute-start | bytes 786440 | tf_op jit(solution)/shard_map/ppermute | solution.py:191
  3.3 2.9 %focus.1 = (bf16[2,2,80,256]{3,2,1,0:T(8,128)(2,1)}, bf16[2,2,64,256]{3,2,1,0:T(8,128)(2,1)}, bf16[2,2,64,256]{3,2,1,0:T(8,128)(2,1)}, bf16[2,2,64,256]{3,2,1,0:T(8,128)(2,1)}) custom-call(s32[8]{0:T(128)} %lat_ref.1, s32[8]{0:T(128)} %ver_ref.1, bf16[2,8,64,512]{3,2,1,0:T(8,128)(2,1)} %echo_ref.1, bf16[2,512,256]{2,1,0:T(8,128)(2,1)} %kern_ref.1), custom_call_target="tpu_custom_call" | custom-call | tf_op jit(solution)/shard_map/focus/pallas_call | solution.py:205
  6.2 0.3 collective-permute-start.2
  6.4 3.7 %collective-permute-start.3 = (bf16[2,2,64,256]{3,2,1,0:T(8,128)(2,1)}, bf16[2,2,64,256]{3,2,1,0:T(8,128)(2,1)S(1)}, u32[]{:S(2)}, u32[]{:S(2)}) collective-permute-start(bf16[2,2,64,256]{3,2,1,0:T(8,128)(2,1)} %get-tuple-element.24), channel_id=1, source_target_pairs={{0,128},{64,192},{128,0},{192,64},{1,129},{65,193},{129,1},{193,65... | collective-permute-start | bytes 393224 | tf_op jit(solution)/shard_map/ppermute | solution.py:191
  10.1 1.9 %collective-permute-start.6 = (bf16[64,1024]{1,0:T(8,128)(2,1)S(1)}, bf16[64,1024]{1,0:T(8,128)(2,1)S(1)}, u32[]{:S(2)}, u32[]{:S(2)}) collective-permute-start(bf16[64,1024]{1,0:T(8,128)(2,1)S(1)} %slice_bitcast_fusion), channel_id=1, source_target_pairs={{0,192},{64,0},{128,64},{192,128},{1,193},{65,1},{129,65},{193,129... | collective-permute-start | bytes 393224 | tf_op jit(solution)/shard_map/ppermute | solution.py:191
  12.0 0.1 collective-permute-start.5
  12.1 1.0 %broadcast_select_fusion.refs_0_ = bf16[2,64,1024]{2,1,0:T(8,128)(2,1)S(1)} fusion(bf16[2,64,1024]{2,1,0:T(8,128)(2,1)} %bitcast.13, pred[]{:T(512)S(6)} %lt.3), kind=kLoop, calls=%fused_computation.6 | loop fusion | flops 131072 | bytes 524289 | tf_op jit(solution)/shard_map/jit(_where)/select_n | solution.py:215
  13.1 0.9 %broadcast_select_fusion.1.refs_10_ = bf16[2,2,80,256]{3,2,1,0:T(8,128)(2,1)S(1)} fusion(bf16[2,2,80,256]{3,2,1,0:T(8,128)(2,1)} %get-tuple-element.34, pred[]{:T(512)S(6)} %lt.3), kind=kLoop, calls=%fused_computation.7 | loop fusion | flops 81920 | bytes 327681 | tf_op jit(solution)/shard_map/jit(_where)/select_n | solution.py:216
  14.0 1.0 %collective-permute-done.2.refs_11_ = bf16[2,2,64,256]{3,2,1,0:T(8,128)(2,1)S(1)} collective-permute-done((bf16[2,2,64,256]{3,2,1,0:T(8,128)(2,1)}, bf16[2,2,64,256]{3,2,1,0:T(8,128)(2,1)S(1)}, u32[]{:S(2)}, u32[]{:S(2)}) %collective-permute-start.2) | collective-permute-done | bytes 131104 | tf_op jit(solution)/shard_map/ppermute | solution.py:191
  15.1 1.5 %collective-permute-done.3.refs_12_ = bf16[2,2,64,256]{3,2,1,0:T(8,128)(2,1)S(1)} collective-permute-done((bf16[2,2,64,256]{3,2,1,0:T(8,128)(2,1)}, bf16[2,2,64,256]{3,2,1,0:T(8,128)(2,1)S(1)}, u32[]{:S(2)}, u32[]{:S(2)}) %collective-permute-start.3) | collective-permute-done | bytes 131104 | tf_op jit(solution)/shard_map/ppermute | solution.py:191
  16.5 3.5 %collective-permute-start.13 = (bf16[2,2,64,256]{3,2,1,0:T(8,128)(2,1)S(1)}, bf16[2,2,64,256]{3,2,1,0:T(8,128)(2,1)S(1)}, u32[]{:S(2)}, u32[]{:S(2)}) collective-permute-start(bf16[2,2,64,256]{3,2,1,0:T(8,128)(2,1)S(1)} %collective-permute-done.2.refs_11_), channel_id=1, source_target_pairs={{0,8},{8,0},{1,9},{9,1},{2,10},{10,2},{3,11},{11,3},{4,12},{12,4},... | collective-permute-start | bytes 393224 | tf_op jit(solution)/shard_map/ppermute | solution.py:194
  20.0 0.1 collective-permute-start.14
  20.1 0.4 collective-permute-start.12
  20.5 0.1 collective-permute-start.15
  20.6 1.3 %collective-permute-start.7 = (bf16[2,64,1024]{2,1,0:T(8,128)(2,1)}, bf16[2,64,1024]{2,1,0:T(8,128)(2,1)S(1)}, u32[]{:S(2)}, u32[]{:S(2)}) collective-permute-start(bf16[2,64,1024]{2,1,0:T(8,128)(2,1)} %bitcast.14), channel_id=1, source_target_pairs={{0,8},{8,0},{1,9},{9,1},{2,10},{10,2},{3,11},{11,3},{4,12},{12,4},... | collective-permute-start | bytes 786440 | tf_op jit(solution)/shard_map/ppermute | solution.py:194
  21.9 0.0 collective-permute-start.8
  21.9 0.5 collective-permute-start.11
  22.4 0.1 collective-permute-start.10
  22.5 0.4 collective-permute-start.9
  22.9 1.1 %collective-permute-done.10.refs_8_ = bf16[64,1024]{1,0:T(8,128)(2,1)S(1)} collective-permute-done((bf16[64,1024]{1,0:T(8,128)(2,1)S(1)}, bf16[64,1024]{1,0:T(8,128)(2,1)S(1)}, u32[]{:S(2)}, u32[]{:S(2)}) %collective-permute-start.10) | collective-permute-done | bytes 131104 | tf_op jit(solution)/shard_map/ppermute | solution.py:194
  24.0 0.2 collective-permute-done.9.refs_7_
  24.2 2.6 %image.1 = bf16[2048,256]{1,0:T(8,128)(2,1)} custom-call(bf16[2,64,1024]{2,1,0:T(8,128)(2,1)S(1)} %broadcast_select_fusion.refs_0_, bf16[2,64,1024]{2,1,0:T(8,128)(2,1)S(1)} %collective-permute-done.refs_1_, bf16[64,1024]{1,0:T(8,128)(2,1)S(1)} %collective-permute-done.5.refs_2_, bf16[64,1024]{1,0:T(8,128)(2,1)S(1)} %collective-permute-done.6.refs_3_, ...), custom_call_target="tpu_custom_call" | custom-call | tf_op jit(solution)/shard_map/image/pallas_call | solution.py:225
  26.8 12.5 %all-to-all-start = ((bf16[256,8,256]{2,1,0:T(8,128)(2,1)}), bf16[256,8,256]{2,1,0:T(8,128)(2,1)S(1)}, u32[]{:S(2)}, u32[]{:S(2)}) async-start(bf16[256,8,256]{2,1,0:T(8,128)(2,1)} %bitcast.3), calls=%async_computation | async-start | bytes 2097152 | tf_op jit(solution)/shard_map/all_to_all | solution.py:247
  39.4 0.1 reshape.21
  39.4 0.1 copy.10
  39.5 0.1 eq.15
  39.6 0.2 select_reduce_fusion
  39.8 1.0 %fusion.1 = (f32[64,512]{0,1:T(8,128)S(1)}, f32[64,512]{0,1:T(8,128)S(1)}, f32[64,512]{0,1:T(8,128)S(1)}) fusion(f32[512]{0:T(512)S(1)} %convert_add_fusion, f32[64]{0:T(128)S(1)} %broadcast_multiply_fusion), kind=kLoop, calls=%fused_computation.10 | loop fusion | flops 65536 | bytes 395520 | tf_op jit(solution)/shard_map/neg | solution.py:252
  40.8 0.2 fusion
  41.0 0.1 copy.11.g_ref
  41.2 30.4 %all-to-all-done = bf16[256,8,256]{2,1,0:T(8,128)(2,1)S(1)} async-done(((bf16[256,8,256]{2,1,0:T(8,128)(2,1)}), bf16[256,8,256]{2,1,0:T(8,128)(2,1)S(1)}, u32[]{:S(2)}, u32[]{:S(2)}) %all-to-all-start) | async-done | bytes 1048608 | tf_op jit(solution)/shard_map/all_to_all | solution.py:247
  71.5 5.2 %recover.1 = f32[2,4,256,512]{3,2,1,0:T(8,128)} custom-call(bf16[4,4,16,8,256]{4,3,2,1,0:T(8,128)(2,1)S(1)} %bitcast.10, bf16[128,1024]{1,0:T(8,128)(2,1)S(1)} %copy.11.g_ref, bf16[1024,128]{1,0:T(8,128)(2,1)S(1)} %get-tuple-element.35.h_ref), custom_call_target="tpu_custom_call" | custom-call | tf_op jit(solution)/shard_map/recover/pallas_call | solution.py:258
  (22 shorter events, 0.1 us)
Async XLA Ops:
  0.0 10.1 %collective-permute-start.1 = (bf16[2,64,1024]{2,1,0:T(8,128)(2,1)}, bf16[2,64,1024]{2,1,0:T(8,128)(2,1)S(1)}, u32[]{:S(2)}, u32[]{:S(2)}) collective-permute-start(bf16[2,64,1024]{2,1,0:T(8,128)(2,1)} %bitcast.11), channel_id=1, source_target_pairs={{0,192},{64,0},{128,64},{192,128},{1,193},{65,1},{129,65},{193,129... | collective-permute-start | bytes 786440 | tf_op jit(solution)/shard_map/ppermute | solution.py:191
  3.3 8.7 %collective-permute-start = (bf16[2,64,1024]{2,1,0:T(8,128)(2,1)}, bf16[2,64,1024]{2,1,0:T(8,128)(2,1)S(1)}, u32[]{:S(2)}, u32[]{:S(2)}) collective-permute-start(bf16[2,64,1024]{2,1,0:T(8,128)(2,1)} %bitcast.12), channel_id=1, source_target_pairs={{0,64},{64,128},{128,192},{192,0},{1,65},{65,129},{129,193},{193,1... | collective-permute-start | bytes 786440 | tf_op jit(solution)/shard_map/ppermute | solution.py:191
  6.2 33.2 %copy-start = (s32[64]{0:T(128)S(1)}, s32[64]{0:T(128)}, u32[]{:S(2)}) copy-start(s32[64]{0:T(128)} %param.12) | copy-start | bytes 772
  6.2 33.4 %copy-start.1 = (f32[64]{0:T(128)S(1)}, f32[64]{0:T(128)}, u32[]{:S(2)}) copy-start(f32[64]{0:T(128)} %param.13) | copy-start | bytes 772
  6.2 8.9 %collective-permute-start.2 = (bf16[2,2,64,256]{3,2,1,0:T(8,128)(2,1)}, bf16[2,2,64,256]{3,2,1,0:T(8,128)(2,1)S(1)}, u32[]{:S(2)}, u32[]{:S(2)}) collective-permute-start(bf16[2,2,64,256]{3,2,1,0:T(8,128)(2,1)} %get-tuple-element.23), channel_id=1, source_target_pairs={{0,64},{64,128},{128,192},{192,0},{1,65},{65,129},{129,193},{193,1... | collective-permute-start | bytes 393224 | tf_op jit(solution)/shard_map/ppermute | solution.py:191
  6.4 10.1 %collective-permute-start.3 = (bf16[2,2,64,256]{3,2,1,0:T(8,128)(2,1)}, bf16[2,2,64,256]{3,2,1,0:T(8,128)(2,1)S(1)}, u32[]{:S(2)}, u32[]{:S(2)}) collective-permute-start(bf16[2,2,64,256]{3,2,1,0:T(8,128)(2,1)} %get-tuple-element.24), channel_id=1, source_target_pairs={{0,128},{64,192},{128,0},{192,64},{1,129},{65,193},{129,1},{193,65... | collective-permute-start | bytes 393224 | tf_op jit(solution)/shard_map/ppermute | solution.py:191
  10.1 6.4 %collective-permute-start.4 = (bf16[2,2,64,256]{3,2,1,0:T(8,128)(2,1)}, bf16[2,2,64,256]{3,2,1,0:T(8,128)(2,1)S(1)}, u32[]{:S(2)}, u32[]{:S(2)}) collective-permute-start(bf16[2,2,64,256]{3,2,1,0:T(8,128)(2,1)} %get-tuple-element.25), channel_id=1, source_target_pairs={{0,192},{64,0},{128,64},{192,128},{1,193},{65,1},{129,65},{193,129... | collective-permute-start | bytes 393224 | tf_op jit(solution)/shard_map/ppermute | solution.py:191
  10.1 10.4 %collective-permute-start.6 = (bf16[64,1024]{1,0:T(8,128)(2,1)S(1)}, bf16[64,1024]{1,0:T(8,128)(2,1)S(1)}, u32[]{:S(2)}, u32[]{:S(2)}) collective-permute-start(bf16[64,1024]{1,0:T(8,128)(2,1)S(1)} %slice_bitcast_fusion), channel_id=1, source_target_pairs={{0,192},{64,0},{128,64},{192,128},{1,193},{65,1},{129,65},{193,129... | collective-permute-start | bytes 393224 | tf_op jit(solution)/shard_map/ppermute | solution.py:191
  12.0 8.6 %collective-permute-start.5 = (bf16[64,1024]{1,0:T(8,128)(2,1)S(1)}, bf16[64,1024]{1,0:T(8,128)(2,1)S(1)}, u32[]{:S(2)}, u32[]{:S(2)}) collective-permute-start(bf16[64,1024]{1,0:T(8,128)(2,1)S(1)} %slice_bitcast_fusion.1), channel_id=1, source_target_pairs={{0,64},{64,128},{128,192},{192,0},{1,65},{65,129},{129,193},{193,1... | collective-permute-start | bytes 393224 | tf_op jit(solution)/shard_map/ppermute | solution.py:191
  16.5 5.4 %collective-permute-start.13 = (bf16[2,2,64,256]{3,2,1,0:T(8,128)(2,1)S(1)}, bf16[2,2,64,256]{3,2,1,0:T(8,128)(2,1)S(1)}, u32[]{:S(2)}, u32[]{:S(2)}) collective-permute-start(bf16[2,2,64,256]{3,2,1,0:T(8,128)(2,1)S(1)} %collective-permute-done.2.refs_11_), channel_id=1, source_target_pairs={{0,8},{8,0},{1,9},{9,1},{2,10},{10,2},{3,11},{11,3},{4,12},{12,4},... | collective-permute-start | bytes 393224 | tf_op jit(solution)/shard_map/ppermute | solution.py:194
  20.0 1.9 %collective-permute-start.14 = (bf16[2,2,64,256]{3,2,1,0:T(8,128)(2,1)S(1)}, bf16[2,2,64,256]{3,2,1,0:T(8,128)(2,1)S(1)}, u32[]{:S(2)}, u32[]{:S(2)}) collective-permute-start(bf16[2,2,64,256]{3,2,1,0:T(8,128)(2,1)S(1)} %collective-permute-done.3.refs_12_), channel_id=1, source_target_pairs={{0,8},{8,0},{1,9},{9,1},{2,10},{10,2},{3,11},{11,3},{4,12},{12,4},... | collective-permute-start | bytes 393224 | tf_op jit(solution)/shard_map/ppermute | solution.py:194
  20.1 2.4 %collective-permute-start.12 = (bf16[2,2,80,256]{3,2,1,0:T(8,128)(2,1)}, bf16[2,2,80,256]{3,2,1,0:T(8,128)(2,1)S(1)}, u32[]{:S(2)}, u32[]{:S(2)}) collective-permute-start(bf16[2,2,80,256]{3,2,1,0:T(8,128)(2,1)} %get-tuple-element.34), channel_id=1, source_target_pairs={{0,8},{8,0},{1,9},{9,1},{2,10},{10,2},{3,11},{11,3},{4,12},{12,4},... | collective-permute-start | bytes 491528 | tf_op jit(solution)/shard_map/ppermute | solution.py:194
  20.5 1.9 %collective-permute-start.15 = (bf16[2,2,64,256]{3,2,1,0:T(8,128)(2,1)S(1)}, bf16[2,2,64,256]{3,2,1,0:T(8,128)(2,1)S(1)}, u32[]{:S(2)}, u32[]{:S(2)}) collective-permute-start(bf16[2,2,64,256]{3,2,1,0:T(8,128)(2,1)S(1)} %collective-permute-done.4.refs_13_), channel_id=1, source_target_pairs={{0,8},{8,0},{1,9},{9,1},{2,10},{10,2},{3,11},{11,3},{4,12},{12,4},... | collective-permute-start | bytes 393224 | tf_op jit(solution)/shard_map/ppermute | solution.py:194
  20.6 3.5 %collective-permute-start.7 = (bf16[2,64,1024]{2,1,0:T(8,128)(2,1)}, bf16[2,64,1024]{2,1,0:T(8,128)(2,1)S(1)}, u32[]{:S(2)}, u32[]{:S(2)}) collective-permute-start(bf16[2,64,1024]{2,1,0:T(8,128)(2,1)} %bitcast.14), channel_id=1, source_target_pairs={{0,8},{8,0},{1,9},{9,1},{2,10},{10,2},{3,11},{11,3},{4,12},{12,4},... | collective-permute-start | bytes 786440 | tf_op jit(solution)/shard_map/ppermute | solution.py:194
  21.9 2.3 %collective-permute-start.8 = (bf16[2,64,1024]{2,1,0:T(8,128)(2,1)S(1)}, bf16[2,64,1024]{2,1,0:T(8,128)(2,1)S(1)}, u32[]{:S(2)}, u32[]{:S(2)}) collective-permute-start(bf16[2,64,1024]{2,1,0:T(8,128)(2,1)S(1)} %collective-permute-done.refs_1_), channel_id=1, source_target_pairs={{0,8},{8,0},{1,9},{9,1},{2,10},{10,2},{3,11},{11,3},{4,12},{12,4},... | collective-permute-start | bytes 786440 | tf_op jit(solution)/shard_map/ppermute | solution.py:194
  21.9 2.3 %collective-permute-start.11 = (bf16[2,64,1024]{2,1,0:T(8,128)(2,1)S(1)}, bf16[2,64,1024]{2,1,0:T(8,128)(2,1)S(1)}, u32[]{:S(2)}, u32[]{:S(2)}) collective-permute-start(bf16[2,64,1024]{2,1,0:T(8,128)(2,1)S(1)} %collective-permute-done.1.refs_4_), channel_id=1, source_target_pairs={{0,8},{8,0},{1,9},{9,1},{2,10},{10,2},{3,11},{11,3},{4,12},{12,4},... | collective-permute-start | bytes 786440 | tf_op jit(solution)/shard_map/ppermute | solution.py:194
  22.4 1.6 %collective-permute-start.10 = (bf16[64,1024]{1,0:T(8,128)(2,1)S(1)}, bf16[64,1024]{1,0:T(8,128)(2,1)S(1)}, u32[]{:S(2)}, u32[]{:S(2)}) collective-permute-start(bf16[64,1024]{1,0:T(8,128)(2,1)S(1)} %collective-permute-done.6.refs_3_), channel_id=1, source_target_pairs={{0,8},{8,0},{1,9},{9,1},{2,10},{10,2},{3,11},{11,3},{4,12},{12,4},... | collective-permute-start | bytes 393224 | tf_op jit(solution)/shard_map/ppermute | solution.py:194
  22.5 1.7 %collective-permute-start.9 = (bf16[64,1024]{1,0:T(8,128)(2,1)S(1)}, bf16[64,1024]{1,0:T(8,128)(2,1)S(1)}, u32[]{:S(2)}, u32[]{:S(2)}) collective-permute-start(bf16[64,1024]{1,0:T(8,128)(2,1)S(1)} %collective-permute-done.5.refs_2_), channel_id=1, source_target_pairs={{0,8},{8,0},{1,9},{9,1},{2,10},{10,2},{3,11},{11,3},{4,12},{12,4},... | collective-permute-start | bytes 393224 | tf_op jit(solution)/shard_map/ppermute | solution.py:194
  26.8 44.7 %all-to-all-start = ((bf16[256,8,256]{2,1,0:T(8,128)(2,1)}), bf16[256,8,256]{2,1,0:T(8,128)(2,1)S(1)}, u32[]{:S(2)}, u32[]{:S(2)}) async-start(bf16[256,8,256]{2,1,0:T(8,128)(2,1)} %bitcast.3), calls=%async_computation | async-start | bytes 2097152 | tf_op jit(solution)/shard_map/all_to_all | solution.py:247
